TPU v7x, 32 devices: a whole 2x2x4 slice. The times are simulated.
32 devices in a mesh: shard: 4 (over y, x), context: 2 (over core), tensor: 4 (over z).
Axes of the slice: x: 2, y: 2, z: 4, core: 2. Of those that a mesh axis runs over, the one named last changes fastest.
Arguments:
- tokens: bfloat16 [16, 1024, 768], P('shard', ('context', 'tensor')), may hold values from -6 to 6
- lengths: int32 [16], P('shard'), may hold values from 256 to 1024, as said below
- features: bfloat16 [12, 256, 64], P('tensor'), may hold values from -3 to 3, as said below
- w_qkv: bfloat16 [768, 3, 12, 64], P('shard', None, 'tensor'), may hold values from -0.3125 to 0.3125
- b_qkv: bfloat16 [3, 12, 64], P(None, 'tensor', 'shard'), may hold values from -1.5 to 1.5
- w_out: bfloat16 [768, 768], P('tensor', 'shard'), may hold values from -1.75 to 1.75
- b_out: bfloat16 [768], P('shard'), may hold values from -3 to 3
- gain_one: bfloat16 [768], P('shard'), may hold values from 0.099609375 to 1.8984375
- shift_one: bfloat16 [768], P('shard'), may hold values from -3 to 3
- w_up: bfloat16 [768, 3072], P('shard', 'tensor'), may hold values from -0.21875 to 0.21875
- b_up: bfloat16 [24, 128], P('tensor', 'shard'), may hold values from -3 to 3
- w_down: bfloat16 [3072, 768], P('tensor', 'shard'), may hold values from -0.109375 to 0.109375
- b_down: bfloat16 [768], P('shard'), may hold values from -3 to 3
- gain_two: bfloat16 [768], P('shard'), may hold values from 0.099609375 to 1.8984375
- shift_two: bfloat16 [768], P('shard'), may hold values from -3 to 3
- cotangent: bfloat16 [16, 1024, 768], P('shard', ('context', 'tensor')), may hold values from -6 to 6
Outputs:
- out: bfloat16 [16, 1024, 768], P('shard', ('context', 'tensor'))
- grad_tokens: float32 [16, 1024, 768], P('shard', ('context', 'tensor'))
- grad_w_qkv: float32 [768, 3, 12, 64], P('shard', None, 'tensor')
- grad_b_qkv: float32 [3, 12, 64], P(None, 'tensor', 'shard')
- grad_w_out: float32 [768, 768], P('tensor', 'shard')
- grad_b_out: float32 [768], P('shard')
- grad_gain_one: float32 [768], P('shard')
- grad_shift_one: float32 [768], P('shard')
- grad_w_up: float32 [768, 3072], P('shard', 'tensor')
- grad_b_up: float32 [24, 128], P('tensor', 'shard')
- grad_w_down: float32 [3072, 768], P('tensor', 'shard')
- grad_b_down: float32 [768], P('shard')
- grad_gain_two: float32 [768], P('shard')
- grad_shift_two: float32 [768], P('shard')
Inputs may be any that keep to these rules, and one draw needn't show every extreme that they name: `lengths`: at least one sequence is valid in all 1024 slots and at least one in a quarter of them. `features`: independent entries of mean 0 and variance about 1.
All inputs are finite; a program needn't handle non-finite values.
Results may differ from a plain program's by a relative error of at most 0.034.
Values may be sent and summed in bfloat16 or wider, within the bound.
No kernel may reach another device: no remote copies, remote signals or barrier semaphores. Data moves between devices by JAX's collectives and lax.ppermute only.
A program may use at most 192 MiB of HBM per device.

v0:
```python
import functools

import jax
import jax.numpy as jnp
from jax import lax
from jax.experimental import pallas as pl
from jax.experimental.pallas import tpu as pltpu
from jax.sharding import PartitionSpec as P

F = jnp.float32
B = jnp.bfloat16


def wide_add(*terms):
    total = terms[0].astype(F)
    for term in terms[1:]:
        total = total + term.astype(F)
    return total


def together(*values):
    return lax.optimization_barrier(values)


class Links:
    def __init__(self, sizes):
        self.sizes = sizes
        self.s = lax.axis_index("shard")
        self.c = lax.axis_index("context")
        self.t = lax.axis_index("tensor")
        self.core = self.c % 2

    def perm_t(self, value, step):
        n = self.sizes["tensor"]
        return lax.ppermute(value, "tensor", [(i, (i + step) % n) for i in range(n)])

    def perm_s(self, value, mask):
        n = self.sizes["shard"]
        return lax.ppermute(value, "shard", [(i, i ^ mask) for i in range(n)])

    def perm_c(self, value, mask=1):
        n = self.sizes["context"]
        return lax.ppermute(value, "context", [(i, i ^ mask) for i in range(n)])

    def undeal_some(self, rows, steps):
        n = self.sizes["tensor"]
        rows = rows.reshape(n, rows.shape[0] // n, rows.shape[1])
        return {d: self.perm_t(rows[d], n - d) for d in steps if d < n}

    def undealt(self, rows, moved, dtype):
        n = self.sizes["tensor"]
        rows = rows.reshape(n, rows.shape[0] // n, rows.shape[1])
        return lay(self.t, [rows[0]] + [moved[d] for d in range(1, n)], dtype)

    def half(self, local):
        rows = local.shape[0] // 2
        return lax.dynamic_slice_in_dim(local, self.core * rows, rows, 0)

    def spread_t(self, local):
        n = self.sizes["tensor"]
        return jnp.stack([local] + [self.perm_t(local, d) for d in range(1, n)])

    def spread_near(self, block):
        return self.perm_s(block, 1), self.perm_s(block, 2)

    def spread_far(self, near):
        h = self.sizes["tensor"] // 2
        over_x, over_y = near
        return self.perm_s(over_x[:h], 2), self.perm_s(over_y[h:], 1)

    def carry(self, rows, extra, steps):
        n = self.sizes["tensor"]
        take = lambda d: lax.dynamic_index_in_dim(rows, (self.t + d) % n, 0, keepdims=False)
        return {d: self.perm_t(jnp.concatenate([take(d), extra]), d) for d in steps if d < n}

    def unload(self, rows, extra, moved):
        length = rows.shape[1]
        own = lax.dynamic_index_in_dim(rows, self.t, 0, keepdims=False)
        steps = sorted(moved)
        return (
            jnp.concatenate([own] + [moved[d][:length] for d in steps]),
            jnp.stack([extra] + [moved[d][length:] for d in steps]),
        )

    def swap(self, values):
        return tuple(self.perm_c(value) for value in values)

    def collect_one(self, parts):
        h = parts.shape[1] // 2
        return (
            self.perm_s(jnp.stack([parts[3, h:], parts[1, h:]]), 1),
            self.perm_s(jnp.stack([parts[3, :h], parts[2, :h]]), 2),
        )

    def collect_two(self, parts, one):
        h = parts.shape[1] // 2
        return (
            self.perm_s(wide_add(parts[1, :h], one[1][0]).astype(B), 1),
            self.perm_s(wide_add(parts[2, h:], one[0][0]).astype(B), 2),
        )

    def sums(self, parts, one, two):
        h = parts.shape[1] // 2
        return jnp.concatenate(
            [
                wide_add(parts[0, :h], two[0], one[1][1]).astype(B),
                wide_add(parts[0, h:], one[0][1], two[1]).astype(B),
            ]
        )

    def collect_t(self, total, slots):
        n = self.sizes["tensor"]
        return [self.perm_t(total[i], n - i) for i in slots if i < n]

    def collect_end(self, terms):
        total = wide_add(*terms)
        mask = 2
        while mask < self.sizes["context"]:
            low = total.astype(B)
            total = wide_add(low, self.perm_c(low, mask))
            mask *= 2
        low = total.astype(B)
        other = self.perm_c(low)
        first = jnp.where(self.core == 0, low, other)
        second = jnp.where(self.core == 0, other, low)
        return jnp.concatenate([first, second])


def dot(a, b, ca=1, cb=0):
    return lax.dot_general(a, b, (((ca,), (cb,)), ((), ())), preferred_element_type=F)


def iota(shape, axis):
    return lax.broadcasted_iota(jnp.int32, shape, axis)


def block_diagonal(compact, heads):
    k, m = compact.shape[0], compact.shape[1] // heads
    zero = jnp.zeros((k, m), compact.dtype)
    rows = []
    for h in range(heads):
        row = [zero] * heads
        row[h] = compact[:, h * m : (h + 1) * m]
        rows.append(jnp.concatenate(row, axis=1))
    return jnp.concatenate(rows, axis=0)


def diagonal_blocks(full, heads):
    k, m = full.shape[0] // heads, full.shape[1] // heads
    return jnp.concatenate(
        [full[h * k : (h + 1) * k, h * m : (h + 1) * m] for h in range(heads)], axis=1
    )


def stacked(upper, lower, heads):
    a, b = block_diagonal(upper, heads), block_diagonal(lower, heads)
    gap = jnp.zeros((second_start(a.shape[0]) - a.shape[0], a.shape[1]), a.dtype)
    return jnp.concatenate([a, gap, b], axis=0)


def second_start(width):
    return -(-width // 128) * 128


def beside(left, right):
    gap = jnp.zeros((left.shape[0], second_start(left.shape[1]) - left.shape[1]), left.dtype)
    return jnp.concatenate([left, gap, right], axis=1)


def rows_to_lanes(rows, lanes):
    k = rows.shape[1]
    tile = (iota((k, lanes), 1) % k == iota((k, lanes), 0)).astype(F).astype(B)
    spread = dot(rows, tile)
    hit = iota(spread.shape, 1) // k == iota(spread.shape, 0)
    return jnp.sum(jnp.where(hit, spread, 0.0), axis=0, keepdims=True)


class Pieces:
    def __init__(self, n, m, where, refs, dest, sems, start, cols, slots=None):
        self.n, self.m, self.where, self.refs = n, m, where, refs
        self.slots = slots or range(n)
        self.dest, self.sems, self.start_col, self.cols = dest, sems, start, cols
        self.rows = refs[0].shape[1]

    def copies(self, t):
        s, c = self.where[0], self.where[1]
        made = []
        for i in range(2):
            half = c if i == 0 else 1 - c
            for j in range(self.m):
                row = pl.multiple_of((s ^ j) * (2 * self.rows) + half * self.rows, 8)
                src = self.refs[i * self.m + j].at[t]
                src = src.at[:, pl.ds(self.start_col, self.cols)]
                u = t - self.slots[0]
                target = self.dest.at[u, pl.ds(row, self.rows)]
                made.append(pltpu.make_async_copy(src, target, self.sems.at[u, i * self.m + j]))
        return made

    def start(self):
        for t in self.slots:
            for copy in self.copies(t):
                copy.start()

    def wait(self, t):
        for u in self.slots:

            @pl.when(t == u - self.slots[0])
            def _():
                for copy in self.copies(u):
                    copy.wait()


ANY = pl.BlockSpec(memory_space=pl.ANY)
SCALARS = pl.BlockSpec(memory_space=pltpu.SMEM)


def slot(*shape, first=0):
    zeros = (0,) * len(shape)
    return pl.BlockSpec((1,) + shape, lambda t: (t + first,) + zeros)


def fixed(*shape):
    zeros = (0,) * len(shape)
    return pl.BlockSpec(shape, lambda *_: zeros)


COST = {
    "project": 11,
    "attend": 6,
    "widen": 10,
    "narrow": 13,
    "ffn_grad": 9,
    "widen_back": 10,
    "attend_back": 7,
    "project_back": 11,
}


def call(body, grid, in_specs, out_specs, outs, scratch, name, flops=0):
    return pl.pallas_call(
        body,
        grid=grid,
        in_specs=in_specs,
        out_specs=out_specs,
        out_shape=[jax.ShapeDtypeStruct(s, d) for s, d in outs],
        scratch_shapes=scratch,
        compiler_params=pltpu.CompilerParams(
            dimension_semantics=("arbitrary",) * len(grid), vmem_limit_bytes=60 * 1024 * 1024
        ),
        cost_estimate=pl.CostEstimate(
            flops=COST[name] * 300_000_000, transcendentals=0, bytes_accessed=COST[name] * 800_000
        ),
        name=name,
    )


def lay(t, chunks, dtype):
    n, shape = len(chunks), chunks[0].shape

    def body(t, *refs):
        for d in range(n):

            @pl.when(pl.program_id(0) == d)
            def _():
                refs[n][0] = refs[d][...].astype(dtype)

    return pl.pallas_call(
        body,
        grid_spec=pltpu.PrefetchScalarGridSpec(
            num_scalar_prefetch=1,
            grid=(n,),
            in_specs=[pl.BlockSpec(shape, lambda d, t: (0, 0))] * n,
            out_specs=pl.BlockSpec((1,) + shape, lambda d, t: ((t[0] + d) % n, 0, 0)),
        ),
        out_shape=jax.ShapeDtypeStruct((n,) + shape, dtype),
        cost_estimate=pl.CostEstimate(flops=0, transcendentals=0, bytes_accessed=800_000),
        compiler_params=pltpu.CompilerParams(dimension_semantics=("arbitrary",)),
        name="lay",
    )(t[None].astype(jnp.int32), *chunks)


def gather_rows(vectors, count):
    def body(*refs):
        row, k = iota((count, 64), 0), 0
        total = jnp.zeros((count, 64), F)
        for ref in refs[:-1]:
            value = ref[...].astype(F).reshape(1, ref.shape[0])
            for start in range(0, ref.shape[0], 64):
                total = jnp.where(row == k, value[:, start : start + 64], total)
                k += 1
        refs[-1][...] = total.astype(B)

    return pl.pallas_call(
        body,
        out_shape=jax.ShapeDtypeStruct((count, 64), B),
        cost_estimate=pl.CostEstimate(flops=0, transcendentals=0, bytes_accessed=8_000),
        name="gather_rows",
    )(*vectors)


def norm_stats(res):
    mean = jnp.mean(res, axis=-1, keepdims=True)
    centered = res - mean
    var = jnp.mean(centered * centered, axis=-1, keepdims=True)
    inverse = lax.rsqrt(var + 1e-05)
    return centered * inverse, inverse


def norm_back(normal, inverse, gain, upstream):
    scaled = upstream * gain
    inner = (
        scaled
        - jnp.mean(scaled, axis=-1, keepdims=True)
        - normal * jnp.mean(scaled * normal, axis=-1, keepdims=True)
    )
    return inner * inverse


def as_rows(vectors, first):
    width = vectors[0].shape[1]
    row = iota((8, width), 0)
    total = jnp.zeros((8, width), F)
    for i, vector in enumerate(vectors):
        total = jnp.where(row == first + i, vector, total)
    return total


def turn(dest, spare, value, where, m):
    spare[...] = value
    rows = value.shape[0] // (2 * m)
    s, c = where[0], where[1]
    for part in range(2):
        half = c if part == 0 else 1 - c
        for i in range(m):
            src = pl.multiple_of(((s ^ i) * 2 + half) * rows, 16)
            row = (part * m + i) * rows
            dest[row : row + rows] = spare[pl.ds(src, rows)]


def store_turned(value, col, keep, give, m):
    rows, cols = value.shape[0] // (2 * m), value.shape[1]
    for i in range(m):
        keep[i, 0, :, col : col + cols] = value[i * rows : (i + 1) * rows].astype(B)
        give[i, 0, :, col : col + cols] = value[(m + i) * rows : (m + i + 1) * rows].astype(B)


def folded(laid):
    pair = laid[:, :128]
    for k in range(128, laid.shape[1], 128):
        pair = pair + laid[:, k : k + 128]
    return jnp.concatenate([jnp.zeros((laid.shape[0], 64), F), pair[:, :64] + pair[:, 64:]], axis=1)


def over_rows(span, step_rows):
    step = 256 if span % 256 == 0 else span

    def one(i, carry):
        step_rows(pl.ds(pl.multiple_of(i * step, step), step))
        return carry

    lax.fori_loop(0, span // step, one, 0)


class Shape:
    def __init__(self, sizes, features, tokens, b_up):
        self.n, self.m = sizes["tensor"], sizes["shard"]
        self.hl, self.feats, self.hd = features.shape
        self.chunk, self.width = tokens.shape[1], tokens.shape[2]
        self.span = self.chunk * self.n
        self.share = self.width // self.m
        self.rows = self.share // 2
        self.oc = self.hl * self.hd
        self.qc = 3 * self.oc
        self.hm = self.hl * self.feats
        self.ff = b_up.size * self.m
        self.q_cols = self.qc + 64
        self.a_cols = self.q_cols + self.oc + 64
        self.scale = self.hd ** (-0.25)


def project(z, where, pieces, x, feat, valid, slots):
    cnt, first = len(slots), slots[0]
    n, span, hl, feats, hd = z.n, z.span, z.hl, z.feats, z.hd

    def body(where, *refs):
        pcs, refs = refs[:8], refs[8:]
        x, feat, valid, q_out, k_out, v_out, qf_out, kf_out, st_out, top_out, w, k_dash, peak, sems = refs
        t = pl.program_id(0)
        fetch = Pieces(n, z.m, where, pcs, w, sems, 0, z.q_cols, slots)
        pl.when(t == 0)(fetch.start)
        fetch.wait(t)
        bias = jnp.zeros((16, 64), F)
        for s in range(z.m):
            bias = bias + w[t, s * z.share : s * z.share + 16, z.qc :].astype(F)
        bias = rows_to_lanes(bias.astype(B), z.qc)
        table = block_diagonal(feat[0], hl)
        peak[...] = jnp.full((8, z.hm), -1e30, F)

        def queries_keys(r):
            qkv = dot(x[r], w[t, :, : z.qc]) + bias
            q = (qkv[:, : z.oc] * z.scale).astype(B)
            k = (qkv[:, z.oc : 2 * z.oc] * z.scale).astype(B)
            q_out[0, r], k_out[0, r], v_out[0, r] = q, k, qkv[:, 2 * z.oc :].astype(B)
            qd, kd = dot(q, table), dot(k, table)
            qs, ks = q.astype(F), k.astype(F)
            qs, ks = qs * qs, ks * ks
            live = valid[r] > 0
            for h in range(hl):
                seg, cols = slice(h * hd, (h + 1) * hd), slice(h * feats, (h + 1) * feats)
                dash = qd[:, cols] - 0.5 * jnp.sum(qs[:, seg], axis=-1, keepdims=True)
                qf_out[0, r, cols] = jnp.exp(
                    dash - jnp.floor(jnp.max(dash, axis=-1, keepdims=True))
                ).astype(B)
                dash = kd[:, cols] - 0.5 * jnp.sum(ks[:, seg], axis=-1, keepdims=True)
                k_dash[r, cols] = dash
                top = jnp.max(jnp.where(live, dash, -1e30), axis=0, keepdims=True)
                peak[:, cols] = jnp.maximum(peak[:, cols], top)

        over_rows(span, queries_keys)
        tops = []
        for h in range(hl):
            top = jnp.max(peak[0:1, h * feats : (h + 1) * feats], axis=1, keepdims=True)
            tops.append(jnp.broadcast_to(jnp.floor(top), (8, feats)))
        top = jnp.concatenate(tops, axis=1)
        top_out[0] = top

        def keys(r):
            live = valid[r] > 0
            kf_out[0, r] = jnp.where(live, jnp.exp(k_dash[r] - top[0:1]), 0.0).astype(B)

        over_rows(span, keys)
        vx = jnp.concatenate([v_out[0], jnp.ones((span, 64), B)], axis=1)
        state = dot(vx, kf_out[0], 0, 0)
        high = top.astype(B).astype(F)
        mid = (top - high).astype(B).astype(F)
        row, last = iota((8, z.hm), 0), state[z.oc : z.oc + 8]
        for i, term in enumerate((high, mid, top - high - mid)):
            last = jnp.where(row == i + 1, term, last)
        st_out[0] = jnp.concatenate([diagonal_blocks(state[: z.oc], hl), last], axis=0).astype(B)

    return call(
        body,
        (cnt,),
        [SCALARS] + [ANY] * 8 + [fixed(span, z.width), slot(hd, z.hm, first=first), fixed(span, 1)],
        [slot(span, z.oc)] * 3 + [slot(span, z.hm)] * 2 + [slot(hd + 8, z.hm), slot(8, z.hm)],
        [((cnt, span, z.oc), B)] * 3
        + [((cnt, span, z.hm), B)] * 2
        + [((cnt, hd + 8, z.hm), B), ((cnt, 8, z.hm), F)],
        [
            pltpu.VMEM((cnt, z.width, z.q_cols), B),
            pltpu.VMEM((span, z.hm), F),
            pltpu.VMEM((8, z.hm), F),
            pltpu.SemaphoreType.DMA((cnt, 2 * z.m)),
        ],
        "project",
    )(where, *pieces, x, feat, valid)


def attend(z, where, pieces, qf, state, slots, x=None, before=None):
    cnt, first, last = len(slots), slots[0], x is not None
    n, span, hl, hd = z.n, z.span, z.hl, z.hd

    def body(where, *refs):
        pcs, refs = refs[:8], refs[8:]
        qf, state, refs = refs[0], refs[1], refs[2:]
        if last:
            x, before, refs = refs[0], refs[1], refs[2:]
        mixed_out, den_out, bup_out, refs = refs[0], refs[1], refs[2], refs[3:]
        if last:
            normal_out, inverse_out, vec_out, w, acc, sems = refs
        else:
            acc, w, sems = refs
        t = pl.program_id(0)
        fetch = Pieces(n, z.m, where, pcs, w, sems, z.q_cols, z.oc + 64, slots)
        pl.when(t == 0)(fetch.start)
        compact = state[0, :hd]
        total = jnp.broadcast_to(state[0, hd : hd + 1], (hd, z.hm))
        table = stacked(compact, total, hl)
        fetch.wait(t)

        def ratios(r):
            both = dot(qf[0, r], table, 1, 1)
            den = both[:, second_start(z.oc) :]
            mixed = (both[:, : z.oc] / den).astype(B)
            mixed_out[0, r] = mixed
            den_out[0, r] = den
            so_far = jnp.where(t == 0, before[r] if last else 0.0, acc[r])
            acc[r] = dot(mixed, w[t, :, : z.oc], 1, 1) + so_far

        over_rows(span, ratios)
        bias = jnp.zeros((16, 64), F)
        for s in range(z.m):
            bias = bias + w[t, s * z.share + 24 : s * z.share + 40, z.oc :].astype(F)
        bup_out[0] = jnp.broadcast_to(rows_to_lanes(bias.astype(B), z.ff), (8, z.ff))
        if not last:
            return

        @pl.when(t == cnt - 1)
        def _():
            lanes = z.width
            per = z.share // 64
            tile = (iota((64, lanes), 1) % 64 == iota((64, lanes), 0)).astype(F).astype(B)
            found = jnp.zeros((24, lanes), F)
            for s in range(z.m):
                spread = dot(w[0, s * z.share : s * z.share + 24, z.oc :], tile)
                hit = iota((24, lanes), 1) // 64 == per * s + iota((24, lanes), 0) % per
                found = found + jnp.where(hit, spread, 0.0)
            pick = (iota((8, 24), 1) // per == iota((8, 24), 0)).astype(F).astype(B)
            vec = dot(pick, found.astype(B))
            vec_out[...] = vec

            def norm(r):
                res = acc[r] + vec[0:1] + x[r].astype(F)
                normal_out[r], inverse_out[r] = norm_stats(res)

            over_rows(span, norm)

    wide = fixed(span, z.width)
    ins, extra = [slot(span, z.hm), slot(hd + 8, z.hm)], []
    outs = [slot(span, z.oc), slot(span, z.oc), slot(8, z.ff)]
    shapes = [((cnt, span, z.oc), B), ((cnt, span, z.oc), F), ((cnt, 8, z.ff), F)]
    scratch = [pltpu.VMEM((cnt, z.width, z.oc + 64), B)]
    if last:
        ins, extra = ins + [wide, wide], [x, before]
        outs += [wide, fixed(span, 1), fixed(8, z.width)]
        shapes += [((span, z.width), F), ((span, 1), F), ((8, z.width), F)]
        scratch += [pltpu.VMEM((span, z.width), F)]
    else:
        outs, shapes = outs + [wide], shapes + [((span, z.width), F)]
    return call(
        body,
        (cnt,),
        [SCALARS] + [ANY] * 8 + ins,
        outs,
        shapes,
        scratch + [pltpu.SemaphoreType.DMA((cnt, 2 * z.m))],
        "attend",
    )(where, *pieces, qf, state, *extra)


def widen(z, where, pieces, normal, vec, bup):
    n, span = z.n, z.span

    def body(where, *refs):
        pcs, refs = refs[:8], refs[8:]
        normal, vec, bup, act_out, slope_out, w, low, sems = refs
        t = pl.program_id(0)
        fetch = Pieces(n, z.m, where, pcs, w, sems, 0, z.ff)

        @pl.when(t == 0)
        def _():
            fetch.start()
            low[...] = (normal[...] * vec[1:2] + vec[2:3]).astype(B)

        fetch.wait(t)

        def hidden(r):
            up = dot(low[r], w[t]) + bup[0, 0:1]
            share = 0.5 * (1.0 + lax.erf(up * 0.7071067811865476))
            act_out[0, r] = (up * share).astype(B)
            slope_out[0, r] = (share + up * jnp.exp(-0.5 * up * up) * 0.3989422804014327).astype(B)

        over_rows(span, hidden)

    return call(
        body,
        (n,),
        [SCALARS] + [ANY] * 8 + [fixed(span, z.width), fixed(8, z.width), slot(8, z.ff)],
        [slot(span, z.ff)] * 2,
        [((n, span, z.ff), B)] * 2,
        [
            pltpu.VMEM((n, z.width, z.ff), B),
            pltpu.VMEM((span, z.width), B),
            pltpu.SemaphoreType.DMA((n, 2 * z.m)),
        ],
        "widen",
    )(where, *pieces, normal, vec, bup)


def narrow(z, where, pieces, normal, vec, cot, act, slope):
    n, span, rows, m = z.n, z.span, z.rows, z.m

    def body(where, *refs):
        pcs, refs = refs[:8], refs[8:]
        normal, vec, cot, act, slope = refs[:5]
        out, dres_out, low, dup_out, small_out = refs[5:10]
        w, acc, sems = refs[10:]
        p, t = pl.program_id(0), pl.program_id(1)
        fetch = Pieces(n, m, where, pcs, w, sems, 0, z.ff)

        @pl.when((p == 0) & (t == 0))
        def _():
            fetch.start()

        @pl.when(p == 0)
        def _():
            fetch.wait(t)

            def down(r):
                acc[r] = dot(act[0, r], w[t], 1, 1) + jnp.where(t == 0, 0.0, acc[r])

            over_rows(span, down)

        @pl.when((p == 0) & (t == n - 1))
        def _():
            small_out[...] = jnp.zeros((8, z.width), F)

            def norm(r):
                normed = normal[r] * vec[1:2] + vec[2:3]
                second, inverse = norm_stats(acc[r] + vec[3:4] + normed)
                out[r] = (second * vec[4:5] + vec[5:6]).astype(B)
                up = cot[r].astype(F)
                dres = norm_back(second, inverse, vec[4:5], up)
                dres_out[r] = dres
                low[r] = dres.astype(B)
                small_out[...] += as_rows(
                    [
                        jnp.sum(dres, axis=0, keepdims=True),
                        jnp.sum(up * second, axis=0, keepdims=True),
                        jnp.sum(up, axis=0, keepdims=True),
                    ],
                    3,
                )

            over_rows(span, norm)

        @pl.when(p == 1)
        def _():
            def up_back(r):
                dup_out[0, r] = (dot(low[r], w[t]) * slope[0, r].astype(F)).astype(B)

            over_rows(span, up_back)

    second = lambda *shape: pl.BlockSpec((1,) + shape, lambda p, t: (p * t,) + (0,) * len(shape))
    return call(
        body,
        (2, n),
        [SCALARS]
        + [ANY] * 8
        + [
            fixed(span, z.width),
            fixed(8, z.width),
            fixed(span, z.width),
            pl.BlockSpec((1, span, z.ff), lambda p, t: (t * (1 - p) + (n - 1) * p, 0, 0)),
            second(span, z.ff),
        ],
        [fixed(span, z.width)] * 3 + [second(span, z.ff), fixed(8, z.width)],
        [
            ((span, z.width), B),
            ((span, z.width), F),
            ((span, z.width), B),
            ((n, span, z.ff), B),
            ((8, z.width), F),
        ],
        [
            pltpu.VMEM((n, z.width, z.ff), B),
            pltpu.VMEM((span, z.width), F),
            pltpu.SemaphoreType.DMA((n, 2 * m)),
        ],
        "narrow",
    )(where, *pieces, normal, vec, cot, act, slope)


def ffn_grad(z, where, normal, vec, d_ffn, act, dup):
    n, span, rows, m = z.n, z.span, z.rows, z.m

    def body(where, normal, vec, d_ffn, act, dup, keep, give, bup_out, low_t, normed_t, spare):
        t = pl.program_id(0)

        @pl.when(t == 0)
        def _():
            turn(low_t, spare, d_ffn[...].astype(F).T.astype(B), where, m)
            turn(normed_t, spare, (normal[...] * vec[1:2] + vec[2:3]).T.astype(B), where, m)

        store_turned(dot(low_t[...], act[0]), 0, keep, give, m)
        store_turned(dot(normed_t[...], dup[0]), z.ff, keep, give, m)
        bup_out[0] = jnp.broadcast_to(
            jnp.sum(dup[0].astype(F), axis=0, keepdims=True), (8, z.ff)
        )

    wide, grads = fixed(span, z.width), pl.BlockSpec((m, 1, rows, 2 * z.ff), lambda t: (0, t, 0, 0))
    return call(
        body,
        (n,),
        [SCALARS, wide, fixed(8, z.width), wide, slot(span, z.ff), slot(span, z.ff)],
        [grads, grads, slot(8, z.ff)],
        [((m, n, rows, 2 * z.ff), B)] * 2 + [((n, 8, z.ff), F)],
        [pltpu.VMEM((z.width, span), B)] * 3,
        "ffn_grad",
    )(where, normal, vec, d_ffn, act, dup)


def widen_back(z, where, pieces, normal, inverse, vec, dup, dres):
    n, span = z.n, z.span

    def body(where, *refs):
        pcs, refs = refs[:8], refs[8:]
        normal, inverse, vec, dup, dres, out, small_out, w, acc, sems = refs
        t = pl.program_id(0)
        fetch = Pieces(n, z.m, where, pcs, w, sems, 0, z.ff)
        pl.when(t == 0)(fetch.start)
        fetch.wait(t)

        def back(r):
            acc[r] = dot(dup[0, r], w[t], 1, 1) + jnp.where(t == 0, dres[r], acc[r])

        over_rows(span, back)

        @pl.when(t == n - 1)
        def _():
            small_out[...] = jnp.zeros((8, z.width), F)

            def norm(r):
                up = acc[r]
                back = norm_back(normal[r], inverse[r], vec[1:2], up)
                out[r] = back
                small_out[...] += as_rows(
                    [
                        jnp.sum(back, axis=0, keepdims=True),
                        jnp.sum(up * normal[r], axis=0, keepdims=True),
                        jnp.sum(up, axis=0, keepdims=True),
                    ],
                    0,
                )

            over_rows(span, norm)

    return call(
        body,
        (n,),
        [SCALARS]
        + [ANY] * 8
        + [
            fixed(span, z.width),
            fixed(span, 1),
            fixed(8, z.width),
            slot(span, z.ff),
            fixed(span, z.width),
        ],
        [fixed(span, z.width), fixed(8, z.width)],
        [((span, z.width), F), ((8, z.width), F)],
        [
            pltpu.VMEM((n, z.width, z.ff), B),
            pltpu.VMEM((span, z.width), F),
            pltpu.SemaphoreType.DMA((n, 2 * z.m)),
        ],
        "widen_back",
    )(where, *pieces, normal, inverse, vec, dup, dres)


def attend_back(z, where, pieces, dres, mixed, den, qf, q, state, feat, slots):
    cnt, first = len(slots), slots[0]
    n, span, hl, hd, m = z.n, z.span, z.hl, z.hd, z.m

    def body(where, *refs):
        pcs, refs = refs[:8], refs[8:]
        dres, mixed, den, qf, q, state, feat, dq_out, dstate_out, w, low, pair, sems = refs
        t = pl.program_id(0)
        fetch = Pieces(n, m, where, pcs, w, sems, z.q_cols, z.oc + 64, slots)

        @pl.when(t == 0)
        def _():
            fetch.start()
            low[...] = dres[...].astype(B)

        fetch.wait(t)
        start = second_start(z.oc)
        compact = state[0, :hd]
        total = jnp.broadcast_to(state[0, hd : hd + 1], (hd, z.hm))
        states, tables = stacked(compact, total, hl), stacked(feat[0], jnp.ones((hd, z.hm), B), hl)

        def back(r):
            d_mixed = dot(low[r], w[t, :, : z.oc]).astype(B).astype(F)
            d_num = d_mixed / den[0, r]
            d_den = -(d_num * mixed[0, r].astype(F))
            both = beside(d_num.astype(B), d_den.astype(B))
            pair[r] = both
            dash = (dot(both, states) * qf[0, r].astype(F)).astype(B)
            back = dot(dash, tables, 1, 1)
            dq_out[0, r] = ((back[:, : z.oc] - q[0, r].astype(F) * back[:, start:]) * z.scale).astype(B)

        over_rows(span, back)
        full = dot(pair[...], qf[0], 0, 0)
        row = jnp.concatenate(
            [
                jnp.sum(
                    full[start + h * hd : start + (h + 1) * hd, h * z.feats : (h + 1) * z.feats],
                    axis=0,
                    keepdims=True,
                )
                for h in range(hl)
            ],
            axis=1,
        )
        dstate_out[0] = jnp.concatenate(
            [diagonal_blocks(full[: z.oc], hl), jnp.broadcast_to(row, (8, z.hm))], axis=0
        ).astype(B)

    return call(
        body,
        (cnt,),
        [SCALARS]
        + [ANY] * 8
        + [
            fixed(span, z.width),
            slot(span, z.oc),
            slot(span, z.oc),
            slot(span, z.hm),
            slot(span, z.oc),
            slot(hd + 8, z.hm),
            slot(hd, z.hm, first=first),
        ],
        [slot(span, z.oc), slot(hd + 8, z.hm)],
        [((cnt, span, z.oc), B), ((cnt, hd + 8, z.hm), B)],
        [
            pltpu.VMEM((cnt, z.width, z.oc + 64), B),
            pltpu.VMEM((span, z.width), B),
            pltpu.VMEM((span, second_start(z.oc) + z.oc), B),
            pltpu.SemaphoreType.DMA((cnt, 2 * m)),
        ],
        "attend_back",
    )(where, *pieces, dres, mixed, den, qf, q, state, feat)


def project_back(z, where, pieces, x, dres, dq, k, v, kf, dstate, feat, mixed, small_a, small_b, dbup, slots, before=None):
    cnt, first, last = len(slots), slots[0], before is not None
    n, span, hl, hd, m, rows = z.n, z.span, z.hl, z.hd, z.m, z.rows
    cols = z.a_cols

    def body(where, *refs):
        pcs, refs = refs[:8], refs[8:]
        x, dres, dq, k, v, kf, dstate, feat, mixed, small_a, small_b, dbup = refs[:12]
        refs = refs[12:]
        if last:
            before, refs = refs[0], refs[1:]
            keep, give, out, w, x_t, low_t, spare, dqkv_low, acc, sems = refs
        else:
            keep, give, acc, w, x_t, low_t, spare, dqkv_low, sems = refs
        t = pl.program_id(0)
        fetch = Pieces(n, m, where, pcs, w, sems, 0, z.q_cols, slots)

        @pl.when(t == 0)
        def _():
            fetch.start()
            turn(x_t, spare, x[...].astype(F).T.astype(B), where, m)
            turn(low_t, spare, dres[...].T.astype(B), where, m)

        start = second_start(z.oc)
        table = block_diagonal(dstate[0, :hd], hl)
        total = dstate[0, hd : hd + 1].astype(F)
        dash = ((dot(v[0], table) + total) * kf[0].astype(F)).astype(B)
        dv = dot(kf[0], table, 1, 1)
        back = dot(dash, stacked(feat[0], jnp.ones((hd, z.hm), B), hl), 1, 1)
        dk = (back[:, : z.oc] - k[0].astype(F) * back[:, start:]) * z.scale
        dqkv = jnp.concatenate(
            [dq[0], dk.astype(B), dv.astype(B), jnp.zeros((span, 64), B)], axis=1
        )
        dqkv_low[...] = dqkv
        bias = jnp.sum(dqkv.astype(F), axis=0, keepdims=True)
        laid = jnp.broadcast_to(bias, (rows, z.q_cols))
        laid = jnp.where(iota(laid.shape, 1) // 64 == iota(laid.shape, 0), laid, 0.0)
        grad = dot(x_t[...], dqkv)
        edge = z.q_cols - 128
        store_turned(grad[:, :edge], 0, keep, give, m)
        store_turned(
            grad[:, edge:] + jnp.concatenate([folded(laid)] * (2 * m), axis=0), edge, keep, give, m
        )
        grad = dot(low_t[...], jnp.concatenate([mixed[0], jnp.zeros((span, 64), B)], axis=1))
        packed = small_a[...] + small_b[...] + as_rows([dbup[0, 0:1]], 6)
        per = z.width // 64
        one = (iota((rows, 8), 0) // per == iota((rows, 8), 1)).astype(F).astype(B)
        laid = dot(one, packed.astype(B))
        laid = jnp.where(iota(laid.shape, 1) // 64 == iota(laid.shape, 0) % per, laid, 0.0)
        edge = z.oc + 64 - 128
        store_turned(grad[:, :edge], z.q_cols, keep, give, m)
        store_turned(
            grad[:, edge:] + jnp.concatenate([folded(laid)] * (2 * m), axis=0),
            z.q_cols + edge,
            keep,
            give,
            m,
        )
        fetch.wait(t)

        def tokens_back(r):
            so_far = jnp.where(t == 0, before[r] if last else dres[r], acc[r])
            acc[r] = dot(dqkv_low[r], w[t], 1, 1) + so_far

        over_rows(span, tokens_back)

        if last:

            @pl.when(t == cnt - 1)
            def _():
                out[...] = acc[...].astype(B)

    grads = pl.BlockSpec((m, 1, rows, cols), lambda t: (0, t, 0, 0))
    wide, scratch = fixed(span, z.width), [pltpu.VMEM((cnt, z.width, z.q_cols), B)]
    scratch += [pltpu.VMEM((z.width, span), B)] * 3 + [pltpu.VMEM((span, z.q_cols), B)]
    if last:
        scratch += [pltpu.VMEM((span, z.width), F)]
    return call(
        body,
        (cnt,),
        [SCALARS]
        + [ANY] * 8
        + [
            wide,
            wide,
            slot(span, z.oc),
            slot(span, z.oc),
            slot(span, z.oc),
            slot(span, z.hm),
            slot(hd + 8, z.hm),
            slot(hd, z.hm, first=first),
            slot(span, z.oc),
            fixed(8, z.width),
            fixed(8, z.width),
            slot(8, z.ff, first=first),
        ]
        + ([wide] if last else []),
        [grads, grads, wide],
        [((m, cnt, rows, cols), B)] * 2 + [((span, z.width), B if last else F)],
        scratch + [pltpu.SemaphoreType.DMA((cnt, 2 * m))],
        "project_back",
    )(
        where, *pieces, x, dres, dq, k, v, kf, dstate, feat, mixed, small_a, small_b, dbup,
        *([before] if last else []),
    )


def place(part, axis, index, count):
    shape = list(part.shape)
    shape[axis] *= count
    return lax.dynamic_update_slice_in_dim(
        jnp.zeros(shape, part.dtype), part, index * part.shape[axis], axis
    )


def on_device(
    sizes,
    tokens,
    lengths,
    features,
    w_qkv,
    b_qkv,
    w_out,
    b_out,
    gain_one,
    shift_one,
    w_up,
    b_up,
    w_down,
    b_down,
    gain_two,
    shift_two,
    cotangent,
):
    links = Links(sizes)
    z = Shape(sizes, features, tokens, b_up)
    n, m, share = z.n, z.m, z.share
    where = jnp.stack([links.s, links.core]).astype(jnp.int32)
    def tall(value):
        return jnp.pad(value, ((0, share - value.shape[0]), (0, 0)))

    biases = place(b_qkv, 2, links.s, m).reshape(3 * z.hl, z.hd)
    vectors = gather_rows([b_out, gain_one, shift_one, b_down, gain_two, shift_two], 24)
    vectors = jnp.concatenate([vectors, place(b_up, 1, links.s, m).reshape(-1, 64)])
    local_a = links.half(
        jnp.concatenate([w_qkv.reshape(share, z.qc), tall(biases), w_out.T, tall(vectors)], axis=1)
    )
    feat_half = links.half(features.transpose(2, 0, 1).reshape(z.hd, z.hm))
    local_u, local_d = links.half(w_up), links.half(w_down.T)
    length = lax.dynamic_index_in_dim(lengths, links.t, 0, keepdims=False)
    order = (links.t - jnp.arange(n)) % n
    position = links.c * z.span + order[:, None] * z.chunk + jnp.arange(z.chunk)[None]
    valid = (position.reshape(-1, 1) < length).astype(F)
    halves = (range(n // 2), range(n // 2, n))
    lo, hi = halves

    def join_states(state, top, came):
        row, mask = z.hd + 1, 1
        own = most = top[:, :1]
        while mask < sizes["context"]:
            if mask > 1:
                came = links.perm_c(state, mask), links.perm_c(top, mask)
                other, other_top = came[0], came[1][:, :1]
            else:
                other = came
                other_top = wide_add(*[other[:, row + i : row + i + 1] for i in range(3)])
            joint = jnp.maximum(most, other_top)
            state = (
                state.astype(F) * jnp.exp(most - joint) + other.astype(F) * jnp.exp(other_top - joint)
            ).astype(B)
            most, mask = joint, 2 * mask
            top = jnp.broadcast_to(most, top.shape)
        return state, jnp.exp(own - most)

    def join_grads(state, came, fall):
        mask = 1
        while mask < sizes["context"]:
            other = came if mask == 1 else links.perm_c(state, mask)
            state = wide_add(state, other).astype(B)
            mask *= 2
        return (state.astype(F) * fall).astype(B)

    block_a = links.spread_t(local_a)
    block_a, tokens, feat_half = together(block_a, tokens, feat_half)
    near_a = links.spread_near(block_a)
    moved = links.carry(tokens, feat_half, range(1, n))
    block_a, near_a, moved, local_u, tokens, feat_half = together(
        block_a, near_a, moved, local_u, tokens, feat_half
    )
    far_a = links.spread_far(near_a)
    other_a = links.swap((block_a,) + near_a)
    x, feat_mine = links.unload(tokens, feat_half, moved)
    far_a, feat_mine, other_a, local_u, valid, x = together(far_a, feat_mine, other_a, local_u, valid, x)
    far_a = (jnp.concatenate(far_a),)
    other_a += links.swap(far_a)
    feat_other = links.perm_c(feat_mine)
    feat_low = jnp.where(links.core == 0, feat_mine, feat_other)
    feat_high = jnp.where(links.core == 0, feat_other, feat_mine)
    feat = jnp.concatenate([feat_low, feat_high], axis=1)
    feat, other_a, local_u = together(feat, other_a, local_u)
    pieces_a = (block_a,) + near_a + far_a + other_a
    block_u = links.spread_t(local_u)
    first = project(z, where, pieces_a, x, feat, valid, lo)
    first, block_u, local_d, valid, cot = together(first, block_u, local_d, valid, cotangent)
    near_u = links.spread_near(block_u)
    moved = links.carry(cot, local_d, (2,))
    other_u = links.swap((block_u,))
    came = links.perm_c(first[5])
    second = project(z, where, pieces_a, x, feat, valid, hi)
    first, second, near_u, block_u, other_u, moved, came, cot, local_d = together(
        first, second, near_u, block_u, other_u, moved, came, cot, local_d
    )
    made = (first, second)
    far_u = links.spread_far(near_u)
    moved.update(links.carry(cot, local_d, (1, 3)))
    came_b = links.perm_c(second[5])
    state_a, fall_a = join_states(first[5], first[6], came)
    one = attend(z, where, pieces_a, first[3], state_a, lo)
    one, far_u, near_u, other_u, moved, came_b, cot, local_d = together(
        one, far_u, near_u, other_u, moved, came_b, cot, local_d
    )
    mixed_a, den_a, bup_a, acc = one
    far_u = (jnp.concatenate(far_u),)
    cot, block_d = links.unload(cot, local_d, moved)
    near_d = links.spread_near(block_d)
    other_u += links.swap(near_u + far_u)
    state_b, fall_b = join_states(second[5], second[6], came_b)
    two = attend(z, where, pieces_a, second[3], state_b, hi, x, acc)
    two, near_d, block_d, other_u, cot = together(two, near_d, block_d, other_u, cot)
    mixed_b, den_b, bup_b, normal, inverse, vec = two
    states, falls = (state_a, state_b), (fall_a, fall_b)
    bup = jnp.concatenate([bup_a, bup_b])
    mixed, den = (mixed_a, mixed_b), (den_a, den_b)
    pieces_u = (block_u,) + near_u + far_u + other_u
    far_d = links.spread_far(near_d)
    other_d = links.swap((block_d,) + near_d)
    act, slope = widen(z, where, pieces_u, normal, vec, bup)
    act, slope, far_d, other_d = together(act, slope, far_d, other_d)
    far_d = (jnp.concatenate(far_d),)
    other_d += links.swap(far_d)
    pieces_d = (block_d,) + near_d + far_d + other_d
    out, d_res_two, d_ffn, dup, small_b = narrow(
        z, where, pieces_d, normal, vec, cot, act, slope
    )
    sent = links.undeal_some(out, (2,))
    keep, give, dbup = ffn_grad(z, where, normal, vec, d_ffn, act, dup)
    keep, give, out, dup, sent = together(keep, give, out, dup, sent)
    other = links.perm_c(give)
    sent.update(links.undeal_some(out, (1, 3)))
    d_res_one, small_a = widen_back(z, where, pieces_u, normal, inverse, vec, dup, d_res_two)
    d_res_one, keep, other, sent = together(d_res_one, keep, other, sent)
    result = links.undealt(out, sent, B)
    parts_f = wide_add(keep, other).astype(B)
    one_f = links.collect_one(parts_f)
    dq_a, d_state_a = attend_back(
        z, where, pieces_a, d_res_one, mixed[0], den[0], made[0][3], made[0][0], states[0], feat, lo
    )
    dq_a, d_state_a, d_res_one, parts_f = together(dq_a, d_state_a, d_res_one, parts_f)
    came = links.perm_c(d_state_a)
    dq_b, d_state_b = attend_back(
        z, where, pieces_a, d_res_one, mixed[1], den[1], made[1][3], made[1][0], states[1], feat, hi
    )
    dq_b, d_state_b, came, one_f, parts_f, x = together(dq_b, d_state_b, came, one_f, parts_f, x)
    two_f = links.collect_two(parts_f, one_f)
    came_b = links.perm_c(d_state_b)
    d_state_a = join_grads(d_state_a, came, falls[0])
    dq = (dq_a, dq_b)

    def run_back(i, d_state, x, before):
        return project_back(
            z, where, pieces_a, x, d_res_one, dq[i], made[i][1], made[i][2], made[i][4],
            d_state, feat, mixed[i], small_a, small_b, dbup, halves[i], before,
        )

    keep, give, acc = run_back(0, d_state_a, x, None)
    keep, give, acc, two_f, came_b, parts_f, x = together(keep, give, acc, two_f, came_b, parts_f, x)
    sums_f = links.sums(parts_f, one_f, two_f)
    terms_f = links.collect_t(sums_f, (1, 2))
    other = links.perm_c(give)
    d_state_b = join_grads(d_state_b, came_b, falls[1])
    keep_b, give_b, grad_x = run_back(1, d_state_b, x, acc)
    keep_b, give_b, grad_x, keep, other, terms_f, sums_f = together(
        keep_b, give_b, grad_x, keep, other, terms_f, sums_f
    )
    other_b = links.perm_c(give_b)
    terms_f += links.collect_t(sums_f, range(3, n))
    parts = wide_add(keep, other).astype(B)
    parts_b = wide_add(keep_b, other_b).astype(B)
    parts, grad_x = together(jnp.concatenate([parts, parts_b], axis=1), grad_x)
    one = links.collect_one(parts)
    sent = links.undeal_some(grad_x, (2,))
    one, parts, sent, grad_x, terms_f = together(one, parts, sent, grad_x, terms_f)
    two = links.collect_two(parts, one)
    sent.update(links.undeal_some(grad_x, (1, 3)))
    two, one, parts, sent, grad_x = together(two, one, parts, sent, grad_x)
    grad_tokens = links.undealt(grad_x, sent, F)
    sums = links.sums(parts, one, two)
    terms = [sums[0]] + links.collect_t(sums, range(1, n))
    terms_f = [sums_f[0]] + terms_f
    own_ffn = links.collect_end(terms_f)
    grad_up, grad_down = own_ffn[:, z.ff :].astype(F), own_ffn[:, : z.ff].T.astype(F)
    terms, grad_tokens, result, grad_up, grad_down = together(
        terms, grad_tokens, result, grad_up, grad_down
    )
    own_qkv = links.collect_end(terms)
    def mine(value, axis):
        size = value.shape[axis] // m
        return lax.dynamic_slice_in_dim(value, links.s * size, size, axis).astype(F)

    own_b_qkv = mine(own_qkv[: 3 * z.hl, z.qc : z.q_cols].reshape(3, z.hl, z.hd), 2)
    own_out = own_qkv[:, z.q_cols : z.q_cols + z.oc]
    tail = own_qkv[: z.rows, z.q_cols + z.oc :]
    vecs = mine(tail[: 6 * z.width // 64].reshape(6, z.width), 1)
    start = 6 * z.width // 64
    own_b_up = mine(tail[start : start + z.ff // 64].reshape(b_up.shape[0], -1), 1)
    return (
        result,
        grad_tokens,
        own_qkv[:, : z.qc].reshape(w_qkv.shape).astype(F),
        own_b_qkv,
        own_out.T.astype(F),
        vecs[0],
        vecs[1],
        vecs[2],
        grad_up,
        own_b_up,
        grad_down,
        vecs[3],
        vecs[4],
        vecs[5],
    )


def solution(mesh):
    sizes = dict(mesh.shape)
    in_specs = (
        P("shard", ("context", "tensor"), None),
        P("shard"),
        P("tensor", None, None),
        P("shard", None, "tensor", None),
        P(None, "tensor", "shard"),
        P("tensor", "shard"),
        P("shard"),
        P("shard"),
        P("shard"),
        P("shard", "tensor"),
        P("tensor", "shard"),
        P("tensor", "shard"),
        P("shard"),
        P("shard"),
        P("shard"),
        P("shard", ("context", "tensor"), None),
    )
    out_specs = (
        P("shard", ("context", "tensor"), None),
        P("shard", ("context", "tensor"), None),
        P("shard", None, "tensor", None),
        P(None, "tensor", "shard"),
        P("tensor", "shard"),
        P("shard"),
        P("shard"),
        P("shard"),
        P("shard", "tensor"),
        P("tensor", "shard"),
        P("tensor", "shard"),
        P("shard"),
        P("shard"),
        P("shard"),
    )
    return jax.shard_map(
        functools.partial(on_device, sizes),
        mesh=mesh,
        in_specs=in_specs,
        out_specs=out_specs,
        check_vma=False,
    )
```

profile of v0, /device:TPU:0, one launch (start us, length us, event | category | flops | bytes accessed | tf_op | source)
XLA Modules:
  0.0 368.5 jit_solution(6649342453044443136)
XLA Ops:
  4.7 2.2 gather_rows.1
  7.7 5.1 %collective-permute-start.2 = (bf16[96,896]{1,0:T(8,128)(2,1)S(1)}, bf16[96,896]{1,0:T(8,128)(2,1)S(1)}, u32[]{:S(2)}, u32[]{:S(2)}) collective-permute-start(bf16[96,896]{1,0:T(8,128)(2,1)S(1)} %fusion.19), channel_id=1, source_target_pairs={{0,3},{1,0},{2,1},{3,2},{4,7},{5,4},{6,5},{7,6},{8,11},{9,8},{10,9... | collective-permute-start | bytes 516104 | tf_op jit(solution)/shard_map/ppermute | solution.py:35
  13.9 3.7 %collective-permute-done.2 = bf16[96,896]{1,0:T(8,128)(2,1)S(1)} collective-permute-done((bf16[96,896]{1,0:T(8,128)(2,1)S(1)}, bf16[96,896]{1,0:T(8,128)(2,1)S(1)}, u32[]{:S(2)}, u32[]{:S(2)}) %collective-permute-start.2) | collective-permute-done | bytes 172064 | tf_op jit(solution)/shard_map/ppermute | solution.py:35
  17.6 9.8 %collective-permute-done.1 = bf16[96,896]{1,0:T(8,128)(2,1)S(1)} collective-permute-done((bf16[96,896]{1,0:T(8,128)(2,1)S(1)}, bf16[96,896]{1,0:T(8,128)(2,1)S(1)}, u32[]{:S(2)}, u32[]{:S(2)}) %collective-permute-start.1) | collective-permute-done | bytes 172064 | tf_op jit(solution)/shard_map/ppermute | solution.py:35
  27.5 2.0 collective-permute-start.3
  29.6 1.5 collective-permute-start.4
  32.9 1.9 collective-permute-start.6
  34.8 2.9 collective-permute-start.7
  39.0 3.9 %collective-permute-done.5 = bf16[160,768]{1,0:T(8,128)(2,1)S(1)} collective-permute-done((bf16[160,768]{1,0:T(8,128)(2,1)}, bf16[160,768]{1,0:T(8,128)(2,1)S(1)}, u32[]{:S(2)}, u32[]{:S(2)}) %collective-permute-start.5) | collective-permute-done | bytes 245792 | tf_op jit(solution)/shard_map/ppermute | solution.py:35
  42.9 8.7 %collective-permute-done.6 = bf16[160,768]{1,0:T(8,128)(2,1)S(1)} collective-permute-done((bf16[160,768]{1,0:T(8,128)(2,1)}, bf16[160,768]{1,0:T(8,128)(2,1)S(1)}, u32[]{:S(2)}, u32[]{:S(2)}) %collective-permute-start.6) | collective-permute-done | bytes 245792 | tf_op jit(solution)/shard_map/ppermute | solution.py:35
  57.0 7.5 %collective-permute-done.8 = bf16[2,96,896]{2,1,0:T(8,128)(2,1)S(1)} collective-permute-done((bf16[2,96,896]{2,1,0:T(8,128)(2,1)S(1)}, bf16[2,96,896]{2,1,0:T(8,128)(2,1)S(1)}, u32[]{:S(2)}, u32[]{:S(2)}) %collective-permute-start.8) | collective-permute-done | bytes 344096 | tf_op jit(solution)/shard_map/ppermute | solution.py:39
  69.6 6.7 %collective-permute-start.17 = (bf16[96,768]{1,0:T(8,128)(2,1)S(1)}, bf16[96,768]{1,0:T(8,128)(2,1)S(1)}, u32[]{:S(2)}, u32[]{:S(2)}) collective-permute-start(bf16[96,768]{1,0:T(8,128)(2,1)S(1)} %constant_dynamic-slice_fusion.3), channel_id=1, source_target_pairs={{0,3},{1,0},{2,1},{3,2},{4,7},{5,4},{6,5},{7,6},{8,11},{9,8},{10,9... | collective-permute-start | bytes 442376 | tf_op jit(solution)/shard_map/ppermute | solution.py:35
  77.0 13.0 %project.2 = (bf16[2,512,192]{2,1,0:T(8,128)(2,1)}, bf16[2,512,192]{2,1,0:T(8,128)(2,1)}, bf16[2,512,192]{2,1,0:T(8,128)(2,1)}, bf16[2,512,768]{2,1,0:T(8,128)(2...) custom-call(s32[2]{0:T(128)} %pad_add_fusion.where, ...), custom_call_target="tpu_custom_call" | custom-call | flops 3300000000 | bytes 8800000 | tf_op jit(solution)/shard_map/project/pallas_call | solution.py:441
  90.6 1.6 collective-permute-start.19
  93.0 2.3 collective-permute-start.21
  96.5 13.0 %project.3 = (bf16[2,512,192]{2,1,0:T(8,128)(2,1)}, bf16[2,512,192]{2,1,0:T(8,128)(2,1)}, bf16[2,512,192]{2,1,0:T(8,128)(2,1)}, bf16[2,512,768]{2,1,0:T(8,128)(2...) custom-call(s32[2]{0:T(128)} %pad_add_fusion.where, ...), custom_call_target="tpu_custom_call" | custom-call | flops 3300000000 | bytes 8800000 | tf_op jit(solution)/shard_map/project/pallas_call | solution.py:441
  109.5 2.6 collective-permute-done.21
  115.7 1.6 collective-permute-start.24
  118.5 3.5 collective-permute-start.26
  122.0 1.7 add_convert_fusion.10.refs_9_.refs_13_
  123.7 6.4 %attend.2 = (bf16[2,512,192]{2,1,0:T(8,128)(2,1)}, f32[2,512,192]{2,1,0:T(8,128)}, f32[2,8,768]{2,1,0:T(8,128)}, f32[512,768]{1,0:T(8,128)}) custom-call(s32[2]{0:T(128)} %pad_add_fusion.where, bf16[4,96,896]{2,1,0:T(8,128)(2,1)} %copy-done.2, bf16[4,96,896]{2,1,0:T(8,128)(2,1)} %copy-done.3, bf16[4,96,896]{2,1,0:T(8,128)(2,1)} %copy-done.4, ...), custom_call_target="tpu_custom_call" | custom-call | flops 1800000000 | bytes 4800000 | tf_op jit(solution)/shard_map/attend/pallas_call | solution.py:530
  131.1 3.9 %collective-permute-done.26 = bf16[224,768]{1,0:T(8,128)(2,1)S(1)} collective-permute-done((bf16[224,768]{1,0:T(8,128)(2,1)S(1)}, bf16[224,768]{1,0:T(8,128)(2,1)S(1)}, u32[]{:S(2)}, u32[]{:S(2)}) %collective-permute-start.26) | collective-permute-done | bytes 344096 | tf_op jit(solution)/shard_map/ppermute | solution.py:35
  137.4 1.6 collective-permute-start.29
  145.5 1.7 add_convert_fusion.9.refs_9_.refs_13_
  147.2 8.5 %attend.3 = (bf16[2,512,192]{2,1,0:T(8,128)(2,1)}, f32[2,512,192]{2,1,0:T(8,128)}, f32[2,8,768]{2,1,0:T(8,128)}, f32[512,768]{1,0:T(8,128)}, f32[512,1]{1,0:T(8,128)}, /*index=5*/f32[8,768]{1,0:T(8,128)}) custom-call(s32[2]{0:T(128)} %pad_add_fusion.where, bf16[4,96,896]{2,1,0:T(8,128)(2,1)} %copy-done.2, bf16[4,96,896]{2,1,0:T(8,128)(2,1)} %copy-done.3, ...), custom_call_target="tpu_custom_call" | custom-call | flops 1800000000 | bytes 4800000 | tf_op jit(solution)/shard_map/attend/pallas_call | solution.py:530
  159.2 1.5 collective-permute-start.34
  160.7 1.4 pad_maximum_fusion.21.refs_10_
  162.2 9.8 %widen.1 = (bf16[4,512,768]{2,1,0:T(8,128)(2,1)}, bf16[4,512,768]{2,1,0:T(8,128)(2,1)}) custom-call(s32[2]{0:T(128)} %pad_add_fusion.where, bf16[4,96,768]{2,1,0:T(8,128)(2,1)} %copy-done.11, bf16[4,96,768]{2,1,0:T(8,128)(2,1)} %copy-done.14, bf16[4,96,768]{2,1,0:T(8,128)(2,1)} %copy-done.15, bf16[4,96,768]{2,1,0:T(8,128)(2,1)} %copy-done.16, ...), custom_call_target="tpu_custom_call" | custom-call | flops 3000000000 | bytes 8000000 | tf_op jit(solution)/shard_map/widen/pallas_call | solution.py:565
  172.2 2.0 collective-permute-done.38.refs_7_
  175.0 16.4 %narrow.1 = (bf16[512,768]{1,0:T(8,128)(2,1)}, f32[512,768]{1,0:T(8,128)}, bf16[512,768]{1,0:T(8,128)(2,1)}, bf16[4,512,768]{2,1,0:T(8,128)(2,1)}, f32[8,768]{1,0:T(8,128)}) custom-call(s32[2]{0:T(128)} %pad_add_fusion.where, bf16[4,96,768]{2,1,0:T(8,128)(2,1)} %pad_maximum_fusion.10.refs_0_, bf16[4,96,768]{2,1,0:T(8,128)(2,1)} %collective-permute-done.28.refs_1_, ...), custom_call_target="tpu_custom_call" | custom-call | flops 3900000000 | bytes 10400000 | tf_op jit(solution)/shard_map/narrow/pallas_call | solution.py:635
  192.3 2.2 collective-permute-start.39
  194.6 10.9 %ffn_grad.1 = (bf16[4,4,96,1536]{3,2,1,0:T(8,128)(2,1)}, bf16[4,4,96,1536]{3,2,1,0:T(8,128)(2,1)}, f32[4,8,768]{2,1,0:T(8,128)}) custom-call(s32[2]{0:T(128)} %pad_add_fusion.where, f32[512,768]{1,0:T(8,128)} %get-tuple-element.313.refs_8_.normal, f32[8,768]{1,0:T(8,128)} %get-tuple-element.315.refs_9_.vec.refs_10_, ...), custom_call_target="tpu_custom_call" | custom-call | flops 2700000000 | bytes 7200000 | tf_op jit(solution)/shard_map/ffn_grad/pallas_call | solution.py:682
  206.9 2.3 collective-permute-start.41
  209.2 10.5 %widen_back.1 = (f32[512,768]{1,0:T(8,128)}, f32[8,768]{1,0:T(8,128)}) custom-call(s32[2]{0:T(128)} %pad_add_fusion.where, bf16[4,96,768]{2,1,0:T(8,128)(2,1)} %copy-done.11, bf16[4,96,768]{2,1,0:T(8,128)(2,1)} %copy-done.14, bf16[4,96,768]{2,1,0:T(8,128)(2,1)} %copy-done.15, bf16[4,96,768]{2,1,0:T(8,128)(2,1)} %copy-done.16, ...), custom_call_target="tpu_custom_call" | custom-call | flops 3000000000 | bytes 8000000 | tf_op jit(solution)/shard_map/widen_back/pallas_call | solution.py:728
  219.7 5.4 %add_convert_fusion = bf16[4,4,96,1536]{3,2,1,0:T(8,128)(2,1)S(1)} fusion(bf16[4,4,96,1536]{3,2,1,0:T(8,128)(2,1)} %collective-permute-done.40, bf16[4,4,96,1536]{3,2,1,0:T(8,128)(2,1)} %get-tuple-element.349), kind=kLoop, calls=%fused_computation | loop fusion | flops 9437184 | bytes 14155776 | tf_op jit(solution)/shard_map/convert_element_type | solution.py:1077
  225.4 2.0 copy-done.10
  229.1 1.6 collective-permute-start.45
  230.7 9.2 %attend_back.2 = (bf16[2,512,192]{2,1,0:T(8,128)(2,1)}, bf16[2,72,768]{2,1,0:T(8,128)(2,1)}) custom-call(s32[2]{0:T(128)} %pad_add_fusion.where, bf16[4,96,896]{2,1,0:T(8,128)(2,1)} %copy-done.2, bf16[4,96,896]{2,1,0:T(8,128)(2,1)} %copy-done.3, bf16[4,96,896]{2,1,0:T(8,128)(2,1)} %copy-done.4, bf16[4,96,896]{2,1,0:T(8,128)(2,1)} %copy-done.5, ...), custom_call_target="tpu_custom_call" | custom-call | flops 2100000000 | bytes 5600000 | tf_op jit(solution)/shard_map/attend_back/pallas_call | solution.py:799
  240.0 9.3 %attend_back.3 = (bf16[2,512,192]{2,1,0:T(8,128)(2,1)}, bf16[2,72,768]{2,1,0:T(8,128)(2,1)}) custom-call(s32[2]{0:T(128)} %pad_add_fusion.where, bf16[4,96,896]{2,1,0:T(8,128)(2,1)} %copy-done.2, bf16[4,96,896]{2,1,0:T(8,128)(2,1)} %copy-done.3, bf16[4,96,896]{2,1,0:T(8,128)(2,1)} %copy-done.4, bf16[4,96,896]{2,1,0:T(8,128)(2,1)} %copy-done.5, ...), custom_call_target="tpu_custom_call" | custom-call | flops 2100000000 | bytes 5600000 | tf_op jit(solution)/shard_map/attend_back/pallas_call | solution.py:799
  249.3 6.3 %collective-permute-done.44 = bf16[2,2,96,1536]{3,2,1,0:T(8,128)(2,1)S(1)} collective-permute-done((bf16[2,2,96,1536]{3,2,1,0:T(8,128)(2,1)S(1)}, bf16[2,2,96,1536]{3,2,1,0:T(8,128)(2,1)S(1)}, u32[]{:S(2)}, u32[]{:S(2)}) %collective-permute-start.44) | collective-permute-done | bytes 1179680 | tf_op jit(solution)/shard_map/ppermute | solution.py:39
  255.6 1.5 collective-permute-done.45
  257.2 3.0 fusion.5
  260.1 1.5 collective-permute-start.46
  261.7 1.6 collective-permute-start.47
  264.1 11.5 %project_back.2 = (bf16[4,2,96,896]{3,2,1,0:T(8,128)(2,1)}, bf16[4,2,96,896]{3,2,1,0:T(8,128)(2,1)}, f32[512,768]{1,0:T(8,128)}) custom-call(s32[2]{0:T(128)} %pad_add_fusion.where, bf16[4,96,896]{2,1,0:T(8,128)(2,1)} %copy-done.2, bf16[4,96,896]{2,1,0:T(8,128)(2,1)} %copy-done.3, bf16[4,96,896]{2,1,0:T(8,128)(2,1)} %copy-done.4, ...), custom_call_target="tpu_custom_call" | custom-call | flops 3300000000 | bytes 8800000 | tf_op jit(solution)/shard_map/project_back/pallas_call | solution.py:902
  276.8 2.0 fusion.1
  278.9 3.8 %collective-permute-start.50 = (bf16[96,1536]{1,0:T(8,128)(2,1)S(1)}, bf16[96,1536]{1,0:T(8,128)(2,1)S(1)}, u32[]{:S(2)}, u32[]{:S(2)}) collective-permute-start(bf16[96,1536]{1,0:T(8,128)(2,1)S(1)} %slice_bitcast_fusion.1), channel_id=1, source_target_pairs={{0,3},{1,0},{2,1},{3,2},{4,7},{5,4},{6,5},{7,6},{8,11},{9,8},{10,9... | collective-permute-start | bytes 884744 | tf_op jit(solution)/shard_map/ppermute | solution.py:35
  284.8 12.1 %project_back.3 = (bf16[4,2,96,896]{3,2,1,0:T(8,128)(2,1)}, bf16[4,2,96,896]{3,2,1,0:T(8,128)(2,1)}, bf16[512,768]{1,0:T(8,128)(2,1)}) custom-call(s32[2]{0:T(128)} %pad_add_fusion.where, bf16[4,96,896]{2,1,0:T(8,128)(2,1)} %copy-done.2, bf16[4,96,896]{2,1,0:T(8,128)(2,1)} %copy-done.3, bf16[4,96,896]{2,1,0:T(8,128)(2,1)} %copy-done.4, ...), custom_call_target="tpu_custom_call" | custom-call | flops 3300000000 | bytes 8800000 | tf_op jit(solution)/shard_map/project_back/pallas_call | solution.py:902
  296.9 4.7 %collective-permute-done.51 = bf16[96,1536]{1,0:T(8,128)(2,1)} collective-permute-done((bf16[96,1536]{1,0:T(8,128)(2,1)S(1)}, bf16[96,1536]{1,0:T(8,128)(2,1)}, u32[]{:S(2)}, u32[]{:S(2)}) %collective-permute-start.51) | collective-permute-done | bytes 294944 | tf_op jit(solution)/shard_map/ppermute | solution.py:35
  302.0 3.0 collective-permute-done.52
  310.9 1.6 slice.295
  312.6 3.5 collective-permute-start.55
  316.1 2.7 lay.3
  318.7 3.2 collective-permute-done.56
  321.9 7.1 %collective-permute-done.55.refs_2_ = bf16[128,768]{1,0:T(8,128)(2,1)S(1)} collective-permute-done((bf16[128,768]{1,0:T(8,128)(2,1)}, bf16[128,768]{1,0:T(8,128)(2,1)S(1)}, u32[]{:S(2)}, u32[]{:S(2)}) %collective-permute-start.55) | collective-permute-done | bytes 196640 | tf_op jit(solution)/shard_map/ppermute | solution.py:35
  329.1 1.3 fusion.10
  330.4 1.7 collective-permute-start.57
  333.3 1.8 collective-permute-start.60
  336.6 7.1 %collective-permute-done.59.refs_1_ = bf16[128,768]{1,0:T(8,128)(2,1)S(1)} collective-permute-done((bf16[128,768]{1,0:T(8,128)(2,1)S(1)}, bf16[128,768]{1,0:T(8,128)(2,1)S(1)}, u32[]{:S(2)}, u32[]{:S(2)}) %collective-permute-start.59) | collective-permute-done | bytes 196640 | tf_op jit(solution)/shard_map/ppermute | solution.py:35
  344.4 1.3 fusion.3
  347.6 1.4 collective-permute-start.63
  350.9 2.9 lay.2
  353.8 8.7 %collective-permute-done.62 = bf16[96,896]{1,0:T(8,128)(2,1)S(1)} collective-permute-done((bf16[96,896]{1,0:T(8,128)(2,1)S(1)}, bf16[96,896]{1,0:T(8,128)(2,1)S(1)}, u32[]{:S(2)}, u32[]{:S(2)}) %collective-permute-start.62) | collective-permute-done | bytes 172064 | tf_op jit(solution)/shard_map/ppermute | solution.py:35
  362.7 1.4 collective-permute-done.65
  (307 shorter events, 67.6 us)
Async XLA Ops:
  7.7 9.9 %collective-permute-start.2 = (bf16[96,896]{1,0:T(8,128)(2,1)S(1)}, bf16[96,896]{1,0:T(8,128)(2,1)S(1)}, u32[]{:S(2)}, u32[]{:S(2)}) collective-permute-start(bf16[96,896]{1,0:T(8,128)(2,1)S(1)} %fusion.19), channel_id=1, source_target_pairs={{0,3},{1,0},{2,1},{3,2},{4,7},{5,4},{6,5},{7,6},{8,11},{9,8},{10,9... | collective-permute-start | bytes 516104 | tf_op jit(solution)/shard_map/ppermute | solution.py:35
  12.8 14.6 %collective-permute-start.1 = (bf16[96,896]{1,0:T(8,128)(2,1)S(1)}, bf16[96,896]{1,0:T(8,128)(2,1)S(1)}, u32[]{:S(2)}, u32[]{:S(2)}) collective-permute-start(bf16[96,896]{1,0:T(8,128)(2,1)S(1)} %fusion.19), channel_id=1, source_target_pairs={{0,2},{1,3},{2,0},{3,1},{4,6},{5,7},{6,4},{7,5},{8,10},{9,11},{10,... | collective-permute-start | bytes 516104 | tf_op jit(solution)/shard_map/ppermute | solution.py:35
  12.8 14.6 %collective-permute-start = (bf16[96,896]{1,0:T(8,128)(2,1)S(1)}, bf16[96,896]{1,0:T(8,128)(2,1)S(1)}, u32[]{:S(2)}, u32[]{:S(2)}) collective-permute-start(bf16[96,896]{1,0:T(8,128)(2,1)S(1)} %fusion.19), channel_id=1, source_target_pairs={{0,1},{1,2},{2,3},{3,0},{4,5},{5,6},{6,7},{7,4},{8,9},{9,10},{10,1... | collective-permute-start | bytes 516104 | tf_op jit(solution)/shard_map/ppermute | solution.py:35
  27.5 24.1 %collective-permute-start.3 = (bf16[4,96,896]{2,1,0:T(8,128)(2,1)S(1)}, bf16[4,96,896]{2,1,0:T(8,128)(2,1)S(1)}, u32[]{:S(2)}, u32[]{:S(2)}) collective-permute-start(bf16[4,96,896]{2,1,0:T(8,128)(2,1)S(1)} %pad_maximum_fusion.6.refs_0_), channel_id=1, source_target_pairs={{0,8},{8,0},{16,24},{24,16},{1,9},{9,1},{17,25},{25,17},{2,10},{10... | collective-permute-start | bytes 2064392 | tf_op jit(solution)/shard_map/ppermute | solution.py:39
  29.6 22.8 %collective-permute-start.4 = (bf16[4,96,896]{2,1,0:T(8,128)(2,1)S(1)}, bf16[4,96,896]{2,1,0:T(8,128)(2,1)S(1)}, u32[]{:S(2)}, u32[]{:S(2)}) collective-permute-start(bf16[4,96,896]{2,1,0:T(8,128)(2,1)S(1)} %pad_maximum_fusion.6.refs_0_), channel_id=1, source_target_pairs={{0,16},{8,24},{16,0},{24,8},{1,17},{9,25},{17,1},{25,9},{2,18},{10... | collective-permute-start | bytes 2064392 | tf_op jit(solution)/shard_map/ppermute | solution.py:39
  32.0 10.9 %collective-permute-start.5 = (bf16[160,768]{1,0:T(8,128)(2,1)}, bf16[160,768]{1,0:T(8,128)(2,1)S(1)}, u32[]{:S(2)}, u32[]{:S(2)}) collective-permute-start(bf16[160,768]{1,0:T(8,128)(2,1)} %get-tuple-element.502), channel_id=1, source_target_pairs={{0,1},{1,2},{2,3},{3,0},{4,5},{5,6},{6,7},{7,4},{8,9},{9,10},{10,1... | collective-permute-start | bytes 737288 | tf_op jit(solution)/shard_map/ppermute | solution.py:35
  32.9 18.7 %collective-permute-start.6 = (bf16[160,768]{1,0:T(8,128)(2,1)}, bf16[160,768]{1,0:T(8,128)(2,1)S(1)}, u32[]{:S(2)}, u32[]{:S(2)}) collective-permute-start(bf16[160,768]{1,0:T(8,128)(2,1)} %get-tuple-element.501), channel_id=1, source_target_pairs={{0,2},{1,3},{2,0},{3,1},{4,6},{5,7},{6,4},{7,5},{8,10},{9,11},{10,... | collective-permute-start | bytes 737288 | tf_op jit(solution)/shard_map/ppermute | solution.py:35
  34.8 16.8 %collective-permute-start.7 = (bf16[160,768]{1,0:T(8,128)(2,1)S(1)}, bf16[160,768]{1,0:T(8,128)(2,1)S(1)}, u32[]{:S(2)}, u32[]{:S(2)}) collective-permute-start(bf16[160,768]{1,0:T(8,128)(2,1)S(1)} %get-tuple-element.500), channel_id=1, source_target_pairs={{0,3},{1,0},{2,1},{3,2},{4,7},{5,4},{6,5},{7,6},{8,11},{9,8},{10,9... | collective-permute-start | bytes 737288 | tf_op jit(solution)/shard_map/ppermute | solution.py:35
  52.4 12.4 %collective-permute-start.10 = (bf16[4,96,896]{2,1,0:T(8,128)(2,1)S(1)}, bf16[4,96,896]{2,1,0:T(8,128)(2,1)S(1)}, u32[]{:S(2)}, u32[]{:S(2)}) collective-permute-start(bf16[4,96,896]{2,1,0:T(8,128)(2,1)S(1)} %pad_maximum_fusion.6.refs_0_), channel_id=1, source_target_pairs={{0,4},{4,0},{1,5},{5,1},{2,6},{6,2},{3,7},{7,3},{8,12},{12,8},{9,1... | collective-permute-start | bytes 2064392 | tf_op jit(solution)/shard_map/ppermute | solution.py:43
  52.5 12.3 %collective-permute-start.11 = (bf16[4,96,896]{2,1,0:T(8,128)(2,1)S(1)}, bf16[4,96,896]{2,1,0:T(8,128)(2,1)S(1)}, u32[]{:S(2)}, u32[]{:S(2)}) collective-permute-start(bf16[4,96,896]{2,1,0:T(8,128)(2,1)S(1)} %collective-permute-done.3.refs_1_), channel_id=1, source_target_pairs={{0,4},{4,0},{1,5},{5,1},{2,6},{6,2},{3,7},{7,3},{8,12},{12,8},{9,1... | collective-permute-start | bytes 2064392 | tf_op jit(solution)/shard_map/ppermute | solution.py:43
  53.0 11.8 %collective-permute-start.12 = (bf16[4,96,896]{2,1,0:T(8,128)(2,1)S(1)}, bf16[4,96,896]{2,1,0:T(8,128)(2,1)S(1)}, u32[]{:S(2)}, u32[]{:S(2)}) collective-permute-start(bf16[4,96,896]{2,1,0:T(8,128)(2,1)S(1)} %collective-permute-done.4.refs_2_), channel_id=1, source_target_pairs={{0,4},{4,0},{1,5},{5,1},{2,6},{6,2},{3,7},{7,3},{8,12},{12,8},{9,1... | collective-permute-start | bytes 2064392 | tf_op jit(solution)/shard_map/ppermute | solution.py:43
  54.1 10.5 %collective-permute-start.8 = (bf16[2,96,896]{2,1,0:T(8,128)(2,1)S(1)}, bf16[2,96,896]{2,1,0:T(8,128)(2,1)S(1)}, u32[]{:S(2)}, u32[]{:S(2)}) collective-permute-start(bf16[2,96,896]{2,1,0:T(8,128)(2,1)S(1)} %slice.248), channel_id=1, source_target_pairs={{0,16},{8,24},{16,0},{24,8},{1,17},{9,25},{17,1},{25,9},{2,18},{10... | collective-permute-start | bytes 1032200 | tf_op jit(solution)/shard_map/ppermute | solution.py:39
  54.7 10.1 %collective-permute-start.9 = (bf16[2,96,896]{2,1,0:T(8,128)(2,1)S(1)}, bf16[2,96,896]{2,1,0:T(8,128)(2,1)S(1)}, u32[]{:S(2)}, u32[]{:S(2)}) collective-permute-start(bf16[2,96,896]{2,1,0:T(8,128)(2,1)S(1)} %slice.249), channel_id=1, source_target_pairs={{0,8},{8,0},{16,24},{24,16},{1,9},{9,1},{17,25},{25,17},{2,10},{10... | collective-permute-start | bytes 1032200 | tf_op jit(solution)/shard_map/ppermute | solution.py:39
  65.9 3.7 collective-permute-start.14
  65.9 2.9 collective-permute-start.13
  69.6 20.4 %collective-permute-start.17 = (bf16[96,768]{1,0:T(8,128)(2,1)S(1)}, bf16[96,768]{1,0:T(8,128)(2,1)S(1)}, u32[]{:S(2)}, u32[]{:S(2)}) collective-permute-start(bf16[96,768]{1,0:T(8,128)(2,1)S(1)} %constant_dynamic-slice_fusion.3), channel_id=1, source_target_pairs={{0,3},{1,0},{2,1},{3,2},{4,7},{5,4},{6,5},{7,6},{8,11},{9,8},{10,9... | collective-permute-start | bytes 442376 | tf_op jit(solution)/shard_map/ppermute | solution.py:35
  76.3 13.7 %collective-permute-start.16 = (bf16[96,768]{1,0:T(8,128)(2,1)S(1)}, bf16[96,768]{1,0:T(8,128)(2,1)S(1)}, u32[]{:S(2)}, u32[]{:S(2)}) collective-permute-start(bf16[96,768]{1,0:T(8,128)(2,1)S(1)} %constant_dynamic-slice_fusion.3), channel_id=1, source_target_pairs={{0,2},{1,3},{2,0},{3,1},{4,6},{5,7},{6,4},{7,5},{8,10},{9,11},{10,... | collective-permute-start | bytes 442376 | tf_op jit(solution)/shard_map/ppermute | solution.py:35
  76.3 13.7 %collective-permute-start.15 = (bf16[96,768]{1,0:T(8,128)(2,1)S(1)}, bf16[96,768]{1,0:T(8,128)(2,1)S(1)}, u32[]{:S(2)}, u32[]{:S(2)}) collective-permute-start(bf16[96,768]{1,0:T(8,128)(2,1)S(1)} %constant_dynamic-slice_fusion.3), channel_id=1, source_target_pairs={{0,1},{1,2},{2,3},{3,0},{4,5},{5,6},{6,7},{7,4},{8,9},{9,10},{10,1... | collective-permute-start | bytes 442376 | tf_op jit(solution)/shard_map/ppermute | solution.py:35
  90.2 22.0 %collective-permute-start.18 = (bf16[4,96,768]{2,1,0:T(8,128)(2,1)S(1)}, bf16[4,96,768]{2,1,0:T(8,128)(2,1)S(1)}, u32[]{:S(2)}, u32[]{:S(2)}) collective-permute-start(bf16[4,96,768]{2,1,0:T(8,128)(2,1)S(1)} %pad_maximum_fusion.9.refs_0_), channel_id=1, source_target_pairs={{0,8},{8,0},{16,24},{24,16},{1,9},{9,1},{17,25},{25,17},{2,10},{10... | collective-permute-start | bytes 1769480 | tf_op jit(solution)/shard_map/ppermute | solution.py:39
  90.6 21.5 %collective-permute-start.19 = (bf16[4,96,768]{2,1,0:T(8,128)(2,1)S(1)}, bf16[4,96,768]{2,1,0:T(8,128)(2,1)S(1)}, u32[]{:S(2)}, u32[]{:S(2)}) collective-permute-start(bf16[4,96,768]{2,1,0:T(8,128)(2,1)S(1)} %pad_maximum_fusion.9.refs_0_), channel_id=1, source_target_pairs={{0,16},{8,24},{16,0},{24,8},{1,17},{9,25},{17,1},{25,9},{2,18},{10... | collective-permute-start | bytes 1769480 | tf_op jit(solution)/shard_map/ppermute | solution.py:39
  92.3 19.9 %collective-permute-start.20 = (bf16[4,96,768]{2,1,0:T(8,128)(2,1)S(1)}, bf16[4,96,768]{2,1,0:T(8,128)(2,1)S(1)}, u32[]{:S(2)}, u32[]{:S(2)}) collective-permute-start(bf16[4,96,768]{2,1,0:T(8,128)(2,1)S(1)} %pad_maximum_fusion.9.refs_0_), channel_id=1, source_target_pairs={{0,4},{4,0},{1,5},{5,1},{2,6},{6,2},{3,7},{7,3},{8,12},{12,8},{9,1... | collective-permute-start | bytes 1769480 | tf_op jit(solution)/shard_map/ppermute | solution.py:43
  93.0 19.1 %collective-permute-start.21 = (bf16[224,768]{1,0:T(8,128)(2,1)}, bf16[224,768]{1,0:T(8,128)(2,1)}, u32[]{:S(2)}, u32[]{:S(2)}) collective-permute-start(bf16[224,768]{1,0:T(8,128)(2,1)} %pad_maximum_fusion.17), channel_id=1, source_target_pairs={{0,2},{1,3},{2,0},{3,1},{4,6},{5,7},{6,4},{7,5},{8,10},{9,11},{10,... | collective-permute-start | bytes 1032200 | tf_op jit(solution)/shard_map/ppermute | solution.py:35
  96.2 13.3 %collective-permute-start.22 = (bf16[2,72,768]{2,1,0:T(8,128)(2,1)}, bf16[2,72,768]{2,1,0:T(8,128)(2,1)S(1)}, u32[]{:S(2)}, u32[]{:S(2)}) collective-permute-start(bf16[2,72,768]{2,1,0:T(8,128)(2,1)} %get-tuple-element.275), channel_id=1, source_target_pairs={{0,4},{4,0},{1,5},{5,1},{2,6},{6,2},{3,7},{7,3},{8,12},{12,8},{9,1... | collective-permute-start | bytes 663560 | tf_op jit(solution)/shard_map/ppermute | solution.py:43
  114.6 15.5 %collective-permute-start.23 = (bf16[2,96,768]{2,1,0:T(8,128)(2,1)}, bf16[2,96,768]{2,1,0:T(8,128)(2,1)}, u32[]{:S(2)}, u32[]{:S(2)}) collective-permute-start(bf16[2,96,768]{2,1,0:T(8,128)(2,1)} %slice.260), channel_id=1, source_target_pairs={{0,16},{8,24},{16,0},{24,8},{1,17},{9,25},{17,1},{25,9},{2,18},{10... | collective-permute-start | bytes 884744 | tf_op jit(solution)/shard_map/ppermute | solution.py:39
  115.7 14.4 %collective-permute-start.24 = (bf16[2,96,768]{2,1,0:T(8,128)(2,1)}, bf16[2,96,768]{2,1,0:T(8,128)(2,1)}, u32[]{:S(2)}, u32[]{:S(2)}) collective-permute-start(bf16[2,96,768]{2,1,0:T(8,128)(2,1)} %slice.261), channel_id=1, source_target_pairs={{0,8},{8,0},{16,24},{24,16},{1,9},{9,1},{17,25},{25,17},{2,10},{10... | collective-permute-start | bytes 884744 | tf_op jit(solution)/shard_map/ppermute | solution.py:39
  118.2 13.0 %collective-permute-start.25 = (bf16[224,768]{1,0:T(8,128)(2,1)}, bf16[224,768]{1,0:T(8,128)(2,1)S(1)}, u32[]{:S(2)}, u32[]{:S(2)}) collective-permute-start(bf16[224,768]{1,0:T(8,128)(2,1)} %get-tuple-element.499), channel_id=1, source_target_pairs={{0,1},{1,2},{2,3},{3,0},{4,5},{5,6},{6,7},{7,4},{8,9},{9,10},{10,1... | collective-permute-start | bytes 1032200 | tf_op jit(solution)/shard_map/ppermute | solution.py:35
  118.5 16.5 %collective-permute-start.26 = (bf16[224,768]{1,0:T(8,128)(2,1)S(1)}, bf16[224,768]{1,0:T(8,128)(2,1)S(1)}, u32[]{:S(2)}, u32[]{:S(2)}) collective-permute-start(bf16[224,768]{1,0:T(8,128)(2,1)S(1)} %get-tuple-element.498), channel_id=1, source_target_pairs={{0,3},{1,0},{2,1},{3,2},{4,7},{5,4},{6,5},{7,6},{8,11},{9,8},{10,9... | collective-permute-start | bytes 1032200 | tf_op jit(solution)/shard_map/ppermute | solution.py:35
  122.0 8.1 %collective-permute-start.27 = (bf16[2,72,768]{2,1,0:T(8,128)(2,1)}, bf16[2,72,768]{2,1,0:T(8,128)(2,1)S(1)}, u32[]{:S(2)}, u32[]{:S(2)}) collective-permute-start(bf16[2,72,768]{2,1,0:T(8,128)(2,1)} %get-tuple-element.288), channel_id=1, source_target_pairs={{0,4},{4,0},{1,5},{5,1},{2,6},{6,2},{3,7},{7,3},{8,12},{12,8},{9,1... | collective-permute-start | bytes 663560 | tf_op jit(solution)/shard_map/ppermute | solution.py:43
  136.9 18.9 %collective-permute-start.28 = (bf16[4,96,768]{2,1,0:T(8,128)(2,1)}, bf16[4,96,768]{2,1,0:T(8,128)(2,1)}, u32[]{:S(2)}, u32[]{:S(2)}) collective-permute-start(bf16[4,96,768]{2,1,0:T(8,128)(2,1)} %pad_maximum_fusion.10.refs_0_), channel_id=1, source_target_pairs={{0,8},{8,0},{16,24},{24,16},{1,9},{9,1},{17,25},{25,17},{2,10},{10... | collective-permute-start | bytes 1769480 | tf_op jit(solution)/shard_map/ppermute | solution.py:39
  137.4 18.4 %collective-permute-start.29 = (bf16[4,96,768]{2,1,0:T(8,128)(2,1)}, bf16[4,96,768]{2,1,0:T(8,128)(2,1)}, u32[]{:S(2)}, u32[]{:S(2)}) collective-permute-start(bf16[4,96,768]{2,1,0:T(8,128)(2,1)} %pad_maximum_fusion.10.refs_0_), channel_id=1, source_target_pairs={{0,16},{8,24},{16,0},{24,8},{1,17},{9,25},{17,1},{25,9},{2,18},{10... | collective-permute-start | bytes 1769480 | tf_op jit(solution)/shard_map/ppermute | solution.py:39
  141.7 14.1 %collective-permute-start.30 = (bf16[4,96,768]{2,1,0:T(8,128)(2,1)S(1)}, bf16[4,96,768]{2,1,0:T(8,128)(2,1)S(1)}, u32[]{:S(2)}, u32[]{:S(2)}) collective-permute-start(bf16[4,96,768]{2,1,0:T(8,128)(2,1)S(1)} %collective-permute-done.18.refs_1_), channel_id=1, source_target_pairs={{0,4},{4,0},{1,5},{5,1},{2,6},{6,2},{3,7},{7,3},{8,12},{12,8},{9,1... | collective-permute-start | bytes 1769480 | tf_op jit(solution)/shard_map/ppermute | solution.py:43
  141.8 14.0 %collective-permute-start.31 = (bf16[4,96,768]{2,1,0:T(8,128)(2,1)S(1)}, bf16[4,96,768]{2,1,0:T(8,128)(2,1)}, u32[]{:S(2)}, u32[]{:S(2)}) collective-permute-start(bf16[4,96,768]{2,1,0:T(8,128)(2,1)S(1)} %collective-permute-done.19.refs_2_), channel_id=1, source_target_pairs={{0,4},{4,0},{1,5},{5,1},{2,6},{6,2},{3,7},{7,3},{8,12},{12,8},{9,1... | collective-permute-start | bytes 1769480 | tf_op jit(solution)/shard_map/ppermute | solution.py:43
  143.2 12.5 %collective-permute-start.32 = (bf16[4,96,768]{2,1,0:T(8,128)(2,1)S(1)}, bf16[4,96,768]{2,1,0:T(8,128)(2,1)}, u32[]{:S(2)}, u32[]{:S(2)}) collective-permute-start(bf16[4,96,768]{2,1,0:T(8,128)(2,1)S(1)} %constant_dynamic-update-slice_fusion.2.refs_3_), channel_id=1, source_target_pairs={{0,4},{4,0},{1,5},{5,1},{2,6},{6,2},{3,7},{7,3},{8,12},{12,8},{9,1... | collective-permute-start | bytes 1769480 | tf_op jit(solution)/shard_map/ppermute | solution.py:43
  155.8 16.2 %collective-permute-start.35 = (bf16[4,96,768]{2,1,0:T(8,128)(2,1)}, bf16[4,96,768]{2,1,0:T(8,128)(2,1)S(1)}, u32[]{:S(2)}, u32[]{:S(2)}) collective-permute-start(bf16[4,96,768]{2,1,0:T(8,128)(2,1)} %pad_maximum_fusion.10.refs_0_), channel_id=1, source_target_pairs={{0,4},{4,0},{1,5},{5,1},{2,6},{6,2},{3,7},{7,3},{8,12},{12,8},{9,1... | collective-permute-start | bytes 1769480 | tf_op jit(solution)/shard_map/ppermute | solution.py:43
  156.2 15.8 %collective-permute-start.36 = (bf16[4,96,768]{2,1,0:T(8,128)(2,1)}, bf16[4,96,768]{2,1,0:T(8,128)(2,1)S(1)}, u32[]{:S(2)}, u32[]{:S(2)}) collective-permute-start(bf16[4,96,768]{2,1,0:T(8,128)(2,1)} %collective-permute-done.28.refs_1_), channel_id=1, source_target_pairs={{0,4},{4,0},{1,5},{5,1},{2,6},{6,2},{3,7},{7,3},{8,12},{12,8},{9,1... | collective-permute-start | bytes 1769480 | tf_op jit(solution)/shard_map/ppermute | solution.py:43
  156.4 15.6 %collective-permute-start.37 = (bf16[4,96,768]{2,1,0:T(8,128)(2,1)}, bf16[4,96,768]{2,1,0:T(8,128)(2,1)S(1)}, u32[]{:S(2)}, u32[]{:S(2)}) collective-permute-start(bf16[4,96,768]{2,1,0:T(8,128)(2,1)} %collective-permute-done.29.refs_2_), channel_id=1, source_target_pairs={{0,4},{4,0},{1,5},{5,1},{2,6},{6,2},{3,7},{7,3},{8,12},{12,8},{9,1... | collective-permute-start | bytes 1769480 | tf_op jit(solution)/shard_map/ppermute | solution.py:43
  158.7 13.3 %collective-permute-start.33 = (bf16[2,96,768]{2,1,0:T(8,128)(2,1)S(1)}, bf16[2,96,768]{2,1,0:T(8,128)(2,1)S(1)}, u32[]{:S(2)}, u32[]{:S(2)}) collective-permute-start(bf16[2,96,768]{2,1,0:T(8,128)(2,1)S(1)} %slice.272), channel_id=1, source_target_pairs={{0,16},{8,24},{16,0},{24,8},{1,17},{9,25},{17,1},{25,9},{2,18},{10... | collective-permute-start | bytes 884744 | tf_op jit(solution)/shard_map/ppermute | solution.py:39
  159.2 12.8 %collective-permute-start.34 = (bf16[2,96,768]{2,1,0:T(8,128)(2,1)S(1)}, bf16[2,96,768]{2,1,0:T(8,128)(2,1)S(1)}, u32[]{:S(2)}, u32[]{:S(2)}) collective-permute-start(bf16[2,96,768]{2,1,0:T(8,128)(2,1)S(1)} %slice.273), channel_id=1, source_target_pairs={{0,8},{8,0},{16,24},{24,16},{1,9},{9,1},{17,25},{25,17},{2,10},{10... | collective-permute-start | bytes 884744 | tf_op jit(solution)/shard_map/ppermute | solution.py:39
  192.3 13.1 %collective-permute-start.39 = (bf16[128,768]{1,0:T(8,128)(2,1)S(1)}, bf16[128,768]{1,0:T(8,128)(2,1)S(1)}, u32[]{:S(2)}, u32[]{:S(2)}) collective-permute-start(bf16[128,768]{1,0:T(8,128)(2,1)S(1)} %slice.274), channel_id=1, source_target_pairs={{0,2},{1,3},{2,0},{3,1},{4,6},{5,7},{6,4},{7,5},{8,10},{9,11},{10,... | collective-permute-start | bytes 589832 | tf_op jit(solution)/shard_map/ppermute | solution.py:35
  206.1 13.6 %collective-permute-start.40 = (bf16[4,4,96,1536]{3,2,1,0:T(8,128)(2,1)}, bf16[4,4,96,1536]{3,2,1,0:T(8,128)(2,1)}, u32[]{:S(2)}, u32[]{:S(2)}) collective-permute-start(bf16[4,4,96,1536]{3,2,1,0:T(8,128)(2,1)} %get-tuple-element.340), channel_id=1, source_target_pairs={{0,4},{4,0},{1,5},{5,1},{2,6},{6,2},{3,7},{7,3},{8,12},{12,8},{9,1... | collective-permute-start | bytes 14155784 | tf_op jit(solution)/shard_map/ppermute | solution.py:43
  206.9 12.8 %collective-permute-start.41 = (bf16[128,768]{1,0:T(8,128)(2,1)S(1)}, bf16[128,768]{1,0:T(8,128)(2,1)S(1)}, u32[]{:S(2)}, u32[]{:S(2)}) collective-permute-start(bf16[128,768]{1,0:T(8,128)(2,1)S(1)} %get-tuple-element.478), channel_id=1, source_target_pairs={{0,3},{1,0},{2,1},{3,2},{4,7},{5,4},{6,5},{7,6},{8,11},{9,8},{10,9... | collective-permute-start | bytes 589832 | tf_op jit(solution)/shard_map/ppermute | solution.py:35
  209.2 10.5 %collective-permute-start.42 = (bf16[128,768]{1,0:T(8,128)(2,1)S(1)}, bf16[128,768]{1,0:T(8,128)(2,1)S(1)}, u32[]{:S(2)}, u32[]{:S(2)}) collective-permute-start(bf16[128,768]{1,0:T(8,128)(2,1)S(1)} %get-tuple-element.477), channel_id=1, source_target_pairs={{0,1},{1,2},{2,3},{3,0},{4,5},{5,6},{6,7},{7,4},{8,9},{9,10},{10,1... | collective-permute-start | bytes 589832 | tf_op jit(solution)/shard_map/ppermute | solution.py:35
  227.5 28.2 %collective-permute-start.44 = (bf16[2,2,96,1536]{3,2,1,0:T(8,128)(2,1)S(1)}, bf16[2,2,96,1536]{3,2,1,0:T(8,128)(2,1)S(1)}, u32[]{:S(2)}, u32[]{:S(2)}) collective-permute-start(bf16[2,2,96,1536]{3,2,1,0:T(8,128)(2,1)S(1)} %pad_maximum_fusion.1), channel_id=1, source_target_pairs={{0,8},{8,0},{16,24},{24,16},{1,9},{9,1},{17,25},{25,17},{2,10},{10... | collective-permute-start | bytes 3538952 | tf_op jit(solution)/shard_map/ppermute | solution.py:39
  229.1 28.0 %collective-permute-start.45 = (bf16[2,2,96,1536]{3,2,1,0:T(8,128)(2,1)}, bf16[2,2,96,1536]{3,2,1,0:T(8,128)(2,1)S(1)}, u32[]{:S(2)}, u32[]{:S(2)}) collective-permute-start(bf16[2,2,96,1536]{3,2,1,0:T(8,128)(2,1)} %pad_maximum_fusion.2), channel_id=1, source_target_pairs={{0,16},{8,24},{16,0},{24,8},{1,17},{9,25},{17,1},{25,9},{2,18},{10... | collective-permute-start | bytes 3538952 | tf_op jit(solution)/shard_map/ppermute | solution.py:39
  239.9 9.4 %collective-permute-start.43 = (bf16[2,72,768]{2,1,0:T(8,128)(2,1)}, bf16[2,72,768]{2,1,0:T(8,128)(2,1)S(1)}, u32[]{:S(2)}, u32[]{:S(2)}) collective-permute-start(bf16[2,72,768]{2,1,0:T(8,128)(2,1)} %get-tuple-element.357), channel_id=1, source_target_pairs={{0,4},{4,0},{1,5},{5,1},{2,6},{6,2},{3,7},{7,3},{8,12},{12,8},{9,1... | collective-permute-start | bytes 663560 | tf_op jit(solution)/shard_map/ppermute | solution.py:43
  260.1 15.5 %collective-permute-start.46 = (bf16[2,96,1536]{2,1,0:T(8,128)(2,1)}, bf16[2,96,1536]{2,1,0:T(8,128)(2,1)S(1)}, u32[]{:S(2)}, u32[]{:S(2)}) collective-permute-start(bf16[2,96,1536]{2,1,0:T(8,128)(2,1)} %get-tuple-element.463), channel_id=1, source_target_pairs={{0,8},{8,0},{16,24},{24,16},{1,9},{9,1},{17,25},{25,17},{2,10},{10... | collective-permute-start | bytes 1769480 | tf_op jit(solution)/shard_map/ppermute | solution.py:39
  261.7 14.4 %collective-permute-start.47 = (bf16[2,96,1536]{2,1,0:T(8,128)(2,1)}, bf16[2,96,1536]{2,1,0:T(8,128)(2,1)}, u32[]{:S(2)}, u32[]{:S(2)}) collective-permute-start(bf16[2,96,1536]{2,1,0:T(8,128)(2,1)} %get-tuple-element.462), channel_id=1, source_target_pairs={{0,16},{8,24},{16,0},{24,8},{1,17},{9,25},{17,1},{25,9},{2,18},{10... | collective-permute-start | bytes 1769480 | tf_op jit(solution)/shard_map/ppermute | solution.py:39
  263.3 12.3 %collective-permute-start.48 = (bf16[2,72,768]{2,1,0:T(8,128)(2,1)S(1)}, bf16[2,72,768]{2,1,0:T(8,128)(2,1)S(1)}, u32[]{:S(2)}, u32[]{:S(2)}) collective-permute-start(bf16[2,72,768]{2,1,0:T(8,128)(2,1)S(1)} %copy-done.35), channel_id=1, source_target_pairs={{0,4},{4,0},{1,5},{5,1},{2,6},{6,2},{3,7},{7,3},{8,12},{12,8},{9,1... | collective-permute-start | bytes 663560 | tf_op jit(solution)/shard_map/ppermute | solution.py:43
  276.3 25.3 %collective-permute-start.49 = (bf16[4,2,96,896]{3,2,1,0:T(8,128)(2,1)}, bf16[4,2,96,896]{3,2,1,0:T(8,128)(2,1)S(1)}, u32[]{:S(2)}, u32[]{:S(2)}) collective-permute-start(bf16[4,2,96,896]{3,2,1,0:T(8,128)(2,1)} %get-tuple-element.386), channel_id=1, source_target_pairs={{0,4},{4,0},{1,5},{5,1},{2,6},{6,2},{3,7},{7,3},{8,12},{12,8},{9,1... | collective-permute-start | bytes 4128776 | tf_op jit(solution)/shard_map/ppermute | solution.py:43
  278.9 17.9 %collective-permute-start.50 = (bf16[96,1536]{1,0:T(8,128)(2,1)S(1)}, bf16[96,1536]{1,0:T(8,128)(2,1)S(1)}, u32[]{:S(2)}, u32[]{:S(2)}) collective-permute-start(bf16[96,1536]{1,0:T(8,128)(2,1)S(1)} %slice_bitcast_fusion.1), channel_id=1, source_target_pairs={{0,3},{1,0},{2,1},{3,2},{4,7},{5,4},{6,5},{7,6},{8,11},{9,8},{10,9... | collective-permute-start | bytes 884744 | tf_op jit(solution)/shard_map/ppermute | solution.py:35
  282.8 18.8 %collective-permute-start.51 = (bf16[96,1536]{1,0:T(8,128)(2,1)S(1)}, bf16[96,1536]{1,0:T(8,128)(2,1)}, u32[]{:S(2)}, u32[]{:S(2)}) collective-permute-start(bf16[96,1536]{1,0:T(8,128)(2,1)S(1)} %slice_bitcast_fusion), channel_id=1, source_target_pairs={{0,2},{1,3},{2,0},{3,1},{4,6},{5,7},{6,4},{7,5},{8,10},{9,11},{10,... | collective-permute-start | bytes 884744 | tf_op jit(solution)/shard_map/ppermute | solution.py:35
  301.6 3.3 collective-permute-start.52
  306.6 22.4 %collective-permute-start.53 = (bf16[2,2,96,896]{3,2,1,0:T(8,128)(2,1)}, bf16[2,2,96,896]{3,2,1,0:T(8,128)(2,1)}, u32[]{:S(2)}, u32[]{:S(2)}) collective-permute-start(bf16[2,2,96,896]{3,2,1,0:T(8,128)(2,1)} %pad_maximum_fusion.7), channel_id=1, source_target_pairs={{0,8},{8,0},{16,24},{24,16},{1,9},{9,1},{17,25},{25,17},{2,10},{10... | collective-permute-start | bytes 2064392 | tf_op jit(solution)/shard_map/ppermute | solution.py:39
  308.0 21.1 %collective-permute-start.54 = (bf16[2,2,96,896]{3,2,1,0:T(8,128)(2,1)}, bf16[2,2,96,896]{3,2,1,0:T(8,128)(2,1)}, u32[]{:S(2)}, u32[]{:S(2)}) collective-permute-start(bf16[2,2,96,896]{3,2,1,0:T(8,128)(2,1)} %pad_maximum_fusion.8), channel_id=1, source_target_pairs={{0,16},{8,24},{16,0},{24,8},{1,17},{9,25},{17,1},{25,9},{2,18},{10... | collective-permute-start | bytes 2064392 | tf_op jit(solution)/shard_map/ppermute | solution.py:39
  310.0 12.0 %collective-permute-start.56 = (bf16[96,1536]{1,0:T(8,128)(2,1)S(1)}, bf16[96,1536]{1,0:T(8,128)(2,1)}, u32[]{:S(2)}, u32[]{:S(2)}) collective-permute-start(bf16[96,1536]{1,0:T(8,128)(2,1)S(1)} %slice_bitcast_fusion.2), channel_id=1, source_target_pairs={{0,1},{1,2},{2,3},{3,0},{4,5},{5,6},{6,7},{7,4},{8,9},{9,10},{10,1... | collective-permute-start | bytes 884744 | tf_op jit(solution)/shard_map/ppermute | solution.py:35
  312.6 16.5 %collective-permute-start.55 = (bf16[128,768]{1,0:T(8,128)(2,1)}, bf16[128,768]{1,0:T(8,128)(2,1)S(1)}, u32[]{:S(2)}, u32[]{:S(2)}) collective-permute-start(bf16[128,768]{1,0:T(8,128)(2,1)} %slice.295), channel_id=1, source_target_pairs={{0,2},{1,3},{2,0},{3,1},{4,6},{5,7},{6,4},{7,5},{8,10},{9,11},{10,... | collective-permute-start | bytes 589832 | tf_op jit(solution)/shard_map/ppermute | solution.py:35
  330.4 13.3 %collective-permute-start.57 = (bf16[2,96,896]{2,1,0:T(8,128)(2,1)S(1)}, bf16[2,96,896]{2,1,0:T(8,128)(2,1)S(1)}, u32[]{:S(2)}, u32[]{:S(2)}) collective-permute-start(bf16[2,96,896]{2,1,0:T(8,128)(2,1)S(1)} %get-tuple-element.471), channel_id=1, source_target_pairs={{0,8},{8,0},{16,24},{24,16},{1,9},{9,1},{17,25},{25,17},{2,10},{10... | collective-permute-start | bytes 1032200 | tf_op jit(solution)/shard_map/ppermute | solution.py:39
  332.0 12.3 %collective-permute-start.58 = (bf16[2,96,896]{2,1,0:T(8,128)(2,1)S(1)}, bf16[2,96,896]{2,1,0:T(8,128)(2,1)S(1)}, u32[]{:S(2)}, u32[]{:S(2)}) collective-permute-start(bf16[2,96,896]{2,1,0:T(8,128)(2,1)S(1)} %get-tuple-element.470), channel_id=1, source_target_pairs={{0,16},{8,24},{16,0},{24,8},{1,17},{9,25},{17,1},{25,9},{2,18},{10... | collective-permute-start | bytes 1032200 | tf_op jit(solution)/shard_map/ppermute | solution.py:39
  333.1 10.5 %collective-permute-start.59 = (bf16[128,768]{1,0:T(8,128)(2,1)S(1)}, bf16[128,768]{1,0:T(8,128)(2,1)S(1)}, u32[]{:S(2)}, u32[]{:S(2)}) collective-permute-start(bf16[128,768]{1,0:T(8,128)(2,1)S(1)} %get-tuple-element.480), channel_id=1, source_target_pairs={{0,3},{1,0},{2,1},{3,2},{4,7},{5,4},{6,5},{7,6},{8,11},{9,8},{10,9... | collective-permute-start | bytes 589832 | tf_op jit(solution)/shard_map/ppermute | solution.py:35
  333.3 10.3 %collective-permute-start.60 = (bf16[128,768]{1,0:T(8,128)(2,1)S(1)}, bf16[128,768]{1,0:T(8,128)(2,1)S(1)}, u32[]{:S(2)}, u32[]{:S(2)}) collective-permute-start(bf16[128,768]{1,0:T(8,128)(2,1)S(1)} %get-tuple-element.479), channel_id=1, source_target_pairs={{0,1},{1,2},{2,3},{3,0},{4,5},{5,6},{6,7},{7,4},{8,9},{9,10},{10,1... | collective-permute-start | bytes 589832 | tf_op jit(solution)/shard_map/ppermute | solution.py:35
  336.5 12.6 %collective-permute-start.64 = (bf16[96,1536]{1,0:T(8,128)(2,1)S(1)}, bf16[96,1536]{1,0:T(8,128)(2,1)S(1)}, u32[]{:S(2)}, u32[]{:S(2)}) collective-permute-start(bf16[96,1536]{1,0:T(8,128)(2,1)S(1)} %fusion.8), channel_id=1, source_target_pairs={{0,4},{4,0},{1,5},{5,1},{2,6},{6,2},{3,7},{7,3},{8,12},{12,8},{9,1... | collective-permute-start | bytes 884744 | tf_op jit(solution)/shard_map/ppermute | solution.py:43
  345.7 8.1 %collective-permute-start.61 = (bf16[96,896]{1,0:T(8,128)(2,1)S(1)}, bf16[96,896]{1,0:T(8,128)(2,1)S(1)}, u32[]{:S(2)}, u32[]{:S(2)}) collective-permute-start(bf16[96,896]{1,0:T(8,128)(2,1)S(1)} %get-tuple-element.496), channel_id=1, source_target_pairs={{0,3},{1,0},{2,1},{3,2},{4,7},{5,4},{6,5},{7,6},{8,11},{9,8},{10,9... | collective-permute-start | bytes 516104 | tf_op jit(solution)/shard_map/ppermute | solution.py:35
  346.6 15.9 %collective-permute-start.62 = (bf16[96,896]{1,0:T(8,128)(2,1)S(1)}, bf16[96,896]{1,0:T(8,128)(2,1)S(1)}, u32[]{:S(2)}, u32[]{:S(2)}) collective-permute-start(bf16[96,896]{1,0:T(8,128)(2,1)S(1)} %get-tuple-element.495), channel_id=1, source_target_pairs={{0,2},{1,3},{2,0},{3,1},{4,6},{5,7},{6,4},{7,5},{8,10},{9,11},{10,... | collective-permute-start | bytes 516104 | tf_op jit(solution)/shard_map/ppermute | solution.py:35
  347.6 14.9 %collective-permute-start.63 = (bf16[96,896]{1,0:T(8,128)(2,1)S(1)}, bf16[96,896]{1,0:T(8,128)(2,1)S(1)}, u32[]{:S(2)}, u32[]{:S(2)}) collective-permute-start(bf16[96,896]{1,0:T(8,128)(2,1)S(1)} %get-tuple-element.494), channel_id=1, source_target_pairs={{0,1},{1,2},{2,3},{3,0},{4,5},{5,6},{6,7},{7,4},{8,9},{9,10},{10,1... | collective-permute-start | bytes 516104 | tf_op jit(solution)/shard_map/ppermute | solution.py:35
  (56 other events, 461.0 us)
where the time goes:
time: 370 us; the launch traced here: 368 us
  Pallas kernels  138 us (37%)
  waiting for transfers between devices  86.9 us (23%)
  starting transfers between devices  69.6 us (19%)
  other arithmetic  40.2 us (11%)
  local copies, waits for them, and re-layouts  31.5 us (9%)
    ppermute x24, waiting for transfers between devices, perm_t(): lax.ppermute(value, 'tensor', [(i, (i + step) % n) for i in range(n)])  64.4 us
    ppermute x24, starting transfers between devices, perm_t(): lax.ppermute(value, 'tensor', [(i, (i + step) % n) for i in range(n)])  43.7 us
    pallas_call x2, Pallas kernels, project(): call(body, (cnt,), [SCALARS] + [ANY] * 8 + [fixed(span, z.width), slot(hd...  26 us
    pallas_call x2, Pallas kernels, project_back(): call(body, (cnt,), [SCALARS] + [ANY] * 8 + [wide, wide, slot(span, z.oc),...  23.6 us
    ppermute x20, starting transfers between devices, perm_s(): return lax.ppermute(value, 'shard', [(i, i ^ mask) for i in range(n)])  22.1 us
    pallas_call x2, Pallas kernels, attend_back(): call(body, (cnt,), [SCALARS] + [ANY] * 8 + [fixed(span, z.width), slot(sp...  18.5 us
    pallas_call x1, Pallas kernels, narrow(): call(body, (2, n), [SCALARS] + [ANY] * 8 + [fixed(span, z.width), fixed(8...  16.4 us
    ppermute x20, waiting for transfers between devices, perm_s(): return lax.ppermute(value, 'shard', [(i, i ^ mask) for i in range(n)])  16 us
  transfers between devices with their start and end apart: 66, of which 20 were waited for; matrix products, arithmetic and copies ran while one was open for 11% of the time, Pallas kernels for 33%

commit v1 on v0

--- a/solution.py
+++ b/solution.py
@@ -9,6 +9,7 @@
 
 F = jnp.float32
 B = jnp.bfloat16
+ORDER = (0, 1, 3, 2)
 
 
 def wide_add(*terms):
@@ -85,26 +86,23 @@
     def swap(self, values):
         return tuple(self.perm_c(value) for value in values)
 
-    def collect_one(self, parts):
-        h = parts.shape[1] // 2
+    def collect_one(self, low, high):
         return (
-            self.perm_s(jnp.stack([parts[3, h:], parts[1, h:]]), 1),
-            self.perm_s(jnp.stack([parts[3, :h], parts[2, :h]]), 2),
+            self.perm_s(wide_add(*[term[1:3] for term in high]).astype(B), 1),
+            self.perm_s(wide_add(*[term[2:4] for term in low]).astype(B), 2),
         )
 
-    def collect_two(self, parts, one):
-        h = parts.shape[1] // 2
+    def collect_two(self, low, high, one):
         return (
-            self.perm_s(wide_add(parts[1, :h], one[1][0]).astype(B), 1),
-            self.perm_s(wide_add(parts[2, h:], one[0][0]).astype(B), 2),
+            self.perm_s(wide_add(*[term[1] for term in low], one[1][0]).astype(B), 1),
+            self.perm_s(wide_add(*[term[3] for term in high], one[0][1]).astype(B), 2),
         )
 
-    def sums(self, parts, one, two):
-        h = parts.shape[1] // 2
+    def sums(self, low, high, one, two):
         return jnp.concatenate(
             [
-                wide_add(parts[0, :h], two[0], one[1][1]).astype(B),
-                wide_add(parts[0, h:], one[0][1], two[1]).astype(B),
+                wide_add(*[term[0] for term in low], two[0], one[1][1]).astype(B),
+                wide_add(*[term[0] for term in high], one[0][0], two[1]).astype(B),
             ]
         )
 
@@ -332,7 +330,7 @@
     for part in range(2):
         half = c if part == 0 else 1 - c
         for i in range(m):
-            src = pl.multiple_of(((s ^ i) * 2 + half) * rows, 16)
+            src = pl.multiple_of(((s ^ ORDER[i]) * 2 + half) * rows, 16)
             row = (part * m + i) * rows
             dest[row : row + rows] = spare[pl.ds(src, rows)]
 
@@ -1074,18 +1072,19 @@
     d_res_one, small_a = widen_back(z, where, pieces_u, normal, inverse, vec, dup, d_res_two)
     d_res_one, keep, other, sent = together(d_res_one, keep, other, sent)
     result = links.undealt(out, sent, B)
-    parts_f = wide_add(keep, other).astype(B)
-    one_f = links.collect_one(parts_f)
+    slots_f = keep, other
+    split = lambda slots: ([term[:, : n // 2] for term in slots], [term[:, n // 2 :] for term in slots])
+    one_f = links.collect_one(*split(slots_f))
     dq_a, d_state_a = attend_back(
         z, where, pieces_a, d_res_one, mixed[0], den[0], made[0][3], made[0][0], states[0], feat, lo
     )
-    dq_a, d_state_a, d_res_one, parts_f = together(dq_a, d_state_a, d_res_one, parts_f)
+    dq_a, d_state_a, d_res_one, slots_f = together(dq_a, d_state_a, d_res_one, slots_f)
     came = links.perm_c(d_state_a)
     dq_b, d_state_b = attend_back(
         z, where, pieces_a, d_res_one, mixed[1], den[1], made[1][3], made[1][0], states[1], feat, hi
     )
-    dq_b, d_state_b, came, one_f, parts_f, x = together(dq_b, d_state_b, came, one_f, parts_f, x)
-    two_f = links.collect_two(parts_f, one_f)
+    dq_b, d_state_b, came, one_f, slots_f, x = together(dq_b, d_state_b, came, one_f, slots_f, x)
+    two_f = links.collect_two(*split(slots_f), one_f)
     came_b = links.perm_c(d_state_b)
     d_state_a = join_grads(d_state_a, came, falls[0])
     dq = (dq_a, dq_b)
@@ -1097,8 +1096,8 @@
         )
 
     keep, give, acc = run_back(0, d_state_a, x, None)
-    keep, give, acc, two_f, came_b, parts_f, x = together(keep, give, acc, two_f, came_b, parts_f, x)
-    sums_f = links.sums(parts_f, one_f, two_f)
+    keep, give, acc, two_f, came_b, slots_f, x = together(keep, give, acc, two_f, came_b, slots_f, x)
+    sums_f = links.sums(*split(slots_f), one_f, two_f)
     terms_f = links.collect_t(sums_f, (1, 2))
     other = links.perm_c(give)
     d_state_b = join_grads(d_state_b, came_b, falls[1])
@@ -1108,17 +1107,16 @@
     )
     other_b = links.perm_c(give_b)
     terms_f += links.collect_t(sums_f, range(3, n))
-    parts = wide_add(keep, other).astype(B)
-    parts_b = wide_add(keep_b, other_b).astype(B)
-    parts, grad_x = together(jnp.concatenate([parts, parts_b], axis=1), grad_x)
-    one = links.collect_one(parts)
+    keep_b, other_b, grad_x = together(keep_b, other_b, grad_x)
+    low, high = (keep, other), (keep_b, other_b)
+    one = links.collect_one(low, high)
     sent = links.undeal_some(grad_x, (2,))
-    one, parts, sent, grad_x, terms_f = together(one, parts, sent, grad_x, terms_f)
-    two = links.collect_two(parts, one)
+    one, low, high, sent, grad_x, terms_f = together(one, low, high, sent, grad_x, terms_f)
+    two = links.collect_two(low, high, one)
     sent.update(links.undeal_some(grad_x, (1, 3)))
-    two, one, parts, sent, grad_x = together(two, one, parts, sent, grad_x)
+    two, one, low, high, sent, grad_x = together(two, one, low, high, sent, grad_x)
     grad_tokens = links.undealt(grad_x, sent, F)
-    sums = links.sums(parts, one, two)
+    sums = links.sums(low, high, one, two)
     terms = [sums[0]] + links.collect_t(sums, range(1, n))
     terms_f = [sums_f[0]] + terms_f
     own_ffn = links.collect_end(terms_f)

time: 370 us -> 363 us (0.981)
  local copies, waits for them, and re-layouts: 31.5 us -> 27.3 us
  waiting for transfers between devices: 86.9 us -> 83.1 us
    convert_element_type x7 -> x9, other arithmetic: 13.7 us -> 17.7 us  [the longest x2 6.41 us: collect_one(): wide_add(*[term[2:4] for term in low]).astype(B)]
    unnamed x117 -> x125, local copies, waits for them, and re-layouts: 9.34 us -> 6.39 us
  transfers between devices with their start and end apart: 66 -> 66, of which waited for: 20 -> 19; matrix products, arithmetic and copies ran while one was open for 11% -> 11% of each run, Pallas kernels for 33% -> 33%
where the time goes in v1:
time: 363 us; the launch traced here: 361 us
  Pallas kernels  138 us (38%)
  waiting for transfers between devices  83.1 us (23%)
  starting transfers between devices  69.8 us (19%)
  other arithmetic  40.6 us (11%)
  local copies, waits for them, and re-layouts  27.3 us (8%)
    ppermute x24, waiting for transfers between devices, perm_t(): lax.ppermute(value, 'tensor', [(i, (i + step) % n) for i in range(n)])  61.2 us
    ppermute x24, starting transfers between devices, perm_t(): lax.ppermute(value, 'tensor', [(i, (i + step) % n) for i in range(n)])  43.7 us
    pallas_call x2, Pallas kernels, project(): call(body, (cnt,), [SCALARS] + [ANY] * 8 + [fixed(span, z.width), slot(hd...  26.1 us
    pallas_call x2, Pallas kernels, project_back(): call(body, (cnt,), [SCALARS] + [ANY] * 8 + [wide, wide, slot(span, z.oc),...  23.5 us
    ppermute x20, starting transfers between devices, perm_s(): return lax.ppermute(value, 'shard', [(i, i ^ mask) for i in range(n)])  22.6 us
    pallas_call x2, Pallas kernels, attend_back(): call(body, (cnt,), [SCALARS] + [ANY] * 8 + [fixed(span, z.width), slot(sp...  18.5 us
    ppermute x20, waiting for transfers between devices, perm_s(): return lax.ppermute(value, 'shard', [(i, i ^ mask) for i in range(n)])  18.4 us
    pallas_call x1, Pallas kernels, narrow(): call(body, (2, n), [SCALARS] + [ANY] * 8 + [fixed(span, z.width), fixed(8...  16.4 us
  transfers between devices with their start and end apart: 66, of which 19 were waited for; matrix products, arithmetic and copies ran while one was open for 11% of the time, Pallas kernels for 33%

profile of v1, /device:TPU:0, one launch (start us, length us, event | category | flops | bytes accessed | tf_op | source)
XLA Modules:
  0.0 361.1 jit_solution(7250287633415204782)
XLA Ops:
  4.7 2.2 gather_rows.1
  7.6 5.1 %collective-permute-start.2 = (bf16[96,896]{1,0:T(8,128)(2,1)S(1)}, bf16[96,896]{1,0:T(8,128)(2,1)S(1)}, u32[]{:S(2)}, u32[]{:S(2)}) collective-permute-start(bf16[96,896]{1,0:T(8,128)(2,1)S(1)} %fusion.19), channel_id=1, source_target_pairs={{0,3},{1,0},{2,1},{3,2},{4,7},{5,4},{6,5},{7,6},{8,11},{9,8},{10,9... | collective-permute-start | bytes 516104 | tf_op jit(solution)/shard_map/ppermute | solution.py:36
  13.8 3.7 %collective-permute-done.2 = bf16[96,896]{1,0:T(8,128)(2,1)S(1)} collective-permute-done((bf16[96,896]{1,0:T(8,128)(2,1)S(1)}, bf16[96,896]{1,0:T(8,128)(2,1)S(1)}, u32[]{:S(2)}, u32[]{:S(2)}) %collective-permute-start.2) | collective-permute-done | bytes 172064 | tf_op jit(solution)/shard_map/ppermute | solution.py:36
  17.6 9.8 %collective-permute-done.1 = bf16[96,896]{1,0:T(8,128)(2,1)S(1)} collective-permute-done((bf16[96,896]{1,0:T(8,128)(2,1)S(1)}, bf16[96,896]{1,0:T(8,128)(2,1)S(1)}, u32[]{:S(2)}, u32[]{:S(2)}) %collective-permute-start.1) | collective-permute-done | bytes 172064 | tf_op jit(solution)/shard_map/ppermute | solution.py:36
  27.5 2.1 collective-permute-start.3
  29.6 1.5 collective-permute-start.4
  32.9 1.9 collective-permute-start.6
  34.8 2.9 collective-permute-start.7
  39.0 3.9 %collective-permute-done.5 = bf16[160,768]{1,0:T(8,128)(2,1)S(1)} collective-permute-done((bf16[160,768]{1,0:T(8,128)(2,1)}, bf16[160,768]{1,0:T(8,128)(2,1)S(1)}, u32[]{:S(2)}, u32[]{:S(2)}) %collective-permute-start.5) | collective-permute-done | bytes 245792 | tf_op jit(solution)/shard_map/ppermute | solution.py:36
  42.9 8.7 %collective-permute-done.6 = bf16[160,768]{1,0:T(8,128)(2,1)S(1)} collective-permute-done((bf16[160,768]{1,0:T(8,128)(2,1)}, bf16[160,768]{1,0:T(8,128)(2,1)S(1)}, u32[]{:S(2)}, u32[]{:S(2)}) %collective-permute-start.6) | collective-permute-done | bytes 245792 | tf_op jit(solution)/shard_map/ppermute | solution.py:36
  57.0 7.5 %collective-permute-done.8 = bf16[2,96,896]{2,1,0:T(8,128)(2,1)S(1)} collective-permute-done((bf16[2,96,896]{2,1,0:T(8,128)(2,1)S(1)}, bf16[2,96,896]{2,1,0:T(8,128)(2,1)S(1)}, u32[]{:S(2)}, u32[]{:S(2)}) %collective-permute-start.8) | collective-permute-done | bytes 344096 | tf_op jit(solution)/shard_map/ppermute | solution.py:40
  69.6 6.7 %collective-permute-start.17 = (bf16[96,768]{1,0:T(8,128)(2,1)S(1)}, bf16[96,768]{1,0:T(8,128)(2,1)S(1)}, u32[]{:S(2)}, u32[]{:S(2)}) collective-permute-start(bf16[96,768]{1,0:T(8,128)(2,1)S(1)} %constant_dynamic-slice_fusion.3), channel_id=1, source_target_pairs={{0,3},{1,0},{2,1},{3,2},{4,7},{5,4},{6,5},{7,6},{8,11},{9,8},{10,9... | collective-permute-start | bytes 442376 | tf_op jit(solution)/shard_map/ppermute | solution.py:36
  77.0 13.1 %project.2 = (bf16[2,512,192]{2,1,0:T(8,128)(2,1)}, bf16[2,512,192]{2,1,0:T(8,128)(2,1)}, bf16[2,512,192]{2,1,0:T(8,128)(2,1)}, bf16[2,512,768]{2,1,0:T(8,128)(2...) custom-call(s32[2]{0:T(128)} %pad_add_fusion.where, ...), custom_call_target="tpu_custom_call" | custom-call | flops 3300000000 | bytes 8800000 | tf_op jit(solution)/shard_map/project/pallas_call | solution.py:439
  90.6 1.7 collective-permute-start.19
  93.1 2.3 collective-permute-start.21
  96.5 13.0 %project.3 = (bf16[2,512,192]{2,1,0:T(8,128)(2,1)}, bf16[2,512,192]{2,1,0:T(8,128)(2,1)}, bf16[2,512,192]{2,1,0:T(8,128)(2,1)}, bf16[2,512,768]{2,1,0:T(8,128)(2...) custom-call(s32[2]{0:T(128)} %pad_add_fusion.where, ...), custom_call_target="tpu_custom_call" | custom-call | flops 3300000000 | bytes 8800000 | tf_op jit(solution)/shard_map/project/pallas_call | solution.py:439
  109.5 2.6 collective-permute-done.21
  115.8 1.6 collective-permute-start.24
  118.6 3.5 collective-permute-start.26
  122.0 1.7 add_convert_fusion.11.refs_9_.refs_13_
  123.8 6.4 %attend.2 = (bf16[2,512,192]{2,1,0:T(8,128)(2,1)}, f32[2,512,192]{2,1,0:T(8,128)}, f32[2,8,768]{2,1,0:T(8,128)}, f32[512,768]{1,0:T(8,128)}) custom-call(s32[2]{0:T(128)} %pad_add_fusion.where, bf16[4,96,896]{2,1,0:T(8,128)(2,1)} %copy-done.2, bf16[4,96,896]{2,1,0:T(8,128)(2,1)} %copy-done.3, bf16[4,96,896]{2,1,0:T(8,128)(2,1)} %copy-done.4, ...), custom_call_target="tpu_custom_call" | custom-call | flops 1800000000 | bytes 4800000 | tf_op jit(solution)/shard_map/attend/pallas_call | solution.py:528
  131.2 3.9 %collective-permute-done.26 = bf16[224,768]{1,0:T(8,128)(2,1)S(1)} collective-permute-done((bf16[224,768]{1,0:T(8,128)(2,1)S(1)}, bf16[224,768]{1,0:T(8,128)(2,1)S(1)}, u32[]{:S(2)}, u32[]{:S(2)}) %collective-permute-start.26) | collective-permute-done | bytes 344096 | tf_op jit(solution)/shard_map/ppermute | solution.py:36
  137.3 1.7 collective-permute-start.29
  145.6 1.7 add_convert_fusion.10.refs_9_.refs_13_
  147.3 8.5 %attend.3 = (bf16[2,512,192]{2,1,0:T(8,128)(2,1)}, f32[2,512,192]{2,1,0:T(8,128)}, f32[2,8,768]{2,1,0:T(8,128)}, f32[512,768]{1,0:T(8,128)}, f32[512,1]{1,0:T(8,128)}, /*index=5*/f32[8,768]{1,0:T(8,128)}) custom-call(s32[2]{0:T(128)} %pad_add_fusion.where, bf16[4,96,896]{2,1,0:T(8,128)(2,1)} %copy-done.2, bf16[4,96,896]{2,1,0:T(8,128)(2,1)} %copy-done.3, ...), custom_call_target="tpu_custom_call" | custom-call | flops 1800000000 | bytes 4800000 | tf_op jit(solution)/shard_map/attend/pallas_call | solution.py:528
  159.1 1.6 collective-permute-start.34
  160.8 1.4 pad_maximum_fusion.16.refs_10_
  162.2 9.7 %widen.1 = (bf16[4,512,768]{2,1,0:T(8,128)(2,1)}, bf16[4,512,768]{2,1,0:T(8,128)(2,1)}) custom-call(s32[2]{0:T(128)} %pad_add_fusion.where, bf16[4,96,768]{2,1,0:T(8,128)(2,1)} %copy-done.10, bf16[4,96,768]{2,1,0:T(8,128)(2,1)} %copy-done.15, bf16[4,96,768]{2,1,0:T(8,128)(2,1)} %copy-done.16, bf16[4,96,768]{2,1,0:T(8,128)(2,1)} %copy-done.17, ...), custom_call_target="tpu_custom_call" | custom-call | flops 3000000000 | bytes 8000000 | tf_op jit(solution)/shard_map/widen/pallas_call | solution.py:563
  172.2 2.0 collective-permute-done.38.refs_7_
  175.0 16.4 %narrow.1 = (bf16[512,768]{1,0:T(8,128)(2,1)}, f32[512,768]{1,0:T(8,128)}, bf16[512,768]{1,0:T(8,128)(2,1)}, bf16[4,512,768]{2,1,0:T(8,128)(2,1)}, f32[8,768]{1,0:T(8,128)}) custom-call(s32[2]{0:T(128)} %pad_add_fusion.where, bf16[4,96,768]{2,1,0:T(8,128)(2,1)} %pad_maximum_fusion.5.refs_0_, bf16[4,96,768]{2,1,0:T(8,128)(2,1)} %collective-permute-done.28.refs_1_, ...), custom_call_target="tpu_custom_call" | custom-call | flops 3900000000 | bytes 10400000 | tf_op jit(solution)/shard_map/narrow/pallas_call | solution.py:633
  192.4 2.3 collective-permute-start.39
  194.7 10.9 %ffn_grad.1 = (bf16[4,4,96,1536]{3,2,1,0:T(8,128)(2,1)}, bf16[4,4,96,1536]{3,2,1,0:T(8,128)(2,1)}, f32[4,8,768]{2,1,0:T(8,128)}) custom-call(s32[2]{0:T(128)} %pad_add_fusion.where, f32[512,768]{1,0:T(8,128)} %get-tuple-element.323.refs_8_.normal, f32[8,768]{1,0:T(8,128)} %get-tuple-element.325.refs_9_.vec.refs_10_, ...), custom_call_target="tpu_custom_call" | custom-call | flops 2700000000 | bytes 7200000 | tf_op jit(solution)/shard_map/ffn_grad/pallas_call | solution.py:680
  207.0 2.3 collective-permute-start.41
  209.4 10.5 %widen_back.1 = (f32[512,768]{1,0:T(8,128)}, f32[8,768]{1,0:T(8,128)}) custom-call(s32[2]{0:T(128)} %pad_add_fusion.where, bf16[4,96,768]{2,1,0:T(8,128)(2,1)} %copy-done.10, bf16[4,96,768]{2,1,0:T(8,128)(2,1)} %copy-done.15, bf16[4,96,768]{2,1,0:T(8,128)(2,1)} %copy-done.16, bf16[4,96,768]{2,1,0:T(8,128)(2,1)} %copy-done.17, ...), custom_call_target="tpu_custom_call" | custom-call | flops 3000000000 | bytes 8000000 | tf_op jit(solution)/shard_map/widen_back/pallas_call | solution.py:726
  219.9 4.2 %add_convert_fusion = (bf16[2,2,96,1536]{3,2,1,0:T(8,128)(2,1)S(1)}, bf16[2,2,96,1536]{3,2,1,0:T(8,128)(2,1)}) fusion(bf16[4,4,96,1536]{3,2,1,0:T(8,128)(2,1)} %collective-permute-done.40, bf16[4,4,96,1536]{3,2,1,0:T(8,128)(2,1)} %get-tuple-element.399), kind=kLoop, calls=%fused_computation | loop fusion | flops 4718592 | bytes 7077888 | tf_op jit(solution)/shard_map/convert_element_type | solution.py:92
  224.5 1.8 collective-permute-start.45
  226.2 9.2 %attend_back.2 = (bf16[2,512,192]{2,1,0:T(8,128)(2,1)}, bf16[2,72,768]{2,1,0:T(8,128)(2,1)}) custom-call(s32[2]{0:T(128)} %pad_add_fusion.where, bf16[4,96,896]{2,1,0:T(8,128)(2,1)} %copy-done.2, bf16[4,96,896]{2,1,0:T(8,128)(2,1)} %copy-done.3, bf16[4,96,896]{2,1,0:T(8,128)(2,1)} %copy-done.4, bf16[4,96,896]{2,1,0:T(8,128)(2,1)} %copy-done.5, ...), custom_call_target="tpu_custom_call" | custom-call | flops 2100000000 | bytes 5600000 | tf_op jit(solution)/shard_map/attend_back/pallas_call | solution.py:797
  235.5 9.2 %attend_back.3 = (bf16[2,512,192]{2,1,0:T(8,128)(2,1)}, bf16[2,72,768]{2,1,0:T(8,128)(2,1)}) custom-call(s32[2]{0:T(128)} %pad_add_fusion.where, bf16[4,96,896]{2,1,0:T(8,128)(2,1)} %copy-done.2, bf16[4,96,896]{2,1,0:T(8,128)(2,1)} %copy-done.3, bf16[4,96,896]{2,1,0:T(8,128)(2,1)} %copy-done.4, bf16[4,96,896]{2,1,0:T(8,128)(2,1)} %copy-done.5, ...), custom_call_target="tpu_custom_call" | custom-call | flops 2100000000 | bytes 5600000 | tf_op jit(solution)/shard_map/attend_back/pallas_call | solution.py:797
  244.8 7.6 %collective-permute-done.44 = bf16[2,2,96,1536]{3,2,1,0:T(8,128)(2,1)S(1)} collective-permute-done((bf16[2,2,96,1536]{3,2,1,0:T(8,128)(2,1)}, bf16[2,2,96,1536]{3,2,1,0:T(8,128)(2,1)S(1)}, u32[]{:S(2)}, u32[]{:S(2)}) %collective-permute-start.44) | collective-permute-done | bytes 1179680 | tf_op jit(solution)/shard_map/ppermute | solution.py:40
  252.4 3.1 fusion.5
  255.5 1.5 collective-permute-start.46
  257.1 1.5 collective-permute-start.47
  259.4 11.5 %project_back.2 = (bf16[4,2,96,896]{3,2,1,0:T(8,128)(2,1)}, bf16[4,2,96,896]{3,2,1,0:T(8,128)(2,1)}, f32[512,768]{1,0:T(8,128)}) custom-call(s32[2]{0:T(128)} %pad_add_fusion.where, bf16[4,96,896]{2,1,0:T(8,128)(2,1)} %copy-done.2, bf16[4,96,896]{2,1,0:T(8,128)(2,1)} %copy-done.3, bf16[4,96,896]{2,1,0:T(8,128)(2,1)} %copy-done.4, ...), custom_call_target="tpu_custom_call" | custom-call | flops 3300000000 | bytes 8800000 | tf_op jit(solution)/shard_map/project_back/pallas_call | solution.py:900
  271.5 2.2 fusion.1
  273.8 3.8 %collective-permute-start.50 = (bf16[96,1536]{1,0:T(8,128)(2,1)S(1)}, bf16[96,1536]{1,0:T(8,128)(2,1)S(1)}, u32[]{:S(2)}, u32[]{:S(2)}) collective-permute-start(bf16[96,1536]{1,0:T(8,128)(2,1)S(1)} %slice_bitcast_fusion.1), channel_id=1, source_target_pairs={{0,3},{1,0},{2,1},{3,2},{4,7},{5,4},{6,5},{7,6},{8,11},{9,8},{10,9... | collective-permute-start | bytes 884744 | tf_op jit(solution)/shard_map/ppermute | solution.py:36
  277.7 1.7 multiply_convert_fusion.refs_14_
  279.5 12.0 %project_back.3 = (bf16[4,2,96,896]{3,2,1,0:T(8,128)(2,1)}, bf16[4,2,96,896]{3,2,1,0:T(8,128)(2,1)}, bf16[512,768]{1,0:T(8,128)(2,1)}) custom-call(s32[2]{0:T(128)} %pad_add_fusion.where, bf16[4,96,896]{2,1,0:T(8,128)(2,1)} %copy-done.2, bf16[4,96,896]{2,1,0:T(8,128)(2,1)} %copy-done.3, bf16[4,96,896]{2,1,0:T(8,128)(2,1)} %copy-done.4, ...), custom_call_target="tpu_custom_call" | custom-call | flops 3300000000 | bytes 8800000 | tf_op jit(solution)/shard_map/project_back/pallas_call | solution.py:900
  291.6 4.8 %collective-permute-done.51 = bf16[96,1536]{1,0:T(8,128)(2,1)S(1)} collective-permute-done((bf16[96,1536]{1,0:T(8,128)(2,1)S(1)}, bf16[96,1536]{1,0:T(8,128)(2,1)S(1)}, u32[]{:S(2)}, u32[]{:S(2)}) %collective-permute-start.51) | collective-permute-done | bytes 294944 | tf_op jit(solution)/shard_map/ppermute | solution.py:36
  296.4 2.2 add_convert_fusion.2
  298.6 1.4 collective-permute-start.54
  303.2 1.6 slice.347
  304.8 3.4 collective-permute-start.55
  308.2 2.7 lay.3
  310.9 3.2 collective-permute-done.56
  314.1 2.6 collective-permute-done.54
  316.7 4.8 %collective-permute-done.55.refs_2_ = bf16[128,768]{1,0:T(8,128)(2,1)} collective-permute-done((bf16[128,768]{1,0:T(8,128)(2,1)}, bf16[128,768]{1,0:T(8,128)(2,1)}, u32[]{:S(2)}, u32[]{:S(2)}) %collective-permute-start.55) | collective-permute-done | bytes 196640 | tf_op jit(solution)/shard_map/ppermute | solution.py:36
  322.8 1.3 collective-permute-start.57
  327.2 1.2 collective-permute-start.60
  329.7 7.3 %collective-permute-done.59.refs_1_ = bf16[128,768]{1,0:T(8,128)(2,1)S(1)} collective-permute-done((bf16[128,768]{1,0:T(8,128)(2,1)S(1)}, bf16[128,768]{1,0:T(8,128)(2,1)S(1)}, u32[]{:S(2)}, u32[]{:S(2)}) %collective-permute-start.59) | collective-permute-done | bytes 196640 | tf_op jit(solution)/shard_map/ppermute | solution.py:36
  336.9 1.4 fusion.2
  341.4 1.4 collective-permute-start.63
  344.7 2.9 lay.2
  347.6 7.6 %collective-permute-done.62 = bf16[96,896]{1,0:T(8,128)(2,1)S(1)} collective-permute-done((bf16[96,896]{1,0:T(8,128)(2,1)S(1)}, bf16[96,896]{1,0:T(8,128)(2,1)S(1)}, u32[]{:S(2)}, u32[]{:S(2)}) %collective-permute-start.62) | collective-permute-done | bytes 172064 | tf_op jit(solution)/shard_map/ppermute | solution.py:36
  355.3 1.4 collective-permute-done.65
  (310 shorter events, 63.4 us)
Async XLA Ops:
  7.6 9.9 %collective-permute-start.2 = (bf16[96,896]{1,0:T(8,128)(2,1)S(1)}, bf16[96,896]{1,0:T(8,128)(2,1)S(1)}, u32[]{:S(2)}, u32[]{:S(2)}) collective-permute-start(bf16[96,896]{1,0:T(8,128)(2,1)S(1)} %fusion.19), channel_id=1, source_target_pairs={{0,3},{1,0},{2,1},{3,2},{4,7},{5,4},{6,5},{7,6},{8,11},{9,8},{10,9... | collective-permute-start | bytes 516104 | tf_op jit(solution)/shard_map/ppermute | solution.py:36
  12.8 14.6 %collective-permute-start.1 = (bf16[96,896]{1,0:T(8,128)(2,1)S(1)}, bf16[96,896]{1,0:T(8,128)(2,1)S(1)}, u32[]{:S(2)}, u32[]{:S(2)}) collective-permute-start(bf16[96,896]{1,0:T(8,128)(2,1)S(1)} %fusion.19), channel_id=1, source_target_pairs={{0,2},{1,3},{2,0},{3,1},{4,6},{5,7},{6,4},{7,5},{8,10},{9,11},{10,... | collective-permute-start | bytes 516104 | tf_op jit(solution)/shard_map/ppermute | solution.py:36
  12.8 14.6 %collective-permute-start = (bf16[96,896]{1,0:T(8,128)(2,1)S(1)}, bf16[96,896]{1,0:T(8,128)(2,1)S(1)}, u32[]{:S(2)}, u32[]{:S(2)}) collective-permute-start(bf16[96,896]{1,0:T(8,128)(2,1)S(1)} %fusion.19), channel_id=1, source_target_pairs={{0,1},{1,2},{2,3},{3,0},{4,5},{5,6},{6,7},{7,4},{8,9},{9,10},{10,1... | collective-permute-start | bytes 516104 | tf_op jit(solution)/shard_map/ppermute | solution.py:36
  27.5 24.1 %collective-permute-start.3 = (bf16[4,96,896]{2,1,0:T(8,128)(2,1)S(1)}, bf16[4,96,896]{2,1,0:T(8,128)(2,1)S(1)}, u32[]{:S(2)}, u32[]{:S(2)}) collective-permute-start(bf16[4,96,896]{2,1,0:T(8,128)(2,1)S(1)} %pad_maximum_fusion.3.refs_0_), channel_id=1, source_target_pairs={{0,8},{8,0},{16,24},{24,16},{1,9},{9,1},{17,25},{25,17},{2,10},{10... | collective-permute-start | bytes 2064392 | tf_op jit(solution)/shard_map/ppermute | solution.py:40
  29.6 22.8 %collective-permute-start.4 = (bf16[4,96,896]{2,1,0:T(8,128)(2,1)S(1)}, bf16[4,96,896]{2,1,0:T(8,128)(2,1)S(1)}, u32[]{:S(2)}, u32[]{:S(2)}) collective-permute-start(bf16[4,96,896]{2,1,0:T(8,128)(2,1)S(1)} %pad_maximum_fusion.3.refs_0_), channel_id=1, source_target_pairs={{0,16},{8,24},{16,0},{24,8},{1,17},{9,25},{17,1},{25,9},{2,18},{10... | collective-permute-start | bytes 2064392 | tf_op jit(solution)/shard_map/ppermute | solution.py:40
  32.0 10.9 %collective-permute-start.5 = (bf16[160,768]{1,0:T(8,128)(2,1)}, bf16[160,768]{1,0:T(8,128)(2,1)S(1)}, u32[]{:S(2)}, u32[]{:S(2)}) collective-permute-start(bf16[160,768]{1,0:T(8,128)(2,1)} %get-tuple-element.512), channel_id=1, source_target_pairs={{0,1},{1,2},{2,3},{3,0},{4,5},{5,6},{6,7},{7,4},{8,9},{9,10},{10,1... | collective-permute-start | bytes 737288 | tf_op jit(solution)/shard_map/ppermute | solution.py:36
  32.9 18.7 %collective-permute-start.6 = (bf16[160,768]{1,0:T(8,128)(2,1)}, bf16[160,768]{1,0:T(8,128)(2,1)S(1)}, u32[]{:S(2)}, u32[]{:S(2)}) collective-permute-start(bf16[160,768]{1,0:T(8,128)(2,1)} %get-tuple-element.511), channel_id=1, source_target_pairs={{0,2},{1,3},{2,0},{3,1},{4,6},{5,7},{6,4},{7,5},{8,10},{9,11},{10,... | collective-permute-start | bytes 737288 | tf_op jit(solution)/shard_map/ppermute | solution.py:36
  34.8 16.8 %collective-permute-start.7 = (bf16[160,768]{1,0:T(8,128)(2,1)S(1)}, bf16[160,768]{1,0:T(8,128)(2,1)S(1)}, u32[]{:S(2)}, u32[]{:S(2)}) collective-permute-start(bf16[160,768]{1,0:T(8,128)(2,1)S(1)} %get-tuple-element.510), channel_id=1, source_target_pairs={{0,3},{1,0},{2,1},{3,2},{4,7},{5,4},{6,5},{7,6},{8,11},{9,8},{10,9... | collective-permute-start | bytes 737288 | tf_op jit(solution)/shard_map/ppermute | solution.py:36
  52.4 12.4 %collective-permute-start.10 = (bf16[4,96,896]{2,1,0:T(8,128)(2,1)S(1)}, bf16[4,96,896]{2,1,0:T(8,128)(2,1)S(1)}, u32[]{:S(2)}, u32[]{:S(2)}) collective-permute-start(bf16[4,96,896]{2,1,0:T(8,128)(2,1)S(1)} %pad_maximum_fusion.3.refs_0_), channel_id=1, source_target_pairs={{0,4},{4,0},{1,5},{5,1},{2,6},{6,2},{3,7},{7,3},{8,12},{12,8},{9,1... | collective-permute-start | bytes 2064392 | tf_op jit(solution)/shard_map/ppermute | solution.py:44
  52.5 12.3 %collective-permute-start.11 = (bf16[4,96,896]{2,1,0:T(8,128)(2,1)S(1)}, bf16[4,96,896]{2,1,0:T(8,128)(2,1)S(1)}, u32[]{:S(2)}, u32[]{:S(2)}) collective-permute-start(bf16[4,96,896]{2,1,0:T(8,128)(2,1)S(1)} %collective-permute-done.3.refs_1_), channel_id=1, source_target_pairs={{0,4},{4,0},{1,5},{5,1},{2,6},{6,2},{3,7},{7,3},{8,12},{12,8},{9,1... | collective-permute-start | bytes 2064392 | tf_op jit(solution)/shard_map/ppermute | solution.py:44
  53.0 11.8 %collective-permute-start.12 = (bf16[4,96,896]{2,1,0:T(8,128)(2,1)S(1)}, bf16[4,96,896]{2,1,0:T(8,128)(2,1)S(1)}, u32[]{:S(2)}, u32[]{:S(2)}) collective-permute-start(bf16[4,96,896]{2,1,0:T(8,128)(2,1)S(1)} %collective-permute-done.4.refs_2_), channel_id=1, source_target_pairs={{0,4},{4,0},{1,5},{5,1},{2,6},{6,2},{3,7},{7,3},{8,12},{12,8},{9,1... | collective-permute-start | bytes 2064392 | tf_op jit(solution)/shard_map/ppermute | solution.py:44
  54.1 10.5 %collective-permute-start.8 = (bf16[2,96,896]{2,1,0:T(8,128)(2,1)S(1)}, bf16[2,96,896]{2,1,0:T(8,128)(2,1)S(1)}, u32[]{:S(2)}, u32[]{:S(2)}) collective-permute-start(bf16[2,96,896]{2,1,0:T(8,128)(2,1)S(1)} %slice.296), channel_id=1, source_target_pairs={{0,16},{8,24},{16,0},{24,8},{1,17},{9,25},{17,1},{25,9},{2,18},{10... | collective-permute-start | bytes 1032200 | tf_op jit(solution)/shard_map/ppermute | solution.py:40
  54.7 10.1 %collective-permute-start.9 = (bf16[2,96,896]{2,1,0:T(8,128)(2,1)S(1)}, bf16[2,96,896]{2,1,0:T(8,128)(2,1)S(1)}, u32[]{:S(2)}, u32[]{:S(2)}) collective-permute-start(bf16[2,96,896]{2,1,0:T(8,128)(2,1)S(1)} %slice.297), channel_id=1, source_target_pairs={{0,8},{8,0},{16,24},{24,16},{1,9},{9,1},{17,25},{25,17},{2,10},{10... | collective-permute-start | bytes 1032200 | tf_op jit(solution)/shard_map/ppermute | solution.py:40
  65.9 3.7 %collective-permute-start.14 = (bf16[4,96,896]{2,1,0:T(8,128)(2,1)S(1)}, bf16[4,96,896]{2,1,0:T(8,128)(2,1)S(1)}, u32[]{:S(2)}, u32[]{:S(2)}) collective-permute-start(bf16[4,96,896]{2,1,0:T(8,128)(2,1)S(1)} %constant_dynamic-update-slice_fusion.refs_3_), channel_id=1, source_target_pairs={{0,4},{4,0},{1,5},{5,1},{2,6},{6,2},{3,7},{7,3},{8,12},{12,8},{9,1... | collective-permute-start | bytes 2064392 | tf_op jit(solution)/shard_map/ppermute | solution.py:44
  65.9 2.9 collective-permute-start.13
  69.6 20.4 %collective-permute-start.17 = (bf16[96,768]{1,0:T(8,128)(2,1)S(1)}, bf16[96,768]{1,0:T(8,128)(2,1)S(1)}, u32[]{:S(2)}, u32[]{:S(2)}) collective-permute-start(bf16[96,768]{1,0:T(8,128)(2,1)S(1)} %constant_dynamic-slice_fusion.3), channel_id=1, source_target_pairs={{0,3},{1,0},{2,1},{3,2},{4,7},{5,4},{6,5},{7,6},{8,11},{9,8},{10,9... | collective-permute-start | bytes 442376 | tf_op jit(solution)/shard_map/ppermute | solution.py:36
  76.4 13.7 %collective-permute-start.16 = (bf16[96,768]{1,0:T(8,128)(2,1)S(1)}, bf16[96,768]{1,0:T(8,128)(2,1)S(1)}, u32[]{:S(2)}, u32[]{:S(2)}) collective-permute-start(bf16[96,768]{1,0:T(8,128)(2,1)S(1)} %constant_dynamic-slice_fusion.3), channel_id=1, source_target_pairs={{0,2},{1,3},{2,0},{3,1},{4,6},{5,7},{6,4},{7,5},{8,10},{9,11},{10,... | collective-permute-start | bytes 442376 | tf_op jit(solution)/shard_map/ppermute | solution.py:36
  76.4 13.7 %collective-permute-start.15 = (bf16[96,768]{1,0:T(8,128)(2,1)S(1)}, bf16[96,768]{1,0:T(8,128)(2,1)S(1)}, u32[]{:S(2)}, u32[]{:S(2)}) collective-permute-start(bf16[96,768]{1,0:T(8,128)(2,1)S(1)} %constant_dynamic-slice_fusion.3), channel_id=1, source_target_pairs={{0,1},{1,2},{2,3},{3,0},{4,5},{5,6},{6,7},{7,4},{8,9},{9,10},{10,1... | collective-permute-start | bytes 442376 | tf_op jit(solution)/shard_map/ppermute | solution.py:36
  90.2 22.0 %collective-permute-start.18 = (bf16[4,96,768]{2,1,0:T(8,128)(2,1)S(1)}, bf16[4,96,768]{2,1,0:T(8,128)(2,1)S(1)}, u32[]{:S(2)}, u32[]{:S(2)}) collective-permute-start(bf16[4,96,768]{2,1,0:T(8,128)(2,1)S(1)} %pad_maximum_fusion.4.refs_0_), channel_id=1, source_target_pairs={{0,8},{8,0},{16,24},{24,16},{1,9},{9,1},{17,25},{25,17},{2,10},{10... | collective-permute-start | bytes 1769480 | tf_op jit(solution)/shard_map/ppermute | solution.py:40
  90.6 21.5 %collective-permute-start.19 = (bf16[4,96,768]{2,1,0:T(8,128)(2,1)S(1)}, bf16[4,96,768]{2,1,0:T(8,128)(2,1)S(1)}, u32[]{:S(2)}, u32[]{:S(2)}) collective-permute-start(bf16[4,96,768]{2,1,0:T(8,128)(2,1)S(1)} %pad_maximum_fusion.4.refs_0_), channel_id=1, source_target_pairs={{0,16},{8,24},{16,0},{24,8},{1,17},{9,25},{17,1},{25,9},{2,18},{10... | collective-permute-start | bytes 1769480 | tf_op jit(solution)/shard_map/ppermute | solution.py:40
  92.3 19.9 %collective-permute-start.20 = (bf16[4,96,768]{2,1,0:T(8,128)(2,1)S(1)}, bf16[4,96,768]{2,1,0:T(8,128)(2,1)S(1)}, u32[]{:S(2)}, u32[]{:S(2)}) collective-permute-start(bf16[4,96,768]{2,1,0:T(8,128)(2,1)S(1)} %pad_maximum_fusion.4.refs_0_), channel_id=1, source_target_pairs={{0,4},{4,0},{1,5},{5,1},{2,6},{6,2},{3,7},{7,3},{8,12},{12,8},{9,1... | collective-permute-start | bytes 1769480 | tf_op jit(solution)/shard_map/ppermute | solution.py:44
  93.1 19.1 %collective-permute-start.21 = (bf16[224,768]{1,0:T(8,128)(2,1)}, bf16[224,768]{1,0:T(8,128)(2,1)}, u32[]{:S(2)}, u32[]{:S(2)}) collective-permute-start(bf16[224,768]{1,0:T(8,128)(2,1)} %pad_maximum_fusion.12), channel_id=1, source_target_pairs={{0,2},{1,3},{2,0},{3,1},{4,6},{5,7},{6,4},{7,5},{8,10},{9,11},{10,... | collective-permute-start | bytes 1032200 | tf_op jit(solution)/shard_map/ppermute | solution.py:36
  96.3 13.3 %collective-permute-start.22 = (bf16[2,72,768]{2,1,0:T(8,128)(2,1)}, bf16[2,72,768]{2,1,0:T(8,128)(2,1)S(1)}, u32[]{:S(2)}, u32[]{:S(2)}) collective-permute-start(bf16[2,72,768]{2,1,0:T(8,128)(2,1)} %get-tuple-element.285), channel_id=1, source_target_pairs={{0,4},{4,0},{1,5},{5,1},{2,6},{6,2},{3,7},{7,3},{8,12},{12,8},{9,1... | collective-permute-start | bytes 663560 | tf_op jit(solution)/shard_map/ppermute | solution.py:44
  114.7 15.6 %collective-permute-start.23 = (bf16[2,96,768]{2,1,0:T(8,128)(2,1)}, bf16[2,96,768]{2,1,0:T(8,128)(2,1)}, u32[]{:S(2)}, u32[]{:S(2)}) collective-permute-start(bf16[2,96,768]{2,1,0:T(8,128)(2,1)} %slice.308), channel_id=1, source_target_pairs={{0,16},{8,24},{16,0},{24,8},{1,17},{9,25},{17,1},{25,9},{2,18},{10... | collective-permute-start | bytes 884744 | tf_op jit(solution)/shard_map/ppermute | solution.py:40
  115.8 14.5 %collective-permute-start.24 = (bf16[2,96,768]{2,1,0:T(8,128)(2,1)}, bf16[2,96,768]{2,1,0:T(8,128)(2,1)}, u32[]{:S(2)}, u32[]{:S(2)}) collective-permute-start(bf16[2,96,768]{2,1,0:T(8,128)(2,1)} %slice.309), channel_id=1, source_target_pairs={{0,8},{8,0},{16,24},{24,16},{1,9},{9,1},{17,25},{25,17},{2,10},{10... | collective-permute-start | bytes 884744 | tf_op jit(solution)/shard_map/ppermute | solution.py:40
  118.2 13.0 %collective-permute-start.25 = (bf16[224,768]{1,0:T(8,128)(2,1)}, bf16[224,768]{1,0:T(8,128)(2,1)S(1)}, u32[]{:S(2)}, u32[]{:S(2)}) collective-permute-start(bf16[224,768]{1,0:T(8,128)(2,1)} %get-tuple-element.509), channel_id=1, source_target_pairs={{0,1},{1,2},{2,3},{3,0},{4,5},{5,6},{6,7},{7,4},{8,9},{9,10},{10,1... | collective-permute-start | bytes 1032200 | tf_op jit(solution)/shard_map/ppermute | solution.py:36
  118.6 16.5 %collective-permute-start.26 = (bf16[224,768]{1,0:T(8,128)(2,1)S(1)}, bf16[224,768]{1,0:T(8,128)(2,1)S(1)}, u32[]{:S(2)}, u32[]{:S(2)}) collective-permute-start(bf16[224,768]{1,0:T(8,128)(2,1)S(1)} %get-tuple-element.508), channel_id=1, source_target_pairs={{0,3},{1,0},{2,1},{3,2},{4,7},{5,4},{6,5},{7,6},{8,11},{9,8},{10,9... | collective-permute-start | bytes 1032200 | tf_op jit(solution)/shard_map/ppermute | solution.py:36
  122.0 8.2 %collective-permute-start.27 = (bf16[2,72,768]{2,1,0:T(8,128)(2,1)}, bf16[2,72,768]{2,1,0:T(8,128)(2,1)S(1)}, u32[]{:S(2)}, u32[]{:S(2)}) collective-permute-start(bf16[2,72,768]{2,1,0:T(8,128)(2,1)} %get-tuple-element.298), channel_id=1, source_target_pairs={{0,4},{4,0},{1,5},{5,1},{2,6},{6,2},{3,7},{7,3},{8,12},{12,8},{9,1... | collective-permute-start | bytes 663560 | tf_op jit(solution)/shard_map/ppermute | solution.py:44
  136.9 18.9 %collective-permute-start.28 = (bf16[4,96,768]{2,1,0:T(8,128)(2,1)}, bf16[4,96,768]{2,1,0:T(8,128)(2,1)}, u32[]{:S(2)}, u32[]{:S(2)}) collective-permute-start(bf16[4,96,768]{2,1,0:T(8,128)(2,1)} %pad_maximum_fusion.5.refs_0_), channel_id=1, source_target_pairs={{0,8},{8,0},{16,24},{24,16},{1,9},{9,1},{17,25},{25,17},{2,10},{10... | collective-permute-start | bytes 1769480 | tf_op jit(solution)/shard_map/ppermute | solution.py:40
  137.3 18.5 %collective-permute-start.29 = (bf16[4,96,768]{2,1,0:T(8,128)(2,1)}, bf16[4,96,768]{2,1,0:T(8,128)(2,1)}, u32[]{:S(2)}, u32[]{:S(2)}) collective-permute-start(bf16[4,96,768]{2,1,0:T(8,128)(2,1)} %pad_maximum_fusion.5.refs_0_), channel_id=1, source_target_pairs={{0,16},{8,24},{16,0},{24,8},{1,17},{9,25},{17,1},{25,9},{2,18},{10... | collective-permute-start | bytes 1769480 | tf_op jit(solution)/shard_map/ppermute | solution.py:40
  141.8 14.1 %collective-permute-start.30 = (bf16[4,96,768]{2,1,0:T(8,128)(2,1)S(1)}, bf16[4,96,768]{2,1,0:T(8,128)(2,1)S(1)}, u32[]{:S(2)}, u32[]{:S(2)}) collective-permute-start(bf16[4,96,768]{2,1,0:T(8,128)(2,1)S(1)} %collective-permute-done.18.refs_1_), channel_id=1, source_target_pairs={{0,4},{4,0},{1,5},{5,1},{2,6},{6,2},{3,7},{7,3},{8,12},{12,8},{9,1... | collective-permute-start | bytes 1769480 | tf_op jit(solution)/shard_map/ppermute | solution.py:44
  141.9 14.0 %collective-permute-start.31 = (bf16[4,96,768]{2,1,0:T(8,128)(2,1)S(1)}, bf16[4,96,768]{2,1,0:T(8,128)(2,1)}, u32[]{:S(2)}, u32[]{:S(2)}) collective-permute-start(bf16[4,96,768]{2,1,0:T(8,128)(2,1)S(1)} %collective-permute-done.19.refs_2_), channel_id=1, source_target_pairs={{0,4},{4,0},{1,5},{5,1},{2,6},{6,2},{3,7},{7,3},{8,12},{12,8},{9,1... | collective-permute-start | bytes 1769480 | tf_op jit(solution)/shard_map/ppermute | solution.py:44
  143.4 12.5 %collective-permute-start.32 = (bf16[4,96,768]{2,1,0:T(8,128)(2,1)S(1)}, bf16[4,96,768]{2,1,0:T(8,128)(2,1)}, u32[]{:S(2)}, u32[]{:S(2)}) collective-permute-start(bf16[4,96,768]{2,1,0:T(8,128)(2,1)S(1)} %constant_dynamic-update-slice_fusion.2.refs_3_), channel_id=1, source_target_pairs={{0,4},{4,0},{1,5},{5,1},{2,6},{6,2},{3,7},{7,3},{8,12},{12,8},{9,1... | collective-permute-start | bytes 1769480 | tf_op jit(solution)/shard_map/ppermute | solution.py:44
  155.9 16.1 %collective-permute-start.35 = (bf16[4,96,768]{2,1,0:T(8,128)(2,1)}, bf16[4,96,768]{2,1,0:T(8,128)(2,1)S(1)}, u32[]{:S(2)}, u32[]{:S(2)}) collective-permute-start(bf16[4,96,768]{2,1,0:T(8,128)(2,1)} %pad_maximum_fusion.5.refs_0_), channel_id=1, source_target_pairs={{0,4},{4,0},{1,5},{5,1},{2,6},{6,2},{3,7},{7,3},{8,12},{12,8},{9,1... | collective-permute-start | bytes 1769480 | tf_op jit(solution)/shard_map/ppermute | solution.py:44
  156.3 15.7 %collective-permute-start.36 = (bf16[4,96,768]{2,1,0:T(8,128)(2,1)}, bf16[4,96,768]{2,1,0:T(8,128)(2,1)S(1)}, u32[]{:S(2)}, u32[]{:S(2)}) collective-permute-start(bf16[4,96,768]{2,1,0:T(8,128)(2,1)} %collective-permute-done.28.refs_1_), channel_id=1, source_target_pairs={{0,4},{4,0},{1,5},{5,1},{2,6},{6,2},{3,7},{7,3},{8,12},{12,8},{9,1... | collective-permute-start | bytes 1769480 | tf_op jit(solution)/shard_map/ppermute | solution.py:44
  156.5 15.6 %collective-permute-start.37 = (bf16[4,96,768]{2,1,0:T(8,128)(2,1)}, bf16[4,96,768]{2,1,0:T(8,128)(2,1)S(1)}, u32[]{:S(2)}, u32[]{:S(2)}) collective-permute-start(bf16[4,96,768]{2,1,0:T(8,128)(2,1)} %collective-permute-done.29.refs_2_), channel_id=1, source_target_pairs={{0,4},{4,0},{1,5},{5,1},{2,6},{6,2},{3,7},{7,3},{8,12},{12,8},{9,1... | collective-permute-start | bytes 1769480 | tf_op jit(solution)/shard_map/ppermute | solution.py:44
  158.8 13.1 %collective-permute-start.33 = (bf16[2,96,768]{2,1,0:T(8,128)(2,1)S(1)}, bf16[2,96,768]{2,1,0:T(8,128)(2,1)S(1)}, u32[]{:S(2)}, u32[]{:S(2)}) collective-permute-start(bf16[2,96,768]{2,1,0:T(8,128)(2,1)S(1)} %slice.320), channel_id=1, source_target_pairs={{0,16},{8,24},{16,0},{24,8},{1,17},{9,25},{17,1},{25,9},{2,18},{10... | collective-permute-start | bytes 884744 | tf_op jit(solution)/shard_map/ppermute | solution.py:40
  159.1 12.8 %collective-permute-start.34 = (bf16[2,96,768]{2,1,0:T(8,128)(2,1)S(1)}, bf16[2,96,768]{2,1,0:T(8,128)(2,1)S(1)}, u32[]{:S(2)}, u32[]{:S(2)}) collective-permute-start(bf16[2,96,768]{2,1,0:T(8,128)(2,1)S(1)} %slice.321), channel_id=1, source_target_pairs={{0,8},{8,0},{16,24},{24,16},{1,9},{9,1},{17,25},{25,17},{2,10},{10... | collective-permute-start | bytes 884744 | tf_op jit(solution)/shard_map/ppermute | solution.py:40
  192.4 13.2 %collective-permute-start.39 = (bf16[128,768]{1,0:T(8,128)(2,1)S(1)}, bf16[128,768]{1,0:T(8,128)(2,1)S(1)}, u32[]{:S(2)}, u32[]{:S(2)}) collective-permute-start(bf16[128,768]{1,0:T(8,128)(2,1)S(1)} %slice.322), channel_id=1, source_target_pairs={{0,2},{1,3},{2,0},{3,1},{4,6},{5,7},{6,4},{7,5},{8,10},{9,11},{10,... | collective-permute-start | bytes 589832 | tf_op jit(solution)/shard_map/ppermute | solution.py:36
  206.3 13.6 %collective-permute-start.40 = (bf16[4,4,96,1536]{3,2,1,0:T(8,128)(2,1)}, bf16[4,4,96,1536]{3,2,1,0:T(8,128)(2,1)}, u32[]{:S(2)}, u32[]{:S(2)}) collective-permute-start(bf16[4,4,96,1536]{3,2,1,0:T(8,128)(2,1)} %get-tuple-element.350), channel_id=1, source_target_pairs={{0,4},{4,0},{1,5},{5,1},{2,6},{6,2},{3,7},{7,3},{8,12},{12,8},{9,1... | collective-permute-start | bytes 14155784 | tf_op jit(solution)/shard_map/ppermute | solution.py:44
  207.0 12.8 %collective-permute-start.41 = (bf16[128,768]{1,0:T(8,128)(2,1)S(1)}, bf16[128,768]{1,0:T(8,128)(2,1)S(1)}, u32[]{:S(2)}, u32[]{:S(2)}) collective-permute-start(bf16[128,768]{1,0:T(8,128)(2,1)S(1)} %get-tuple-element.488), channel_id=1, source_target_pairs={{0,3},{1,0},{2,1},{3,2},{4,7},{5,4},{6,5},{7,6},{8,11},{9,8},{10,9... | collective-permute-start | bytes 589832 | tf_op jit(solution)/shard_map/ppermute | solution.py:36
  209.4 10.5 %collective-permute-start.42 = (bf16[128,768]{1,0:T(8,128)(2,1)S(1)}, bf16[128,768]{1,0:T(8,128)(2,1)S(1)}, u32[]{:S(2)}, u32[]{:S(2)}) collective-permute-start(bf16[128,768]{1,0:T(8,128)(2,1)S(1)} %get-tuple-element.487), channel_id=1, source_target_pairs={{0,1},{1,2},{2,3},{3,0},{4,5},{5,6},{6,7},{7,4},{8,9},{9,10},{10,1... | collective-permute-start | bytes 589832 | tf_op jit(solution)/shard_map/ppermute | solution.py:36
  224.1 28.3 %collective-permute-start.44 = (bf16[2,2,96,1536]{3,2,1,0:T(8,128)(2,1)}, bf16[2,2,96,1536]{3,2,1,0:T(8,128)(2,1)S(1)}, u32[]{:S(2)}, u32[]{:S(2)}) collective-permute-start(bf16[2,2,96,1536]{3,2,1,0:T(8,128)(2,1)} %get-tuple-element.485), channel_id=1, source_target_pairs={{0,8},{8,0},{16,24},{24,16},{1,9},{9,1},{17,25},{25,17},{2,10},{10... | collective-permute-start | bytes 3538952 | tf_op jit(solution)/shard_map/ppermute | solution.py:40
  224.5 27.9 %collective-permute-start.45 = (bf16[2,2,96,1536]{3,2,1,0:T(8,128)(2,1)S(1)}, bf16[2,2,96,1536]{3,2,1,0:T(8,128)(2,1)S(1)}, u32[]{:S(2)}, u32[]{:S(2)}) collective-permute-start(bf16[2,2,96,1536]{3,2,1,0:T(8,128)(2,1)S(1)} %get-tuple-element.484), channel_id=1, source_target_pairs={{0,16},{8,24},{16,0},{24,8},{1,17},{9,25},{17,1},{25,9},{2,18},{10... | collective-permute-start | bytes 3538952 | tf_op jit(solution)/shard_map/ppermute | solution.py:40
  235.4 9.3 %collective-permute-start.43 = (bf16[2,72,768]{2,1,0:T(8,128)(2,1)}, bf16[2,72,768]{2,1,0:T(8,128)(2,1)S(1)}, u32[]{:S(2)}, u32[]{:S(2)}) collective-permute-start(bf16[2,72,768]{2,1,0:T(8,128)(2,1)} %get-tuple-element.367), channel_id=1, source_target_pairs={{0,4},{4,0},{1,5},{5,1},{2,6},{6,2},{3,7},{7,3},{8,12},{12,8},{9,1... | collective-permute-start | bytes 663560 | tf_op jit(solution)/shard_map/ppermute | solution.py:44
  255.5 15.4 %collective-permute-start.46 = (bf16[2,96,1536]{2,1,0:T(8,128)(2,1)}, bf16[2,96,1536]{2,1,0:T(8,128)(2,1)S(1)}, u32[]{:S(2)}, u32[]{:S(2)}) collective-permute-start(bf16[2,96,1536]{2,1,0:T(8,128)(2,1)} %get-tuple-element.483), channel_id=1, source_target_pairs={{0,8},{8,0},{16,24},{24,16},{1,9},{9,1},{17,25},{25,17},{2,10},{10... | collective-permute-start | bytes 1769480 | tf_op jit(solution)/shard_map/ppermute | solution.py:40
  257.1 14.3 %collective-permute-start.47 = (bf16[2,96,1536]{2,1,0:T(8,128)(2,1)}, bf16[2,96,1536]{2,1,0:T(8,128)(2,1)S(1)}, u32[]{:S(2)}, u32[]{:S(2)}) collective-permute-start(bf16[2,96,1536]{2,1,0:T(8,128)(2,1)} %get-tuple-element.482), channel_id=1, source_target_pairs={{0,16},{8,24},{16,0},{24,8},{1,17},{9,25},{17,1},{25,9},{2,18},{10... | collective-permute-start | bytes 1769480 | tf_op jit(solution)/shard_map/ppermute | solution.py:40
  258.6 12.3 %collective-permute-start.48 = (bf16[2,72,768]{2,1,0:T(8,128)(2,1)S(1)}, bf16[2,72,768]{2,1,0:T(8,128)(2,1)S(1)}, u32[]{:S(2)}, u32[]{:S(2)}) collective-permute-start(bf16[2,72,768]{2,1,0:T(8,128)(2,1)S(1)} %copy-done.39), channel_id=1, source_target_pairs={{0,4},{4,0},{1,5},{5,1},{2,6},{6,2},{3,7},{7,3},{8,12},{12,8},{9,1... | collective-permute-start | bytes 663560 | tf_op jit(solution)/shard_map/ppermute | solution.py:44
  271.3 25.1 %collective-permute-start.49 = (bf16[4,2,96,896]{3,2,1,0:T(8,128)(2,1)}, bf16[4,2,96,896]{3,2,1,0:T(8,128)(2,1)}, u32[]{:S(2)}, u32[]{:S(2)}) collective-permute-start(bf16[4,2,96,896]{3,2,1,0:T(8,128)(2,1)} %get-tuple-element.398), channel_id=1, source_target_pairs={{0,4},{4,0},{1,5},{5,1},{2,6},{6,2},{3,7},{7,3},{8,12},{12,8},{9,1... | collective-permute-start | bytes 4128776 | tf_op jit(solution)/shard_map/ppermute | solution.py:44
  273.8 17.8 %collective-permute-start.50 = (bf16[96,1536]{1,0:T(8,128)(2,1)S(1)}, bf16[96,1536]{1,0:T(8,128)(2,1)S(1)}, u32[]{:S(2)}, u32[]{:S(2)}) collective-permute-start(bf16[96,1536]{1,0:T(8,128)(2,1)S(1)} %slice_bitcast_fusion.1), channel_id=1, source_target_pairs={{0,3},{1,0},{2,1},{3,2},{4,7},{5,4},{6,5},{7,6},{8,11},{9,8},{10,9... | collective-permute-start | bytes 884744 | tf_op jit(solution)/shard_map/ppermute | solution.py:36
  277.6 18.8 %collective-permute-start.51 = (bf16[96,1536]{1,0:T(8,128)(2,1)S(1)}, bf16[96,1536]{1,0:T(8,128)(2,1)S(1)}, u32[]{:S(2)}, u32[]{:S(2)}) collective-permute-start(bf16[96,1536]{1,0:T(8,128)(2,1)S(1)} %slice_bitcast_fusion), channel_id=1, source_target_pairs={{0,2},{1,3},{2,0},{3,1},{4,6},{5,7},{6,4},{7,5},{8,10},{9,11},{10,... | collective-permute-start | bytes 884744 | tf_op jit(solution)/shard_map/ppermute | solution.py:36
  296.4 3.7 %collective-permute-start.52 = (bf16[4,2,96,896]{3,2,1,0:T(8,128)(2,1)}, bf16[4,2,96,896]{3,2,1,0:T(8,128)(2,1)S(1)}, u32[]{:S(2)}, u32[]{:S(2)}) collective-permute-start(bf16[4,2,96,896]{3,2,1,0:T(8,128)(2,1)} %get-tuple-element.404), channel_id=1, source_target_pairs={{0,4},{4,0},{1,5},{5,1},{2,6},{6,2},{3,7},{7,3},{8,12},{12,8},{9,1... | collective-permute-start | bytes 4128776 | tf_op jit(solution)/shard_map/ppermute | solution.py:44
  298.6 18.0 %collective-permute-start.54 = (bf16[2,2,96,896]{3,2,1,0:T(8,128)(2,1)}, bf16[2,2,96,896]{3,2,1,0:T(8,128)(2,1)}, u32[]{:S(2)}, u32[]{:S(2)}) collective-permute-start(bf16[2,2,96,896]{3,2,1,0:T(8,128)(2,1)} %add_convert_fusion.2), channel_id=1, source_target_pairs={{0,16},{8,24},{16,0},{24,8},{1,17},{9,25},{17,1},{25,9},{2,18},{10... | collective-permute-start | bytes 2064392 | tf_op jit(solution)/shard_map/ppermute | solution.py:40
  301.3 20.3 %collective-permute-start.53 = (bf16[2,2,96,896]{3,2,1,0:T(8,128)(2,1)}, bf16[2,2,96,896]{3,2,1,0:T(8,128)(2,1)S(1)}, u32[]{:S(2)}, u32[]{:S(2)}) collective-permute-start(bf16[2,2,96,896]{3,2,1,0:T(8,128)(2,1)} %add_convert_fusion.3), channel_id=1, source_target_pairs={{0,8},{8,0},{16,24},{24,16},{1,9},{9,1},{17,25},{25,17},{2,10},{10... | collective-permute-start | bytes 2064392 | tf_op jit(solution)/shard_map/ppermute | solution.py:40
  302.1 12.0 %collective-permute-start.56 = (bf16[96,1536]{1,0:T(8,128)(2,1)S(1)}, bf16[96,1536]{1,0:T(8,128)(2,1)}, u32[]{:S(2)}, u32[]{:S(2)}) collective-permute-start(bf16[96,1536]{1,0:T(8,128)(2,1)S(1)} %slice_bitcast_fusion.2), channel_id=1, source_target_pairs={{0,1},{1,2},{2,3},{3,0},{4,5},{5,6},{6,7},{7,4},{8,9},{9,10},{10,1... | collective-permute-start | bytes 884744 | tf_op jit(solution)/shard_map/ppermute | solution.py:36
  304.8 16.7 %collective-permute-start.55 = (bf16[128,768]{1,0:T(8,128)(2,1)}, bf16[128,768]{1,0:T(8,128)(2,1)}, u32[]{:S(2)}, u32[]{:S(2)}) collective-permute-start(bf16[128,768]{1,0:T(8,128)(2,1)} %slice.347), channel_id=1, source_target_pairs={{0,2},{1,3},{2,0},{3,1},{4,6},{5,7},{6,4},{7,5},{8,10},{9,11},{10,... | collective-permute-start | bytes 589832 | tf_op jit(solution)/shard_map/ppermute | solution.py:36
  322.8 14.2 %collective-permute-start.57 = (bf16[2,96,896]{2,1,0:T(8,128)(2,1)S(1)}, bf16[2,96,896]{2,1,0:T(8,128)(2,1)S(1)}, u32[]{:S(2)}, u32[]{:S(2)}) collective-permute-start(bf16[2,96,896]{2,1,0:T(8,128)(2,1)S(1)} %fusion.9), channel_id=1, source_target_pairs={{0,8},{8,0},{16,24},{24,16},{1,9},{9,1},{17,25},{25,17},{2,10},{10... | collective-permute-start | bytes 1032200 | tf_op jit(solution)/shard_map/ppermute | solution.py:40
  325.2 11.7 %collective-permute-start.58 = (bf16[2,96,896]{2,1,0:T(8,128)(2,1)S(1)}, bf16[2,96,896]{2,1,0:T(8,128)(2,1)S(1)}, u32[]{:S(2)}, u32[]{:S(2)}) collective-permute-start(bf16[2,96,896]{2,1,0:T(8,128)(2,1)S(1)} %fusion.10), channel_id=1, source_target_pairs={{0,16},{8,24},{16,0},{24,8},{1,17},{9,25},{17,1},{25,9},{2,18},{10... | collective-permute-start | bytes 1032200 | tf_op jit(solution)/shard_map/ppermute | solution.py:40
  326.4 10.5 %collective-permute-start.59 = (bf16[128,768]{1,0:T(8,128)(2,1)S(1)}, bf16[128,768]{1,0:T(8,128)(2,1)S(1)}, u32[]{:S(2)}, u32[]{:S(2)}) collective-permute-start(bf16[128,768]{1,0:T(8,128)(2,1)S(1)} %get-tuple-element.490), channel_id=1, source_target_pairs={{0,3},{1,0},{2,1},{3,2},{4,7},{5,4},{6,5},{7,6},{8,11},{9,8},{10,9... | collective-permute-start | bytes 589832 | tf_op jit(solution)/shard_map/ppermute | solution.py:36
  327.2 9.7 %collective-permute-start.60 = (bf16[128,768]{1,0:T(8,128)(2,1)S(1)}, bf16[128,768]{1,0:T(8,128)(2,1)S(1)}, u32[]{:S(2)}, u32[]{:S(2)}) collective-permute-start(bf16[128,768]{1,0:T(8,128)(2,1)S(1)} %get-tuple-element.489), channel_id=1, source_target_pairs={{0,1},{1,2},{2,3},{3,0},{4,5},{5,6},{6,7},{7,4},{8,9},{9,10},{10,1... | collective-permute-start | bytes 589832 | tf_op jit(solution)/shard_map/ppermute | solution.py:36
  329.6 13.3 %collective-permute-start.64 = (bf16[96,1536]{1,0:T(8,128)(2,1)S(1)}, bf16[96,1536]{1,0:T(8,128)(2,1)S(1)}, u32[]{:S(2)}, u32[]{:S(2)}) collective-permute-start(bf16[96,1536]{1,0:T(8,128)(2,1)S(1)} %fusion.8), channel_id=1, source_target_pairs={{0,4},{4,0},{1,5},{5,1},{2,6},{6,2},{3,7},{7,3},{8,12},{12,8},{9,1... | collective-permute-start | bytes 884744 | tf_op jit(solution)/shard_map/ppermute | solution.py:44
  338.4 9.2 %collective-permute-start.61 = (bf16[96,896]{1,0:T(8,128)(2,1)S(1)}, bf16[96,896]{1,0:T(8,128)(2,1)S(1)}, u32[]{:S(2)}, u32[]{:S(2)}) collective-permute-start(bf16[96,896]{1,0:T(8,128)(2,1)S(1)} %get-tuple-element.506), channel_id=1, source_target_pairs={{0,3},{1,0},{2,1},{3,2},{4,7},{5,4},{6,5},{7,6},{8,11},{9,8},{10,9... | collective-permute-start | bytes 516104 | tf_op jit(solution)/shard_map/ppermute | solution.py:36
  340.3 14.9 %collective-permute-start.62 = (bf16[96,896]{1,0:T(8,128)(2,1)S(1)}, bf16[96,896]{1,0:T(8,128)(2,1)S(1)}, u32[]{:S(2)}, u32[]{:S(2)}) collective-permute-start(bf16[96,896]{1,0:T(8,128)(2,1)S(1)} %get-tuple-element.505), channel_id=1, source_target_pairs={{0,2},{1,3},{2,0},{3,1},{4,6},{5,7},{6,4},{7,5},{8,10},{9,11},{10,... | collective-permute-start | bytes 516104 | tf_op jit(solution)/shard_map/ppermute | solution.py:36
  341.4 13.7 %collective-permute-start.63 = (bf16[96,896]{1,0:T(8,128)(2,1)S(1)}, bf16[96,896]{1,0:T(8,128)(2,1)S(1)}, u32[]{:S(2)}, u32[]{:S(2)}) collective-permute-start(bf16[96,896]{1,0:T(8,128)(2,1)S(1)} %get-tuple-element.504), channel_id=1, source_target_pairs={{0,1},{1,2},{2,3},{3,0},{4,5},{5,6},{6,7},{7,4},{8,9},{9,10},{10,1... | collective-permute-start | bytes 516104 | tf_op jit(solution)/shard_map/ppermute | solution.py:36
  (60 other events, 486.1 us)

commit v2 on v1

--- a/solution.py
+++ b/solution.py
@@ -35,6 +35,10 @@
         n = self.sizes["tensor"]
         return lax.ppermute(value, "tensor", [(i, (i + step) % n) for i in range(n)])
 
+    def by_length(self):
+        n = self.sizes["tensor"]
+        return sorted(range(1, n), key=lambda d: -min(d, n - d))
+
     def perm_s(self, value, mask):
         n = self.sizes["shard"]
         return lax.ppermute(value, "shard", [(i, i ^ mask) for i in range(n)])
@@ -59,7 +63,9 @@
 
     def spread_t(self, local):
         n = self.sizes["tensor"]
-        return jnp.stack([local] + [self.perm_t(local, d) for d in range(1, n)])
+        steps = self.by_length()
+        moved = dict(zip(steps, together(*[self.perm_t(local, d) for d in steps])))
+        return jnp.stack([local] + [moved[d] for d in range(1, n)])
 
     def spread_near(self, block):
         return self.perm_s(block, 1), self.perm_s(block, 2)
@@ -1005,10 +1011,12 @@
     block_a = links.spread_t(local_a)
     block_a, tokens, feat_half = together(block_a, tokens, feat_half)
     near_a = links.spread_near(block_a)
-    moved = links.carry(tokens, feat_half, range(1, n))
-    block_a, near_a, moved, local_u, tokens, feat_half = together(
-        block_a, near_a, moved, local_u, tokens, feat_half
-    )
+    moved = links.carry(tokens, feat_half, links.by_length())
+    steps = links.by_length()
+    *moved, block_a, near_a, local_u, tokens, feat_half = together(
+        *[moved[d] for d in steps], block_a, near_a, local_u, tokens, feat_half
+    )
+    moved = dict(zip(steps, moved))
     far_a = links.spread_far(near_a)
     other_a = links.swap((block_a,) + near_a)
     x, feat_mine = links.unload(tokens, feat_half, moved)
@@ -1098,7 +1106,7 @@
     keep, give, acc = run_back(0, d_state_a, x, None)
     keep, give, acc, two_f, came_b, slots_f, x = together(keep, give, acc, two_f, came_b, slots_f, x)
     sums_f = links.sums(*split(slots_f), one_f, two_f)
-    terms_f = links.collect_t(sums_f, (1, 2))
+    terms_f = links.collect_t(sums_f, (2, 1))
     other = links.perm_c(give)
     d_state_b = join_grads(d_state_b, came_b, falls[1])
     keep_b, give_b, grad_x = run_back(1, d_state_b, x, acc)
@@ -1117,7 +1125,7 @@
     two, one, low, high, sent, grad_x = together(two, one, low, high, sent, grad_x)
     grad_tokens = links.undealt(grad_x, sent, F)
     sums = links.sums(low, high, one, two)
-    terms = [sums[0]] + links.collect_t(sums, range(1, n))
+    terms = [sums[0]] + links.collect_t(sums, links.by_length())
     terms_f = [sums_f[0]] + terms_f
     own_ffn = links.collect_end(terms_f)
     grad_up, grad_down = own_ffn[:, z.ff :].astype(F), own_ffn[:, : z.ff].T.astype(F)

time: 363 us -> 358 us (0.986)
  waiting for transfers between devices: 83.1 us -> 72 us
  starting transfers between devices: 69.8 us -> 75.3 us
    ppermute x24, waiting for transfers between devices: 61.2 us -> 53.3 us  [perm_t(): lax.ppermute(value, 'tensor', [(i, (i + step) % n) for i in range(n)])]
    ppermute x24, starting transfers between devices: 43.7 us -> 49.2 us  [perm_t(): lax.ppermute(value, 'tensor', [(i, (i + step) % n) for i in range(n)])]
  transfers between devices with their start and end apart: 66 -> 66, of which waited for: 19 -> 18; matrix products, arithmetic and copies ran while one was open for 11% -> 12% of each run, Pallas kernels for 33% -> 34%
where the time goes in v2:
time: 358 us; the launch traced here: 356 us
  Pallas kernels  138 us (39%)
  starting transfers between devices  75.3 us (21%)
  waiting for transfers between devices  72 us (20%)
  other arithmetic  40.5 us (11%)
  local copies, waits for them, and re-layouts  27.9 us (8%)
    ppermute x24, waiting for transfers between devices, perm_t(): lax.ppermute(value, 'tensor', [(i, (i + step) % n) for i in range(n)])  53.3 us
    ppermute x24, starting transfers between devices, perm_t(): lax.ppermute(value, 'tensor', [(i, (i + step) % n) for i in range(n)])  49.2 us
    pallas_call x2, Pallas kernels, project(): call(body, (cnt,), [SCALARS] + [ANY] * 8 + [fixed(span, z.width), slot(hd...  26.1 us
    pallas_call x2, Pallas kernels, project_back(): call(body, (cnt,), [SCALARS] + [ANY] * 8 + [wide, wide, slot(span, z.oc),...  23.6 us
    ppermute x20, starting transfers between devices, perm_s(): return lax.ppermute(value, 'shard', [(i, i ^ mask) for i in range(n)])  22 us
    pallas_call x2, Pallas kernels, attend_back(): call(body, (cnt,), [SCALARS] + [ANY] * 8 + [fixed(span, z.width), slot(sp...  18.5 us
    pallas_call x1, Pallas kernels, narrow(): call(body, (2, n), [SCALARS] + [ANY] * 8 + [fixed(span, z.width), fixed(8...  16.4 us
    ppermute x20, waiting for transfers between devices, perm_s(): return lax.ppermute(value, 'shard', [(i, i ^ mask) for i in range(n)])  15.3 us
  transfers between devices with their start and end apart: 66, of which 18 were waited for; matrix products, arithmetic and copies ran while one was open for 12% of the time, Pallas kernels for 34%

profile of v2, /device:TPU:0, one launch (start us, length us, event | category | flops | bytes accessed | tf_op | source)
XLA Modules:
  0.0 356.0 jit_solution(15395941341796920701)
XLA Ops:
  4.7 2.2 gather_rows.1
  7.6 4.1 %collective-permute-start = (bf16[96,896]{1,0:T(8,128)(2,1)S(1)}, bf16[96,896]{1,0:T(8,128)(2,1)S(1)}, u32[]{:S(2)}, u32[]{:S(2)}) collective-permute-start(bf16[96,896]{1,0:T(8,128)(2,1)S(1)} %fusion.19), channel_id=1, source_target_pairs={{0,2},{1,3},{2,0},{3,1},{4,6},{5,7},{6,4},{7,5},{8,10},{9,11},{10,... | collective-permute-start | bytes 516104 | tf_op jit(solution)/shard_map/ppermute | solution.py:36
  11.8 1.6 collective-permute-start.1
  13.3 2.2 collective-permute-start.2
  15.6 8.8 %collective-permute-done = bf16[96,896]{1,0:T(8,128)(2,1)S(1)} collective-permute-done((bf16[96,896]{1,0:T(8,128)(2,1)S(1)}, bf16[96,896]{1,0:T(8,128)(2,1)S(1)}, u32[]{:S(2)}, u32[]{:S(2)}) %collective-permute-start) | collective-permute-done | bytes 172064 | tf_op jit(solution)/shard_map/ppermute | solution.py:36
  25.2 2.1 collective-permute-start.6
  27.4 1.5 collective-permute-start.7
  29.8 4.7 %collective-permute-start.3 = (bf16[160,768]{1,0:T(8,128)(2,1)}, bf16[160,768]{1,0:T(8,128)(2,1)S(1)}, u32[]{:S(2)}, u32[]{:S(2)}) collective-permute-start(bf16[160,768]{1,0:T(8,128)(2,1)} %get-tuple-element.524), channel_id=1, source_target_pairs={{0,2},{1,3},{2,0},{3,1},{4,6},{5,7},{6,4},{7,5},{8,10},{9,11},{10,... | collective-permute-start | bytes 737288 | tf_op jit(solution)/shard_map/ppermute | solution.py:36
  34.5 3.8 %collective-permute-start.5 = (bf16[160,768]{1,0:T(8,128)(2,1)S(1)}, bf16[160,768]{1,0:T(8,128)(2,1)S(1)}, u32[]{:S(2)}, u32[]{:S(2)}) collective-permute-start(bf16[160,768]{1,0:T(8,128)(2,1)S(1)} %get-tuple-element.522), channel_id=1, source_target_pairs={{0,3},{1,0},{2,1},{3,2},{4,7},{5,4},{6,5},{7,6},{8,11},{9,8},{10,9... | collective-permute-start | bytes 737288 | tf_op jit(solution)/shard_map/ppermute | solution.py:36
  39.6 11.5 %collective-permute-done.3 = bf16[160,768]{1,0:T(8,128)(2,1)S(1)} collective-permute-done((bf16[160,768]{1,0:T(8,128)(2,1)}, bf16[160,768]{1,0:T(8,128)(2,1)S(1)}, u32[]{:S(2)}, u32[]{:S(2)}) %collective-permute-start.3) | collective-permute-done | bytes 245792 | tf_op jit(solution)/shard_map/ppermute | solution.py:36
  57.1 7.5 %collective-permute-done.8 = bf16[2,96,896]{2,1,0:T(8,128)(2,1)S(1)} collective-permute-done((bf16[2,96,896]{2,1,0:T(8,128)(2,1)S(1)}, bf16[2,96,896]{2,1,0:T(8,128)(2,1)S(1)}, u32[]{:S(2)}, u32[]{:S(2)}) %collective-permute-start.8) | collective-permute-done | bytes 344096 | tf_op jit(solution)/shard_map/ppermute | solution.py:44
  69.7 4.0 %collective-permute-start.15 = (bf16[96,768]{1,0:T(8,128)(2,1)S(1)}, bf16[96,768]{1,0:T(8,128)(2,1)S(1)}, u32[]{:S(2)}, u32[]{:S(2)}) collective-permute-start(bf16[96,768]{1,0:T(8,128)(2,1)S(1)} %constant_dynamic-slice_fusion.3), channel_id=1, source_target_pairs={{0,2},{1,3},{2,0},{3,1},{4,6},{5,7},{6,4},{7,5},{8,10},{9,11},{10,... | collective-permute-start | bytes 442376 | tf_op jit(solution)/shard_map/ppermute | solution.py:36
  74.7 2.8 collective-permute-start.17
  77.6 13.1 %project.2 = (bf16[2,512,192]{2,1,0:T(8,128)(2,1)}, bf16[2,512,192]{2,1,0:T(8,128)(2,1)}, bf16[2,512,192]{2,1,0:T(8,128)(2,1)}, bf16[2,512,768]{2,1,0:T(8,128)(2...) custom-call(s32[2]{0:T(128)} %pad_add_fusion.where, ...), custom_call_target="tpu_custom_call" | custom-call | flops 3300000000 | bytes 8800000 | tf_op jit(solution)/shard_map/project/pallas_call | solution.py:445
  91.2 1.7 collective-permute-start.19
  95.0 13.0 %project.3 = (bf16[2,512,192]{2,1,0:T(8,128)(2,1)}, bf16[2,512,192]{2,1,0:T(8,128)(2,1)}, bf16[2,512,192]{2,1,0:T(8,128)(2,1)}, bf16[2,512,768]{2,1,0:T(8,128)(2...) custom-call(s32[2]{0:T(128)} %pad_add_fusion.where, ...), custom_call_target="tpu_custom_call" | custom-call | flops 3300000000 | bytes 8800000 | tf_op jit(solution)/shard_map/project/pallas_call | solution.py:445
  108.1 3.5 collective-permute-done.21
  115.2 1.7 collective-permute-start.24
  117.7 3.8 %collective-permute-start.26 = (bf16[224,768]{1,0:T(8,128)(2,1)S(1)}, bf16[224,768]{1,0:T(8,128)(2,1)S(1)}, u32[]{:S(2)}, u32[]{:S(2)}) collective-permute-start(bf16[224,768]{1,0:T(8,128)(2,1)S(1)} %get-tuple-element.520), channel_id=1, source_target_pairs={{0,3},{1,0},{2,1},{3,2},{4,7},{5,4},{6,5},{7,6},{8,11},{9,8},{10,9... | collective-permute-start | bytes 1032200 | tf_op jit(solution)/shard_map/ppermute | solution.py:36
  121.5 1.7 add_convert_fusion.11.refs_9_.refs_13_
  123.2 6.5 %attend.2 = (bf16[2,512,192]{2,1,0:T(8,128)(2,1)}, f32[2,512,192]{2,1,0:T(8,128)}, f32[2,8,768]{2,1,0:T(8,128)}, f32[512,768]{1,0:T(8,128)}) custom-call(s32[2]{0:T(128)} %pad_add_fusion.where, bf16[4,96,896]{2,1,0:T(8,128)(2,1)} %copy-done.2, bf16[4,96,896]{2,1,0:T(8,128)(2,1)} %copy-done.3, bf16[4,96,896]{2,1,0:T(8,128)(2,1)} %copy-done.4, ...), custom_call_target="tpu_custom_call" | custom-call | flops 1800000000 | bytes 4800000 | tf_op jit(solution)/shard_map/attend/pallas_call | solution.py:534
  130.6 4.1 %collective-permute-done.26 = bf16[224,768]{1,0:T(8,128)(2,1)S(1)} collective-permute-done((bf16[224,768]{1,0:T(8,128)(2,1)S(1)}, bf16[224,768]{1,0:T(8,128)(2,1)S(1)}, u32[]{:S(2)}, u32[]{:S(2)}) %collective-permute-start.26) | collective-permute-done | bytes 344096 | tf_op jit(solution)/shard_map/ppermute | solution.py:36
  137.0 1.7 collective-permute-start.29
  145.2 1.7 add_convert_fusion.10.refs_9_.refs_13_
  146.9 8.5 %attend.3 = (bf16[2,512,192]{2,1,0:T(8,128)(2,1)}, f32[2,512,192]{2,1,0:T(8,128)}, f32[2,8,768]{2,1,0:T(8,128)}, f32[512,768]{1,0:T(8,128)}, f32[512,1]{1,0:T(8,128)}, /*index=5*/f32[8,768]{1,0:T(8,128)}) custom-call(s32[2]{0:T(128)} %pad_add_fusion.where, bf16[4,96,896]{2,1,0:T(8,128)(2,1)} %copy-done.2, bf16[4,96,896]{2,1,0:T(8,128)(2,1)} %copy-done.3, ...), custom_call_target="tpu_custom_call" | custom-call | flops 1800000000 | bytes 4800000 | tf_op jit(solution)/shard_map/attend/pallas_call | solution.py:534
  158.8 1.7 collective-permute-start.34
  160.4 1.4 pad_maximum_fusion.16.refs_10_
  161.9 9.7 %widen.1 = (bf16[4,512,768]{2,1,0:T(8,128)(2,1)}, bf16[4,512,768]{2,1,0:T(8,128)(2,1)}) custom-call(s32[2]{0:T(128)} %pad_add_fusion.where, bf16[4,96,768]{2,1,0:T(8,128)(2,1)} %copy-done.10, bf16[4,96,768]{2,1,0:T(8,128)(2,1)} %copy-done.15, bf16[4,96,768]{2,1,0:T(8,128)(2,1)} %copy-done.16, bf16[4,96,768]{2,1,0:T(8,128)(2,1)} %copy-done.17, ...), custom_call_target="tpu_custom_call" | custom-call | flops 3000000000 | bytes 8000000 | tf_op jit(solution)/shard_map/widen/pallas_call | solution.py:569
  171.9 2.0 collective-permute-done.38.refs_7_
  174.7 16.4 %narrow.1 = (bf16[512,768]{1,0:T(8,128)(2,1)}, f32[512,768]{1,0:T(8,128)}, bf16[512,768]{1,0:T(8,128)(2,1)}, bf16[4,512,768]{2,1,0:T(8,128)(2,1)}, f32[8,768]{1,0:T(8,128)}) custom-call(s32[2]{0:T(128)} %pad_add_fusion.where, bf16[4,96,768]{2,1,0:T(8,128)(2,1)} %pad_maximum_fusion.5.refs_0_, bf16[4,96,768]{2,1,0:T(8,128)(2,1)} %collective-permute-done.28.refs_1_, ...), custom_call_target="tpu_custom_call" | custom-call | flops 3900000000 | bytes 10400000 | tf_op jit(solution)/shard_map/narrow/pallas_call | solution.py:639
  192.1 2.4 collective-permute-start.39
  194.5 10.9 %ffn_grad.1 = (bf16[4,4,96,1536]{3,2,1,0:T(8,128)(2,1)}, bf16[4,4,96,1536]{3,2,1,0:T(8,128)(2,1)}, f32[4,8,768]{2,1,0:T(8,128)}) custom-call(s32[2]{0:T(128)} %pad_add_fusion.where, f32[512,768]{1,0:T(8,128)} %get-tuple-element.335.refs_8_.normal, f32[8,768]{1,0:T(8,128)} %get-tuple-element.337.refs_9_.vec.refs_10_, ...), custom_call_target="tpu_custom_call" | custom-call | flops 2700000000 | bytes 7200000 | tf_op jit(solution)/shard_map/ffn_grad/pallas_call | solution.py:686
  208.9 10.5 %widen_back.1 = (f32[512,768]{1,0:T(8,128)}, f32[8,768]{1,0:T(8,128)}) custom-call(s32[2]{0:T(128)} %pad_add_fusion.where, bf16[4,96,768]{2,1,0:T(8,128)(2,1)} %copy-done.10, bf16[4,96,768]{2,1,0:T(8,128)(2,1)} %copy-done.15, bf16[4,96,768]{2,1,0:T(8,128)(2,1)} %copy-done.16, bf16[4,96,768]{2,1,0:T(8,128)(2,1)} %copy-done.17, ...), custom_call_target="tpu_custom_call" | custom-call | flops 3000000000 | bytes 8000000 | tf_op jit(solution)/shard_map/widen_back/pallas_call | solution.py:732
  219.4 4.2 %add_convert_fusion = (bf16[2,2,96,1536]{3,2,1,0:T(8,128)(2,1)S(1)}, bf16[2,2,96,1536]{3,2,1,0:T(8,128)(2,1)}) fusion(bf16[4,4,96,1536]{3,2,1,0:T(8,128)(2,1)} %collective-permute-done.40, bf16[4,4,96,1536]{3,2,1,0:T(8,128)(2,1)} %get-tuple-element.411), kind=kLoop, calls=%fused_computation | loop fusion | flops 4718592 | bytes 7077888 | tf_op jit(solution)/shard_map/convert_element_type | solution.py:98
  224.0 1.7 collective-permute-start.45
  225.7 9.2 %attend_back.2 = (bf16[2,512,192]{2,1,0:T(8,128)(2,1)}, bf16[2,72,768]{2,1,0:T(8,128)(2,1)}) custom-call(s32[2]{0:T(128)} %pad_add_fusion.where, bf16[4,96,896]{2,1,0:T(8,128)(2,1)} %copy-done.2, bf16[4,96,896]{2,1,0:T(8,128)(2,1)} %copy-done.3, bf16[4,96,896]{2,1,0:T(8,128)(2,1)} %copy-done.4, bf16[4,96,896]{2,1,0:T(8,128)(2,1)} %copy-done.5, ...), custom_call_target="tpu_custom_call" | custom-call | flops 2100000000 | bytes 5600000 | tf_op jit(solution)/shard_map/attend_back/pallas_call | solution.py:803
  235.0 9.2 %attend_back.3 = (bf16[2,512,192]{2,1,0:T(8,128)(2,1)}, bf16[2,72,768]{2,1,0:T(8,128)(2,1)}) custom-call(s32[2]{0:T(128)} %pad_add_fusion.where, bf16[4,96,896]{2,1,0:T(8,128)(2,1)} %copy-done.2, bf16[4,96,896]{2,1,0:T(8,128)(2,1)} %copy-done.3, bf16[4,96,896]{2,1,0:T(8,128)(2,1)} %copy-done.4, bf16[4,96,896]{2,1,0:T(8,128)(2,1)} %copy-done.5, ...), custom_call_target="tpu_custom_call" | custom-call | flops 2100000000 | bytes 5600000 | tf_op jit(solution)/shard_map/attend_back/pallas_call | solution.py:803
  244.3 7.4 %collective-permute-done.44 = bf16[2,2,96,1536]{3,2,1,0:T(8,128)(2,1)S(1)} collective-permute-done((bf16[2,2,96,1536]{3,2,1,0:T(8,128)(2,1)}, bf16[2,2,96,1536]{3,2,1,0:T(8,128)(2,1)S(1)}, u32[]{:S(2)}, u32[]{:S(2)}) %collective-permute-start.44) | collective-permute-done | bytes 1179680 | tf_op jit(solution)/shard_map/ppermute | solution.py:44
  251.7 3.1 fusion.5
  254.8 1.5 collective-permute-start.46
  256.3 1.5 collective-permute-start.47
  258.6 11.5 %project_back.2 = (bf16[4,2,96,896]{3,2,1,0:T(8,128)(2,1)}, bf16[4,2,96,896]{3,2,1,0:T(8,128)(2,1)}, f32[512,768]{1,0:T(8,128)}) custom-call(s32[2]{0:T(128)} %pad_add_fusion.where, bf16[4,96,896]{2,1,0:T(8,128)(2,1)} %copy-done.2, bf16[4,96,896]{2,1,0:T(8,128)(2,1)} %copy-done.3, bf16[4,96,896]{2,1,0:T(8,128)(2,1)} %copy-done.4, ...), custom_call_target="tpu_custom_call" | custom-call | flops 3300000000 | bytes 8800000 | tf_op jit(solution)/shard_map/project_back/pallas_call | solution.py:906
  270.7 2.2 fusion
  273.6 2.8 collective-permute-start.51
  276.4 1.7 multiply_convert_fusion.refs_14_
  278.2 12.0 %project_back.3 = (bf16[4,2,96,896]{3,2,1,0:T(8,128)(2,1)}, bf16[4,2,96,896]{3,2,1,0:T(8,128)(2,1)}, bf16[512,768]{1,0:T(8,128)(2,1)}) custom-call(s32[2]{0:T(128)} %pad_add_fusion.where, bf16[4,96,896]{2,1,0:T(8,128)(2,1)} %copy-done.2, bf16[4,96,896]{2,1,0:T(8,128)(2,1)} %copy-done.3, bf16[4,96,896]{2,1,0:T(8,128)(2,1)} %copy-done.4, ...), custom_call_target="tpu_custom_call" | custom-call | flops 3300000000 | bytes 8800000 | tf_op jit(solution)/shard_map/project_back/pallas_call | solution.py:906
  291.1 2.1 add_convert_fusion.2
  296.2 6.3 %collective-permute-start.56 = (bf16[96,1536]{1,0:T(8,128)(2,1)S(1)}, bf16[96,1536]{1,0:T(8,128)(2,1)}, u32[]{:S(2)}, u32[]{:S(2)}) collective-permute-start(bf16[96,1536]{1,0:T(8,128)(2,1)S(1)} %slice_bitcast_fusion.2), channel_id=1, source_target_pairs={{0,1},{1,2},{2,3},{3,0},{4,5},{5,6},{6,7},{7,4},{8,9},{9,10},{10,1... | collective-permute-start | bytes 884744 | tf_op jit(solution)/shard_map/ppermute | solution.py:36
  302.5 1.6 slice.347
  304.1 1.3 collective-permute-start.55
  305.5 2.7 lay.3
  308.2 3.2 collective-permute-done.56
  311.4 7.1 %collective-permute-done.55.refs_2_ = bf16[128,768]{1,0:T(8,128)(2,1)} collective-permute-done((bf16[128,768]{1,0:T(8,128)(2,1)}, bf16[128,768]{1,0:T(8,128)(2,1)}, u32[]{:S(2)}, u32[]{:S(2)}) %collective-permute-start.55) | collective-permute-done | bytes 196640 | tf_op jit(solution)/shard_map/ppermute | solution.py:36
  319.6 1.3 collective-permute-start.57
  320.9 1.2 fusion.10
  323.1 1.7 collective-permute-start.59
  326.4 7.3 %collective-permute-done.59.refs_1_ = bf16[128,768]{1,0:T(8,128)(2,1)S(1)} collective-permute-done((bf16[128,768]{1,0:T(8,128)(2,1)S(1)}, bf16[128,768]{1,0:T(8,128)(2,1)S(1)}, u32[]{:S(2)}, u32[]{:S(2)}) %collective-permute-start.59) | collective-permute-done | bytes 196640 | tf_op jit(solution)/shard_map/ppermute | solution.py:36
  333.6 1.4 fusion.3
  335.1 1.5 collective-permute-start.61
  337.7 1.8 collective-permute-start.62
  341.6 2.9 lay.2
  344.6 2.4 collective-permute-done.61
  347.0 3.2 collective-permute-done.62
  350.3 1.4 collective-permute-done.65
  (310 shorter events, 63.0 us)
Async XLA Ops:
  7.6 16.8 %collective-permute-start = (bf16[96,896]{1,0:T(8,128)(2,1)S(1)}, bf16[96,896]{1,0:T(8,128)(2,1)S(1)}, u32[]{:S(2)}, u32[]{:S(2)}) collective-permute-start(bf16[96,896]{1,0:T(8,128)(2,1)S(1)} %fusion.19), channel_id=1, source_target_pairs={{0,2},{1,3},{2,0},{3,1},{4,6},{5,7},{6,4},{7,5},{8,10},{9,11},{10,... | collective-permute-start | bytes 516104 | tf_op jit(solution)/shard_map/ppermute | solution.py:36
  11.8 12.6 %collective-permute-start.1 = (bf16[96,896]{1,0:T(8,128)(2,1)S(1)}, bf16[96,896]{1,0:T(8,128)(2,1)S(1)}, u32[]{:S(2)}, u32[]{:S(2)}) collective-permute-start(bf16[96,896]{1,0:T(8,128)(2,1)S(1)} %fusion.19), channel_id=1, source_target_pairs={{0,1},{1,2},{2,3},{3,0},{4,5},{5,6},{6,7},{7,4},{8,9},{9,10},{10,1... | collective-permute-start | bytes 516104 | tf_op jit(solution)/shard_map/ppermute | solution.py:36
  13.3 11.8 %collective-permute-start.2 = (bf16[96,896]{1,0:T(8,128)(2,1)S(1)}, bf16[96,896]{1,0:T(8,128)(2,1)S(1)}, u32[]{:S(2)}, u32[]{:S(2)}) collective-permute-start(bf16[96,896]{1,0:T(8,128)(2,1)S(1)} %fusion.19), channel_id=1, source_target_pairs={{0,3},{1,0},{2,1},{3,2},{4,7},{5,4},{6,5},{7,6},{8,11},{9,8},{10,9... | collective-permute-start | bytes 516104 | tf_op jit(solution)/shard_map/ppermute | solution.py:36
  25.2 26.6 %collective-permute-start.6 = (bf16[4,96,896]{2,1,0:T(8,128)(2,1)S(1)}, bf16[4,96,896]{2,1,0:T(8,128)(2,1)S(1)}, u32[]{:S(2)}, u32[]{:S(2)}) collective-permute-start(bf16[4,96,896]{2,1,0:T(8,128)(2,1)S(1)} %pad_maximum_fusion.3.refs_0_), channel_id=1, source_target_pairs={{0,8},{8,0},{16,24},{24,16},{1,9},{9,1},{17,25},{25,17},{2,10},{10... | collective-permute-start | bytes 2064392 | tf_op jit(solution)/shard_map/ppermute | solution.py:44
  27.4 25.1 %collective-permute-start.7 = (bf16[4,96,896]{2,1,0:T(8,128)(2,1)S(1)}, bf16[4,96,896]{2,1,0:T(8,128)(2,1)S(1)}, u32[]{:S(2)}, u32[]{:S(2)}) collective-permute-start(bf16[4,96,896]{2,1,0:T(8,128)(2,1)S(1)} %pad_maximum_fusion.3.refs_0_), channel_id=1, source_target_pairs={{0,16},{8,24},{16,0},{24,8},{1,17},{9,25},{17,1},{25,9},{2,18},{10... | collective-permute-start | bytes 2064392 | tf_op jit(solution)/shard_map/ppermute | solution.py:44
  29.8 21.3 %collective-permute-start.3 = (bf16[160,768]{1,0:T(8,128)(2,1)}, bf16[160,768]{1,0:T(8,128)(2,1)S(1)}, u32[]{:S(2)}, u32[]{:S(2)}) collective-permute-start(bf16[160,768]{1,0:T(8,128)(2,1)} %get-tuple-element.524), channel_id=1, source_target_pairs={{0,2},{1,3},{2,0},{3,1},{4,6},{5,7},{6,4},{7,5},{8,10},{9,11},{10,... | collective-permute-start | bytes 737288 | tf_op jit(solution)/shard_map/ppermute | solution.py:36
  34.5 16.6 %collective-permute-start.4 = (bf16[160,768]{1,0:T(8,128)(2,1)}, bf16[160,768]{1,0:T(8,128)(2,1)S(1)}, u32[]{:S(2)}, u32[]{:S(2)}) collective-permute-start(bf16[160,768]{1,0:T(8,128)(2,1)} %get-tuple-element.523), channel_id=1, source_target_pairs={{0,1},{1,2},{2,3},{3,0},{4,5},{5,6},{6,7},{7,4},{8,9},{9,10},{10,1... | collective-permute-start | bytes 737288 | tf_op jit(solution)/shard_map/ppermute | solution.py:36
  34.5 17.3 %collective-permute-start.5 = (bf16[160,768]{1,0:T(8,128)(2,1)S(1)}, bf16[160,768]{1,0:T(8,128)(2,1)S(1)}, u32[]{:S(2)}, u32[]{:S(2)}) collective-permute-start(bf16[160,768]{1,0:T(8,128)(2,1)S(1)} %get-tuple-element.522), channel_id=1, source_target_pairs={{0,3},{1,0},{2,1},{3,2},{4,7},{5,4},{6,5},{7,6},{8,11},{9,8},{10,9... | collective-permute-start | bytes 737288 | tf_op jit(solution)/shard_map/ppermute | solution.py:36
  52.5 12.4 %collective-permute-start.10 = (bf16[4,96,896]{2,1,0:T(8,128)(2,1)S(1)}, bf16[4,96,896]{2,1,0:T(8,128)(2,1)S(1)}, u32[]{:S(2)}, u32[]{:S(2)}) collective-permute-start(bf16[4,96,896]{2,1,0:T(8,128)(2,1)S(1)} %pad_maximum_fusion.3.refs_0_), channel_id=1, source_target_pairs={{0,4},{4,0},{1,5},{5,1},{2,6},{6,2},{3,7},{7,3},{8,12},{12,8},{9,1... | collective-permute-start | bytes 2064392 | tf_op jit(solution)/shard_map/ppermute | solution.py:48
  52.6 12.3 %collective-permute-start.11 = (bf16[4,96,896]{2,1,0:T(8,128)(2,1)S(1)}, bf16[4,96,896]{2,1,0:T(8,128)(2,1)S(1)}, u32[]{:S(2)}, u32[]{:S(2)}) collective-permute-start(bf16[4,96,896]{2,1,0:T(8,128)(2,1)S(1)} %collective-permute-done.6.refs_1_), channel_id=1, source_target_pairs={{0,4},{4,0},{1,5},{5,1},{2,6},{6,2},{3,7},{7,3},{8,12},{12,8},{9,1... | collective-permute-start | bytes 2064392 | tf_op jit(solution)/shard_map/ppermute | solution.py:48
  53.1 11.8 %collective-permute-start.12 = (bf16[4,96,896]{2,1,0:T(8,128)(2,1)S(1)}, bf16[4,96,896]{2,1,0:T(8,128)(2,1)S(1)}, u32[]{:S(2)}, u32[]{:S(2)}) collective-permute-start(bf16[4,96,896]{2,1,0:T(8,128)(2,1)S(1)} %collective-permute-done.7.refs_2_), channel_id=1, source_target_pairs={{0,4},{4,0},{1,5},{5,1},{2,6},{6,2},{3,7},{7,3},{8,12},{12,8},{9,1... | collective-permute-start | bytes 2064392 | tf_op jit(solution)/shard_map/ppermute | solution.py:48
  54.2 10.5 %collective-permute-start.8 = (bf16[2,96,896]{2,1,0:T(8,128)(2,1)S(1)}, bf16[2,96,896]{2,1,0:T(8,128)(2,1)S(1)}, u32[]{:S(2)}, u32[]{:S(2)}) collective-permute-start(bf16[2,96,896]{2,1,0:T(8,128)(2,1)S(1)} %slice.296), channel_id=1, source_target_pairs={{0,16},{8,24},{16,0},{24,8},{1,17},{9,25},{17,1},{25,9},{2,18},{10... | collective-permute-start | bytes 1032200 | tf_op jit(solution)/shard_map/ppermute | solution.py:44
  54.8 10.1 %collective-permute-start.9 = (bf16[2,96,896]{2,1,0:T(8,128)(2,1)S(1)}, bf16[2,96,896]{2,1,0:T(8,128)(2,1)S(1)}, u32[]{:S(2)}, u32[]{:S(2)}) collective-permute-start(bf16[2,96,896]{2,1,0:T(8,128)(2,1)S(1)} %slice.297), channel_id=1, source_target_pairs={{0,8},{8,0},{16,24},{24,16},{1,9},{9,1},{17,25},{25,17},{2,10},{10... | collective-permute-start | bytes 1032200 | tf_op jit(solution)/shard_map/ppermute | solution.py:44
  66.0 3.7 %collective-permute-start.14 = (bf16[4,96,896]{2,1,0:T(8,128)(2,1)S(1)}, bf16[4,96,896]{2,1,0:T(8,128)(2,1)S(1)}, u32[]{:S(2)}, u32[]{:S(2)}) collective-permute-start(bf16[4,96,896]{2,1,0:T(8,128)(2,1)S(1)} %constant_dynamic-update-slice_fusion.refs_3_), channel_id=1, source_target_pairs={{0,4},{4,0},{1,5},{5,1},{2,6},{6,2},{3,7},{7,3},{8,12},{12,8},{9,1... | collective-permute-start | bytes 2064392 | tf_op jit(solution)/shard_map/ppermute | solution.py:48
  66.0 2.9 collective-permute-start.13
  69.7 20.9 %collective-permute-start.15 = (bf16[96,768]{1,0:T(8,128)(2,1)S(1)}, bf16[96,768]{1,0:T(8,128)(2,1)S(1)}, u32[]{:S(2)}, u32[]{:S(2)}) collective-permute-start(bf16[96,768]{1,0:T(8,128)(2,1)S(1)} %constant_dynamic-slice_fusion.3), channel_id=1, source_target_pairs={{0,2},{1,3},{2,0},{3,1},{4,6},{5,7},{6,4},{7,5},{8,10},{9,11},{10,... | collective-permute-start | bytes 442376 | tf_op jit(solution)/shard_map/ppermute | solution.py:36
  73.7 16.9 %collective-permute-start.16 = (bf16[96,768]{1,0:T(8,128)(2,1)S(1)}, bf16[96,768]{1,0:T(8,128)(2,1)S(1)}, u32[]{:S(2)}, u32[]{:S(2)}) collective-permute-start(bf16[96,768]{1,0:T(8,128)(2,1)S(1)} %constant_dynamic-slice_fusion.3), channel_id=1, source_target_pairs={{0,1},{1,2},{2,3},{3,0},{4,5},{5,6},{6,7},{7,4},{8,9},{9,10},{10,1... | collective-permute-start | bytes 442376 | tf_op jit(solution)/shard_map/ppermute | solution.py:36
  74.7 15.9 %collective-permute-start.17 = (bf16[96,768]{1,0:T(8,128)(2,1)S(1)}, bf16[96,768]{1,0:T(8,128)(2,1)S(1)}, u32[]{:S(2)}, u32[]{:S(2)}) collective-permute-start(bf16[96,768]{1,0:T(8,128)(2,1)S(1)} %constant_dynamic-slice_fusion.3), channel_id=1, source_target_pairs={{0,3},{1,0},{2,1},{3,2},{4,7},{5,4},{6,5},{7,6},{8,11},{9,8},{10,9... | collective-permute-start | bytes 442376 | tf_op jit(solution)/shard_map/ppermute | solution.py:36
  90.7 20.8 %collective-permute-start.18 = (bf16[4,96,768]{2,1,0:T(8,128)(2,1)S(1)}, bf16[4,96,768]{2,1,0:T(8,128)(2,1)S(1)}, u32[]{:S(2)}, u32[]{:S(2)}) collective-permute-start(bf16[4,96,768]{2,1,0:T(8,128)(2,1)S(1)} %pad_maximum_fusion.4.refs_0_), channel_id=1, source_target_pairs={{0,8},{8,0},{16,24},{24,16},{1,9},{9,1},{17,25},{25,17},{2,10},{10... | collective-permute-start | bytes 1769480 | tf_op jit(solution)/shard_map/ppermute | solution.py:44
  91.2 20.4 %collective-permute-start.19 = (bf16[4,96,768]{2,1,0:T(8,128)(2,1)S(1)}, bf16[4,96,768]{2,1,0:T(8,128)(2,1)S(1)}, u32[]{:S(2)}, u32[]{:S(2)}) collective-permute-start(bf16[4,96,768]{2,1,0:T(8,128)(2,1)S(1)} %pad_maximum_fusion.4.refs_0_), channel_id=1, source_target_pairs={{0,16},{8,24},{16,0},{24,8},{1,17},{9,25},{17,1},{25,9},{2,18},{10... | collective-permute-start | bytes 1769480 | tf_op jit(solution)/shard_map/ppermute | solution.py:44
  92.9 18.7 %collective-permute-start.20 = (bf16[4,96,768]{2,1,0:T(8,128)(2,1)S(1)}, bf16[4,96,768]{2,1,0:T(8,128)(2,1)S(1)}, u32[]{:S(2)}, u32[]{:S(2)}) collective-permute-start(bf16[4,96,768]{2,1,0:T(8,128)(2,1)S(1)} %pad_maximum_fusion.4.refs_0_), channel_id=1, source_target_pairs={{0,4},{4,0},{1,5},{5,1},{2,6},{6,2},{3,7},{7,3},{8,12},{12,8},{9,1... | collective-permute-start | bytes 1769480 | tf_op jit(solution)/shard_map/ppermute | solution.py:48
  93.6 17.9 %collective-permute-start.21 = (bf16[224,768]{1,0:T(8,128)(2,1)}, bf16[224,768]{1,0:T(8,128)(2,1)}, u32[]{:S(2)}, u32[]{:S(2)}) collective-permute-start(bf16[224,768]{1,0:T(8,128)(2,1)} %pad_maximum_fusion.12), channel_id=1, source_target_pairs={{0,2},{1,3},{2,0},{3,1},{4,6},{5,7},{6,4},{7,5},{8,10},{9,11},{10,... | collective-permute-start | bytes 1032200 | tf_op jit(solution)/shard_map/ppermute | solution.py:36
  94.6 13.5 %collective-permute-start.22 = (bf16[2,72,768]{2,1,0:T(8,128)(2,1)}, bf16[2,72,768]{2,1,0:T(8,128)(2,1)S(1)}, u32[]{:S(2)}, u32[]{:S(2)}) collective-permute-start(bf16[2,72,768]{2,1,0:T(8,128)(2,1)} %get-tuple-element.297), channel_id=1, source_target_pairs={{0,4},{4,0},{1,5},{5,1},{2,6},{6,2},{3,7},{7,3},{8,12},{12,8},{9,1... | collective-permute-start | bytes 663560 | tf_op jit(solution)/shard_map/ppermute | solution.py:48
  114.1 15.6 %collective-permute-start.23 = (bf16[2,96,768]{2,1,0:T(8,128)(2,1)}, bf16[2,96,768]{2,1,0:T(8,128)(2,1)}, u32[]{:S(2)}, u32[]{:S(2)}) collective-permute-start(bf16[2,96,768]{2,1,0:T(8,128)(2,1)} %slice.308), channel_id=1, source_target_pairs={{0,16},{8,24},{16,0},{24,8},{1,17},{9,25},{17,1},{25,9},{2,18},{10... | collective-permute-start | bytes 884744 | tf_op jit(solution)/shard_map/ppermute | solution.py:44
  115.2 14.5 %collective-permute-start.24 = (bf16[2,96,768]{2,1,0:T(8,128)(2,1)}, bf16[2,96,768]{2,1,0:T(8,128)(2,1)}, u32[]{:S(2)}, u32[]{:S(2)}) collective-permute-start(bf16[2,96,768]{2,1,0:T(8,128)(2,1)} %slice.309), channel_id=1, source_target_pairs={{0,8},{8,0},{16,24},{24,16},{1,9},{9,1},{17,25},{25,17},{2,10},{10... | collective-permute-start | bytes 884744 | tf_op jit(solution)/shard_map/ppermute | solution.py:44
  117.6 12.9 %collective-permute-start.25 = (bf16[224,768]{1,0:T(8,128)(2,1)}, bf16[224,768]{1,0:T(8,128)(2,1)S(1)}, u32[]{:S(2)}, u32[]{:S(2)}) collective-permute-start(bf16[224,768]{1,0:T(8,128)(2,1)} %get-tuple-element.521), channel_id=1, source_target_pairs={{0,1},{1,2},{2,3},{3,0},{4,5},{5,6},{6,7},{7,4},{8,9},{9,10},{10,1... | collective-permute-start | bytes 1032200 | tf_op jit(solution)/shard_map/ppermute | solution.py:36
  117.7 17.1 %collective-permute-start.26 = (bf16[224,768]{1,0:T(8,128)(2,1)S(1)}, bf16[224,768]{1,0:T(8,128)(2,1)S(1)}, u32[]{:S(2)}, u32[]{:S(2)}) collective-permute-start(bf16[224,768]{1,0:T(8,128)(2,1)S(1)} %get-tuple-element.520), channel_id=1, source_target_pairs={{0,3},{1,0},{2,1},{3,2},{4,7},{5,4},{6,5},{7,6},{8,11},{9,8},{10,9... | collective-permute-start | bytes 1032200 | tf_op jit(solution)/shard_map/ppermute | solution.py:36
  121.5 8.2 %collective-permute-start.27 = (bf16[2,72,768]{2,1,0:T(8,128)(2,1)}, bf16[2,72,768]{2,1,0:T(8,128)(2,1)S(1)}, u32[]{:S(2)}, u32[]{:S(2)}) collective-permute-start(bf16[2,72,768]{2,1,0:T(8,128)(2,1)} %get-tuple-element.310), channel_id=1, source_target_pairs={{0,4},{4,0},{1,5},{5,1},{2,6},{6,2},{3,7},{7,3},{8,12},{12,8},{9,1... | collective-permute-start | bytes 663560 | tf_op jit(solution)/shard_map/ppermute | solution.py:48
  136.6 18.8 %collective-permute-start.28 = (bf16[4,96,768]{2,1,0:T(8,128)(2,1)}, bf16[4,96,768]{2,1,0:T(8,128)(2,1)}, u32[]{:S(2)}, u32[]{:S(2)}) collective-permute-start(bf16[4,96,768]{2,1,0:T(8,128)(2,1)} %pad_maximum_fusion.5.refs_0_), channel_id=1, source_target_pairs={{0,8},{8,0},{16,24},{24,16},{1,9},{9,1},{17,25},{25,17},{2,10},{10... | collective-permute-start | bytes 1769480 | tf_op jit(solution)/shard_map/ppermute | solution.py:44
  137.0 18.4 %collective-permute-start.29 = (bf16[4,96,768]{2,1,0:T(8,128)(2,1)}, bf16[4,96,768]{2,1,0:T(8,128)(2,1)}, u32[]{:S(2)}, u32[]{:S(2)}) collective-permute-start(bf16[4,96,768]{2,1,0:T(8,128)(2,1)} %pad_maximum_fusion.5.refs_0_), channel_id=1, source_target_pairs={{0,16},{8,24},{16,0},{24,8},{1,17},{9,25},{17,1},{25,9},{2,18},{10... | collective-permute-start | bytes 1769480 | tf_op jit(solution)/shard_map/ppermute | solution.py:44
  141.3 14.0 %collective-permute-start.30 = (bf16[4,96,768]{2,1,0:T(8,128)(2,1)S(1)}, bf16[4,96,768]{2,1,0:T(8,128)(2,1)S(1)}, u32[]{:S(2)}, u32[]{:S(2)}) collective-permute-start(bf16[4,96,768]{2,1,0:T(8,128)(2,1)S(1)} %collective-permute-done.18.refs_1_), channel_id=1, source_target_pairs={{0,4},{4,0},{1,5},{5,1},{2,6},{6,2},{3,7},{7,3},{8,12},{12,8},{9,1... | collective-permute-start | bytes 1769480 | tf_op jit(solution)/shard_map/ppermute | solution.py:48
  141.4 14.0 %collective-permute-start.31 = (bf16[4,96,768]{2,1,0:T(8,128)(2,1)S(1)}, bf16[4,96,768]{2,1,0:T(8,128)(2,1)}, u32[]{:S(2)}, u32[]{:S(2)}) collective-permute-start(bf16[4,96,768]{2,1,0:T(8,128)(2,1)S(1)} %collective-permute-done.19.refs_2_), channel_id=1, source_target_pairs={{0,4},{4,0},{1,5},{5,1},{2,6},{6,2},{3,7},{7,3},{8,12},{12,8},{9,1... | collective-permute-start | bytes 1769480 | tf_op jit(solution)/shard_map/ppermute | solution.py:48
  142.9 12.5 %collective-permute-start.32 = (bf16[4,96,768]{2,1,0:T(8,128)(2,1)S(1)}, bf16[4,96,768]{2,1,0:T(8,128)(2,1)}, u32[]{:S(2)}, u32[]{:S(2)}) collective-permute-start(bf16[4,96,768]{2,1,0:T(8,128)(2,1)S(1)} %constant_dynamic-update-slice_fusion.2.refs_3_), channel_id=1, source_target_pairs={{0,4},{4,0},{1,5},{5,1},{2,6},{6,2},{3,7},{7,3},{8,12},{12,8},{9,1... | collective-permute-start | bytes 1769480 | tf_op jit(solution)/shard_map/ppermute | solution.py:48
  155.4 16.2 %collective-permute-start.35 = (bf16[4,96,768]{2,1,0:T(8,128)(2,1)}, bf16[4,96,768]{2,1,0:T(8,128)(2,1)S(1)}, u32[]{:S(2)}, u32[]{:S(2)}) collective-permute-start(bf16[4,96,768]{2,1,0:T(8,128)(2,1)} %pad_maximum_fusion.5.refs_0_), channel_id=1, source_target_pairs={{0,4},{4,0},{1,5},{5,1},{2,6},{6,2},{3,7},{7,3},{8,12},{12,8},{9,1... | collective-permute-start | bytes 1769480 | tf_op jit(solution)/shard_map/ppermute | solution.py:48
  155.9 15.8 %collective-permute-start.36 = (bf16[4,96,768]{2,1,0:T(8,128)(2,1)}, bf16[4,96,768]{2,1,0:T(8,128)(2,1)S(1)}, u32[]{:S(2)}, u32[]{:S(2)}) collective-permute-start(bf16[4,96,768]{2,1,0:T(8,128)(2,1)} %collective-permute-done.28.refs_1_), channel_id=1, source_target_pairs={{0,4},{4,0},{1,5},{5,1},{2,6},{6,2},{3,7},{7,3},{8,12},{12,8},{9,1... | collective-permute-start | bytes 1769480 | tf_op jit(solution)/shard_map/ppermute | solution.py:48
  156.0 15.7 %collective-permute-start.37 = (bf16[4,96,768]{2,1,0:T(8,128)(2,1)}, bf16[4,96,768]{2,1,0:T(8,128)(2,1)S(1)}, u32[]{:S(2)}, u32[]{:S(2)}) collective-permute-start(bf16[4,96,768]{2,1,0:T(8,128)(2,1)} %collective-permute-done.29.refs_2_), channel_id=1, source_target_pairs={{0,4},{4,0},{1,5},{5,1},{2,6},{6,2},{3,7},{7,3},{8,12},{12,8},{9,1... | collective-permute-start | bytes 1769480 | tf_op jit(solution)/shard_map/ppermute | solution.py:48
  158.3 13.3 %collective-permute-start.33 = (bf16[2,96,768]{2,1,0:T(8,128)(2,1)S(1)}, bf16[2,96,768]{2,1,0:T(8,128)(2,1)S(1)}, u32[]{:S(2)}, u32[]{:S(2)}) collective-permute-start(bf16[2,96,768]{2,1,0:T(8,128)(2,1)S(1)} %slice.320), channel_id=1, source_target_pairs={{0,16},{8,24},{16,0},{24,8},{1,17},{9,25},{17,1},{25,9},{2,18},{10... | collective-permute-start | bytes 884744 | tf_op jit(solution)/shard_map/ppermute | solution.py:44
  158.8 12.9 %collective-permute-start.34 = (bf16[2,96,768]{2,1,0:T(8,128)(2,1)S(1)}, bf16[2,96,768]{2,1,0:T(8,128)(2,1)S(1)}, u32[]{:S(2)}, u32[]{:S(2)}) collective-permute-start(bf16[2,96,768]{2,1,0:T(8,128)(2,1)S(1)} %slice.321), channel_id=1, source_target_pairs={{0,8},{8,0},{16,24},{24,16},{1,9},{9,1},{17,25},{25,17},{2,10},{10... | collective-permute-start | bytes 884744 | tf_op jit(solution)/shard_map/ppermute | solution.py:44
  192.1 13.4 %collective-permute-start.39 = (bf16[128,768]{1,0:T(8,128)(2,1)S(1)}, bf16[128,768]{1,0:T(8,128)(2,1)S(1)}, u32[]{:S(2)}, u32[]{:S(2)}) collective-permute-start(bf16[128,768]{1,0:T(8,128)(2,1)S(1)} %slice.322), channel_id=1, source_target_pairs={{0,2},{1,3},{2,0},{3,1},{4,6},{5,7},{6,4},{7,5},{8,10},{9,11},{10,... | collective-permute-start | bytes 589832 | tf_op jit(solution)/shard_map/ppermute | solution.py:36
  206.1 13.3 %collective-permute-start.40 = (bf16[4,4,96,1536]{3,2,1,0:T(8,128)(2,1)}, bf16[4,4,96,1536]{3,2,1,0:T(8,128)(2,1)}, u32[]{:S(2)}, u32[]{:S(2)}) collective-permute-start(bf16[4,4,96,1536]{3,2,1,0:T(8,128)(2,1)} %get-tuple-element.362), channel_id=1, source_target_pairs={{0,4},{4,0},{1,5},{5,1},{2,6},{6,2},{3,7},{7,3},{8,12},{12,8},{9,1... | collective-permute-start | bytes 14155784 | tf_op jit(solution)/shard_map/ppermute | solution.py:48
  206.9 12.5 %collective-permute-start.41 = (bf16[128,768]{1,0:T(8,128)(2,1)S(1)}, bf16[128,768]{1,0:T(8,128)(2,1)S(1)}, u32[]{:S(2)}, u32[]{:S(2)}) collective-permute-start(bf16[128,768]{1,0:T(8,128)(2,1)S(1)} %get-tuple-element.500), channel_id=1, source_target_pairs={{0,3},{1,0},{2,1},{3,2},{4,7},{5,4},{6,5},{7,6},{8,11},{9,8},{10,9... | collective-permute-start | bytes 589832 | tf_op jit(solution)/shard_map/ppermute | solution.py:36
  208.0 11.4 %collective-permute-start.42 = (bf16[128,768]{1,0:T(8,128)(2,1)S(1)}, bf16[128,768]{1,0:T(8,128)(2,1)S(1)}, u32[]{:S(2)}, u32[]{:S(2)}) collective-permute-start(bf16[128,768]{1,0:T(8,128)(2,1)S(1)} %get-tuple-element.499), channel_id=1, source_target_pairs={{0,1},{1,2},{2,3},{3,0},{4,5},{5,6},{6,7},{7,4},{8,9},{9,10},{10,1... | collective-permute-start | bytes 589832 | tf_op jit(solution)/shard_map/ppermute | solution.py:36
  223.6 28.0 %collective-permute-start.44 = (bf16[2,2,96,1536]{3,2,1,0:T(8,128)(2,1)}, bf16[2,2,96,1536]{3,2,1,0:T(8,128)(2,1)S(1)}, u32[]{:S(2)}, u32[]{:S(2)}) collective-permute-start(bf16[2,2,96,1536]{3,2,1,0:T(8,128)(2,1)} %get-tuple-element.497), channel_id=1, source_target_pairs={{0,8},{8,0},{16,24},{24,16},{1,9},{9,1},{17,25},{25,17},{2,10},{10... | collective-permute-start | bytes 3538952 | tf_op jit(solution)/shard_map/ppermute | solution.py:44
  224.0 27.7 %collective-permute-start.45 = (bf16[2,2,96,1536]{3,2,1,0:T(8,128)(2,1)S(1)}, bf16[2,2,96,1536]{3,2,1,0:T(8,128)(2,1)S(1)}, u32[]{:S(2)}, u32[]{:S(2)}) collective-permute-start(bf16[2,2,96,1536]{3,2,1,0:T(8,128)(2,1)S(1)} %get-tuple-element.496), channel_id=1, source_target_pairs={{0,16},{8,24},{16,0},{24,8},{1,17},{9,25},{17,1},{25,9},{2,18},{10... | collective-permute-start | bytes 3538952 | tf_op jit(solution)/shard_map/ppermute | solution.py:44
  234.9 9.3 %collective-permute-start.43 = (bf16[2,72,768]{2,1,0:T(8,128)(2,1)}, bf16[2,72,768]{2,1,0:T(8,128)(2,1)S(1)}, u32[]{:S(2)}, u32[]{:S(2)}) collective-permute-start(bf16[2,72,768]{2,1,0:T(8,128)(2,1)} %get-tuple-element.379), channel_id=1, source_target_pairs={{0,4},{4,0},{1,5},{5,1},{2,6},{6,2},{3,7},{7,3},{8,12},{12,8},{9,1... | collective-permute-start | bytes 663560 | tf_op jit(solution)/shard_map/ppermute | solution.py:48
  254.8 15.4 %collective-permute-start.46 = (bf16[2,96,1536]{2,1,0:T(8,128)(2,1)}, bf16[2,96,1536]{2,1,0:T(8,128)(2,1)S(1)}, u32[]{:S(2)}, u32[]{:S(2)}) collective-permute-start(bf16[2,96,1536]{2,1,0:T(8,128)(2,1)} %get-tuple-element.495), channel_id=1, source_target_pairs={{0,8},{8,0},{16,24},{24,16},{1,9},{9,1},{17,25},{25,17},{2,10},{10... | collective-permute-start | bytes 1769480 | tf_op jit(solution)/shard_map/ppermute | solution.py:44
  256.3 14.0 %collective-permute-start.47 = (bf16[2,96,1536]{2,1,0:T(8,128)(2,1)}, bf16[2,96,1536]{2,1,0:T(8,128)(2,1)S(1)}, u32[]{:S(2)}, u32[]{:S(2)}) collective-permute-start(bf16[2,96,1536]{2,1,0:T(8,128)(2,1)} %get-tuple-element.494), channel_id=1, source_target_pairs={{0,16},{8,24},{16,0},{24,8},{1,17},{9,25},{17,1},{25,9},{2,18},{10... | collective-permute-start | bytes 1769480 | tf_op jit(solution)/shard_map/ppermute | solution.py:44
  257.8 12.3 %collective-permute-start.48 = (bf16[2,72,768]{2,1,0:T(8,128)(2,1)S(1)}, bf16[2,72,768]{2,1,0:T(8,128)(2,1)S(1)}, u32[]{:S(2)}, u32[]{:S(2)}) collective-permute-start(bf16[2,72,768]{2,1,0:T(8,128)(2,1)S(1)} %copy-done.39), channel_id=1, source_target_pairs={{0,4},{4,0},{1,5},{5,1},{2,6},{6,2},{3,7},{7,3},{8,12},{12,8},{9,1... | collective-permute-start | bytes 663560 | tf_op jit(solution)/shard_map/ppermute | solution.py:48
  270.3 20.0 %collective-permute-start.49 = (bf16[4,2,96,896]{3,2,1,0:T(8,128)(2,1)}, bf16[4,2,96,896]{3,2,1,0:T(8,128)(2,1)}, u32[]{:S(2)}, u32[]{:S(2)}) collective-permute-start(bf16[4,2,96,896]{3,2,1,0:T(8,128)(2,1)} %get-tuple-element.410), channel_id=1, source_target_pairs={{0,4},{4,0},{1,5},{5,1},{2,6},{6,2},{3,7},{7,3},{8,12},{12,8},{9,1... | collective-permute-start | bytes 4128776 | tf_op jit(solution)/shard_map/ppermute | solution.py:48
  273.0 17.2 %collective-permute-start.50 = (bf16[96,1536]{1,0:T(8,128)(2,1)S(1)}, bf16[96,1536]{1,0:T(8,128)(2,1)S(1)}, u32[]{:S(2)}, u32[]{:S(2)}) collective-permute-start(bf16[96,1536]{1,0:T(8,128)(2,1)S(1)} %slice_bitcast_fusion.1), channel_id=1, source_target_pairs={{0,2},{1,3},{2,0},{3,1},{4,6},{5,7},{6,4},{7,5},{8,10},{9,11},{10,... | collective-permute-start | bytes 884744 | tf_op jit(solution)/shard_map/ppermute | solution.py:36
  273.6 16.6 %collective-permute-start.51 = (bf16[96,1536]{1,0:T(8,128)(2,1)S(1)}, bf16[96,1536]{1,0:T(8,128)(2,1)S(1)}, u32[]{:S(2)}, u32[]{:S(2)}) collective-permute-start(bf16[96,1536]{1,0:T(8,128)(2,1)S(1)} %slice_bitcast_fusion), channel_id=1, source_target_pairs={{0,3},{1,0},{2,1},{3,2},{4,7},{5,4},{6,5},{7,6},{8,11},{9,8},{10,9... | collective-permute-start | bytes 884744 | tf_op jit(solution)/shard_map/ppermute | solution.py:36
  290.3 4.0 %collective-permute-start.52 = (bf16[4,2,96,896]{3,2,1,0:T(8,128)(2,1)}, bf16[4,2,96,896]{3,2,1,0:T(8,128)(2,1)S(1)}, u32[]{:S(2)}, u32[]{:S(2)}) collective-permute-start(bf16[4,2,96,896]{3,2,1,0:T(8,128)(2,1)} %get-tuple-element.416), channel_id=1, source_target_pairs={{0,4},{4,0},{1,5},{5,1},{2,6},{6,2},{3,7},{7,3},{8,12},{12,8},{9,1... | collective-permute-start | bytes 4128776 | tf_op jit(solution)/shard_map/ppermute | solution.py:48
  293.2 18.2 %collective-permute-start.54 = (bf16[2,2,96,896]{3,2,1,0:T(8,128)(2,1)}, bf16[2,2,96,896]{3,2,1,0:T(8,128)(2,1)S(1)}, u32[]{:S(2)}, u32[]{:S(2)}) collective-permute-start(bf16[2,2,96,896]{3,2,1,0:T(8,128)(2,1)} %add_convert_fusion.2), channel_id=1, source_target_pairs={{0,16},{8,24},{16,0},{24,8},{1,17},{9,25},{17,1},{25,9},{2,18},{10... | collective-permute-start | bytes 2064392 | tf_op jit(solution)/shard_map/ppermute | solution.py:44
  295.4 23.1 %collective-permute-start.53 = (bf16[2,2,96,896]{3,2,1,0:T(8,128)(2,1)}, bf16[2,2,96,896]{3,2,1,0:T(8,128)(2,1)}, u32[]{:S(2)}, u32[]{:S(2)}) collective-permute-start(bf16[2,2,96,896]{3,2,1,0:T(8,128)(2,1)} %add_convert_fusion.3), channel_id=1, source_target_pairs={{0,8},{8,0},{16,24},{24,16},{1,9},{9,1},{17,25},{25,17},{2,10},{10... | collective-permute-start | bytes 2064392 | tf_op jit(solution)/shard_map/ppermute | solution.py:44
  296.2 15.1 %collective-permute-start.56 = (bf16[96,1536]{1,0:T(8,128)(2,1)S(1)}, bf16[96,1536]{1,0:T(8,128)(2,1)}, u32[]{:S(2)}, u32[]{:S(2)}) collective-permute-start(bf16[96,1536]{1,0:T(8,128)(2,1)S(1)} %slice_bitcast_fusion.2), channel_id=1, source_target_pairs={{0,1},{1,2},{2,3},{3,0},{4,5},{5,6},{6,7},{7,4},{8,9},{9,10},{10,1... | collective-permute-start | bytes 884744 | tf_op jit(solution)/shard_map/ppermute | solution.py:36
  304.1 14.4 %collective-permute-start.55 = (bf16[128,768]{1,0:T(8,128)(2,1)}, bf16[128,768]{1,0:T(8,128)(2,1)}, u32[]{:S(2)}, u32[]{:S(2)}) collective-permute-start(bf16[128,768]{1,0:T(8,128)(2,1)} %slice.347), channel_id=1, source_target_pairs={{0,2},{1,3},{2,0},{3,1},{4,6},{5,7},{6,4},{7,5},{8,10},{9,11},{10,... | collective-permute-start | bytes 589832 | tf_op jit(solution)/shard_map/ppermute | solution.py:36
  319.6 14.0 %collective-permute-start.57 = (bf16[2,96,896]{2,1,0:T(8,128)(2,1)S(1)}, bf16[2,96,896]{2,1,0:T(8,128)(2,1)S(1)}, u32[]{:S(2)}, u32[]{:S(2)}) collective-permute-start(bf16[2,96,896]{2,1,0:T(8,128)(2,1)S(1)} %fusion.9), channel_id=1, source_target_pairs={{0,8},{8,0},{16,24},{24,16},{1,9},{9,1},{17,25},{25,17},{2,10},{10... | collective-permute-start | bytes 1032200 | tf_op jit(solution)/shard_map/ppermute | solution.py:44
  322.2 11.5 %collective-permute-start.58 = (bf16[2,96,896]{2,1,0:T(8,128)(2,1)S(1)}, bf16[2,96,896]{2,1,0:T(8,128)(2,1)S(1)}, u32[]{:S(2)}, u32[]{:S(2)}) collective-permute-start(bf16[2,96,896]{2,1,0:T(8,128)(2,1)S(1)} %fusion.10), channel_id=1, source_target_pairs={{0,16},{8,24},{16,0},{24,8},{1,17},{9,25},{17,1},{25,9},{2,18},{10... | collective-permute-start | bytes 1032200 | tf_op jit(solution)/shard_map/ppermute | solution.py:44
  323.1 10.5 %collective-permute-start.59 = (bf16[128,768]{1,0:T(8,128)(2,1)S(1)}, bf16[128,768]{1,0:T(8,128)(2,1)S(1)}, u32[]{:S(2)}, u32[]{:S(2)}) collective-permute-start(bf16[128,768]{1,0:T(8,128)(2,1)S(1)} %get-tuple-element.502), channel_id=1, source_target_pairs={{0,3},{1,0},{2,1},{3,2},{4,7},{5,4},{6,5},{7,6},{8,11},{9,8},{10,9... | collective-permute-start | bytes 589832 | tf_op jit(solution)/shard_map/ppermute | solution.py:36
  324.8 8.9 %collective-permute-start.60 = (bf16[128,768]{1,0:T(8,128)(2,1)S(1)}, bf16[128,768]{1,0:T(8,128)(2,1)S(1)}, u32[]{:S(2)}, u32[]{:S(2)}) collective-permute-start(bf16[128,768]{1,0:T(8,128)(2,1)S(1)} %get-tuple-element.501), channel_id=1, source_target_pairs={{0,1},{1,2},{2,3},{3,0},{4,5},{5,6},{6,7},{7,4},{8,9},{9,10},{10,1... | collective-permute-start | bytes 589832 | tf_op jit(solution)/shard_map/ppermute | solution.py:36
  326.3 13.5 %collective-permute-start.64 = (bf16[96,1536]{1,0:T(8,128)(2,1)S(1)}, bf16[96,1536]{1,0:T(8,128)(2,1)S(1)}, u32[]{:S(2)}, u32[]{:S(2)}) collective-permute-start(bf16[96,1536]{1,0:T(8,128)(2,1)S(1)} %fusion.8), channel_id=1, source_target_pairs={{0,4},{4,0},{1,5},{5,1},{2,6},{6,2},{3,7},{7,3},{8,12},{12,8},{9,1... | collective-permute-start | bytes 884744 | tf_op jit(solution)/shard_map/ppermute | solution.py:48
  335.1 11.9 %collective-permute-start.61 = (bf16[96,896]{1,0:T(8,128)(2,1)S(1)}, bf16[96,896]{1,0:T(8,128)(2,1)S(1)}, u32[]{:S(2)}, u32[]{:S(2)}) collective-permute-start(bf16[96,896]{1,0:T(8,128)(2,1)S(1)} %get-tuple-element.517), channel_id=1, source_target_pairs={{0,2},{1,3},{2,0},{3,1},{4,6},{5,7},{6,4},{7,5},{8,10},{9,11},{10,... | collective-permute-start | bytes 516104 | tf_op jit(solution)/shard_map/ppermute | solution.py:36
  337.7 12.4 %collective-permute-start.62 = (bf16[96,896]{1,0:T(8,128)(2,1)S(1)}, bf16[96,896]{1,0:T(8,128)(2,1)S(1)}, u32[]{:S(2)}, u32[]{:S(2)}) collective-permute-start(bf16[96,896]{1,0:T(8,128)(2,1)S(1)} %get-tuple-element.518), channel_id=1, source_target_pairs={{0,3},{1,0},{2,1},{3,2},{4,7},{5,4},{6,5},{7,6},{8,11},{9,8},{10,9... | collective-permute-start | bytes 516104 | tf_op jit(solution)/shard_map/ppermute | solution.py:36
  339.5 10.6 %collective-permute-start.63 = (bf16[96,896]{1,0:T(8,128)(2,1)S(1)}, bf16[96,896]{1,0:T(8,128)(2,1)S(1)}, u32[]{:S(2)}, u32[]{:S(2)}) collective-permute-start(bf16[96,896]{1,0:T(8,128)(2,1)S(1)} %get-tuple-element.516), channel_id=1, source_target_pairs={{0,1},{1,2},{2,3},{3,0},{4,5},{5,6},{6,7},{7,4},{8,9},{9,10},{10,1... | collective-permute-start | bytes 516104 | tf_op jit(solution)/shard_map/ppermute | solution.py:36
  (60 other events, 467.1 us)
